TPU v7x, 128 devices: a whole 4x4x4 slice. The times are simulated.
128 devices in a mesh: dp: 16 (over x, y), tensor: 8 (over z, core).
Axes of the slice: x: 4, y: 4, z: 4, core: 2. Of those that a mesh axis runs over, the one named last changes fastest.
Arguments:
- kv_part: bfloat16 [8, 4096, 12288], P('tensor', 'dp'), may hold values from -2 to 2
- queries: bfloat16 [8192, 6144], P('dp', 'tensor'), may hold values from -6 to 6
- w_out: bfloat16 [6144, 8192], P('tensor'), may hold values from -0.078125 to 0.078125
- d_out: bfloat16 [8192, 8192], P('dp', 'tensor'), may hold values from -48 to 48
- nbr_owner: int32 [128, 2], replicated, may hold values from 0 to 15, as said below
- nbr_slot: int32 [128, 2], replicated, may hold values from 0 to 1, as said below
Outputs:
- mixed: bfloat16 [8192, 8192], P('dp', 'tensor')
- d_kv: bfloat16 [4096, 12288], P('dp', 'tensor')
Inputs may be any that keep to these rules, and one draw needn't show every extreme that they name: `nbr_owner`: the two neighbours of one span have different owners. `nbr_slot`: all neighbours that the spans of one dp index r (spans r * 8 to (r + 1) * 8 - 1) take from one owner have the same slot.
All inputs are finite; a program needn't handle non-finite values.
Results may differ from a plain program's by a relative error of at most 0.025.
Values may be sent and summed in bfloat16 or wider, within the bound.
A program may use at most 192 MiB of HBM per device.

v0:
```python
import jax
import jax.numpy as jnp
from jax import lax
from jax.sharding import PartitionSpec as P

HD = 128
SPAN = 64
NBR_LEN = 128
NB_DEV = 2


def local(kv_part, queries, w_out, d_out, nbr_owner, nbr_slot):
    dp_count = lax.axis_size("dp")
    reader = lax.axis_index("dp")
    head_width = w_out.shape[0]
    heads_here = head_width // HD
    share_width = 2 * head_width
    span_count = queries.shape[0] // SPAN
    read_count = 2 * span_count
    block_width = NBR_LEN * share_width
    local_partial = kv_part[0]
    summed = lax.psum(local_partial, "tensor").astype(jnp.float32)
    shares = lax.dynamic_slice_in_dim(
        summed, lax.axis_index("tensor") * share_width, share_width, 1
    ).astype(jnp.bfloat16)
    share_blocks = shares.reshape(NB_DEV, block_width)
    owner_ids = jnp.arange(dp_count, dtype=jnp.int32)
    slot_ids = jnp.arange(NB_DEV, dtype=jnp.int32)
    owner_hits = nbr_owner[:, :, None] == owner_ids[None, None, :]
    per_reader = owner_hits.reshape(dp_count, read_count, dp_count)
    reads_from = jnp.any(per_reader, axis=1)
    slot_from = jnp.max(jnp.where(per_reader, nbr_slot.reshape(dp_count, read_count, 1), 0), axis=1)
    my_owner = lax.dynamic_slice_in_dim(nbr_owner, reader * span_count, span_count, 0).reshape(
        read_count
    )
    my_slot = lax.dynamic_slice_in_dim(nbr_slot, reader * span_count, span_count, 0).reshape(
        read_count
    )
    read_table = (my_owner[:, None] == owner_ids[None, :]).astype(jnp.bfloat16)
    serving = lax.dynamic_index_in_dim(reads_from, reader, 1, False)
    serving_slot = lax.dynamic_index_in_dim(slot_from, reader, 1, False)
    owner_select = ((serving_slot[:, None] == slot_ids[None, :]) & serving[:, None]).astype(
        jnp.bfloat16
    )
    everyone = lax.all_gather(share_blocks, "dp", axis=0, tiled=True)
    wanted = (my_owner * NB_DEV + my_slot)[:, None] == jnp.arange(
        dp_count * NB_DEV, dtype=jnp.int32
    )[None, :]
    neighbours = jnp.dot(
        wanted.astype(jnp.bfloat16), everyone, preferred_element_type=jnp.float32
    ).astype(jnp.bfloat16)
    layout = neighbours.reshape(span_count, 2 * NBR_LEN, heads_here, 2, HD)
    keys = layout[:, :, :, 0]
    values = layout[:, :, :, 1]
    query_view = queries.reshape(span_count, SPAN, heads_here, HD)
    factor = HD ** (-0.5)
    scores = (
        jnp.einsum("cqhd,ckhd->chqk", query_view, keys, preferred_element_type=jnp.float32) * factor
    )
    highest = jnp.max(scores, axis=-1, keepdims=True)
    expo = jnp.exp(scores - highest)
    probs = expo / jnp.sum(expo, axis=-1, keepdims=True)
    probs_low = probs.astype(jnp.bfloat16)
    attended = jnp.einsum("chqk,ckhd->cqhd", probs_low, values, preferred_element_type=jnp.float32)
    attended = attended.astype(jnp.bfloat16).reshape(span_count * SPAN, head_width)
    partial_out = jnp.dot(attended, w_out, preferred_element_type=jnp.float32)
    mixed = lax.psum_scatter(
        partial_out.astype(jnp.bfloat16), "tensor", scatter_dimension=1, tiled=True
    )
    grad_attended = lax.dot_general(
        lax.all_gather(d_out, "tensor", axis=1, tiled=True),
        w_out,
        (((1,), (1,)), ((), ())),
        preferred_element_type=jnp.float32,
    ).astype(jnp.bfloat16)
    grad_view = grad_attended.reshape(span_count, SPAN, heads_here, HD)
    grad_values = jnp.einsum(
        "chqk,cqhd->ckhd", probs_low, grad_view, preferred_element_type=jnp.float32
    )
    grad_probs = jnp.einsum(
        "cqhd,ckhd->chqk", grad_view, values, preferred_element_type=jnp.float32
    )
    grad_scores = probs * (grad_probs - jnp.sum(probs * grad_probs, axis=-1, keepdims=True))
    grad_scores = grad_scores.astype(jnp.bfloat16)
    grad_keys = (
        jnp.einsum("chqk,cqhd->ckhd", grad_scores, query_view, preferred_element_type=jnp.float32)
        * factor
    )
    grad_blocks = jnp.stack([grad_keys, grad_values], axis=3).reshape(read_count, block_width)
    per_owner = lax.dot_general(
        read_table.astype(jnp.float32),
        grad_blocks,
        (((0,), (0,)), ((), ())),
        precision=lax.Precision.HIGHEST,
        preferred_element_type=jnp.float32,
    ).astype(jnp.bfloat16)
    returned = lax.all_to_all(per_owner, "dp", split_axis=0, concat_axis=0, tiled=True)
    owner_grad = lax.dot_general(
        owner_select, returned, (((0,), (0,)), ((), ())), preferred_element_type=jnp.float32
    )
    d_kv = owner_grad.astype(jnp.bfloat16).reshape(NB_DEV * NBR_LEN, share_width)
    return (mixed, d_kv)


def solution(mesh):
    placed = (
        P("tensor", "dp", None),
        P("dp", "tensor"),
        P("tensor", None),
        P("dp", "tensor"),
        P(),
        P(),
    )
    return jax.shard_map(
        local,
        mesh=mesh,
        in_specs=placed,
        out_specs=(P("dp", "tensor"), P("dp", "tensor")),
        check_vma=False,
    )
```

profile of v0, /device:TPU:28, one launch (start us, length us, event | category | flops | bytes accessed | tf_op | source)
XLA Modules:
  0.0 541.4 jit_solution(5792027820581872935)
XLA Ops:
  7.2 0.7 all-reduce.2.cloned.1.call-update
  7.9 0.0 all-gather.6.cloned.1.call-start
  8.0 89.0 %all-reduce.2.cloned.1.call-done = bf16[256,12288]{1,0:T(8,128)(2,1)} async-done(((bf16[256,12288]{1,0:T(8,128)(2,1)}), bf16[256,12288]{1,0:T(8,128)(2,1)}) %all-reduce.2.cloned.1.call-update) | async-done | bytes 6291472 | tf_op jit(solution)/shard_map/psum | solution.py:22
  97.0 1.2 convert_convert_fusion
  98.2 1.5 reshape.62
  99.7 0.0 all-gather.4.cloned.1.call-start
  99.7 0.7 all-gather.4.cloned.1.call-update
  100.5 0.1 constant_dynamic-slice_fusion
  100.5 0.1 copy.73
  100.6 0.1 reshape.54
  100.7 0.1 copy.72
  100.8 0.1 reshape.53
  100.9 1.9 reshape.57
  102.8 85.0 %all-gather.6.cloned.1.call-done = bf16[16,2,196608]{2,1,0:T(2,128)(2,1)} async-done(((bf16[1,2,196608]{2,1,0:T(2,128)(2,1)}), bf16[16,2,196608]{2,1,0:T(2,128)(2,1)}) %all-gather.6.cloned.1.call-update) | async-done | bytes 12582928 | tf_op jit(solution)/shard_map/all_gather | solution.py:45
  187.7 11.3 %reshape.63 = bf16[32,196608]{1,0:T(8,128)(2,1)} reshape(bf16[16,2,196608]{2,1,0:T(2,128)(2,1)} %all-gather.6.cloned.1.call-done) | data formatting | bytes 25165824
  199.0 10.4 %convolution_convert_fusion.1 = bf16[16,196608]{1,0:T(8,128)(2,1)} fusion(bf16[32,196608]{1,0:T(8,128)(2,1)} %reshape.63, s32[16]{0:T(128)S(1)} %multiply_add_fusion), kind=kOutput, calls=%fused_computation.2 | convolution fusion | flops 204472832 | bytes 18874432 | tf_op jit(solution)/shard_map/dot_general | solution.py:49
  209.4 9.9 %reshape.56 = bf16[8,256,6,2,128]{4,3,2,1,0:T(2,128)(2,1)} reshape(bf16[16,196608]{1,0:T(8,128)(2,1)} %convolution_convert_fusion.1) | data formatting | bytes 12582912 | tf_op jit(solution)/shard_map/reshape | solution.py:52
  219.3 13.7 %fusion.42 = (bf16[8,256,6,1,128]{4,3,2,1,0:T(2,128)(2,1)S(1)}, bf16[8,256,6,1,128]{4,3,2,1,0:T(2,128)(2,1)}) fusion(bf16[8,256,6,2,128]{4,3,2,1,0:T(2,128)(2,1)} %reshape.56), kind=kLoop, calls=%fused_computation.54 | loop fusion | bytes 12582912 | tf_op jit(solution)/shard_map/slice | solution.py:53
  233.0 1.2 fusion.4
  234.2 2.3 fusion.43
  236.5 9.2 %fusion.12 = bf16[8,64,6,128]{3,1,2,0:T(8,128)(2,1)} fusion(bf16[8,256,6,1,128]{4,3,2,1,0:T(2,128)(2,1)} %get-tuple-element.3, f32[8,6,64]{2,1,0:T(8,128)S(1)} %get-tuple-element.4, f32[8,6,256,64]{2,3,1,0:T(8,128)S(1)} %fusion.4), kind=kOutput, calls=%fused_computation.27 | convolution fusion | flops 205655296 | bytes 7090176 | tf_op jit(solution)/shard_map/chqk,ckhd->cqhd/dot_general | solution.py:64
  245.7 1.7 copy.77
  247.4 13.4 %convolution_convert_fusion.3 = bf16[512,8192]{1,0:T(8,128)(2,1)} fusion(bf16[768,8192]{1,0:T(8,128)(2,1)} %param.8, bf16[64,8,6,128]{3,2,1,0:T(8,128)(2,1)S(1)} %bitcast.71), kind=kOutput, calls=%fused_computation.6 | convolution fusion | flops 6446645248 | bytes 21757952 | tf_op jit(solution)/shard_map/dot_general | solution.py:66
  260.9 13.5 %convolution_convert_fusion.5 = bf16[512,768]{1,0:T(8,128)(2,1)} fusion(bf16[512,8192]{1,0:T(8,128)(2,1)} %all-gather.4.cloned.1.call-done, bf16[768,8192]{1,0:T(8,128)(2,1)} %param.8), kind=kOutput, calls=%fused_computation.26 | convolution fusion | flops 6442844160 | bytes 21757952 | tf_op jit(solution)/shard_map/dot_general | solution.py:70
  274.4 2.9 reshape.59
  277.3 10.3 %convolution_bitcast_fusion = f32[8,256,6,1,128]{4,1,2,0,3:T(8,128)} fusion(bf16[8,64,6,128]{3,2,1,0:T(8,128)(2,1)} %reshape.59, f32[8,6,64]{2,1,0:T(8,128)S(1)} %get-tuple-element.4, f32[8,6,256,64]{2,3,1,0:T(8,128)S(1)} %fusion.4), kind=kOutput, calls=%fused_computation.20 | convolution fusion | flops 205262080 | bytes 10235904 | tf_op jit(solution)/shard_map/chqk,cqhd->ckhd/dot_general | solution.py:77
  287.6 7.2 %multiply_reduce_fusion = (f32[8,6,64]{2,1,0:T(8,128)S(1)}, f32[8,6,64,256]{3,2,1,0:T(8,128)}) fusion(f32[8,6,64,256]{3,2,1,0:T(8,128)} %get-tuple-element.5, f32[8,6,64]{2,1,0:T(8,128)S(1)} %get-tuple-element.4, bf16[8,256,6,1,128]{4,3,2,1,0:T(2,128)(2,1)} %get-tuple-element.3, bf16[8,64,6,128]{3,2,1,0:T(8,128)(2,1)} %reshape.59), kind=kOutput, calls=%fused_computation.18 | convolution fusion | flops 203682816 | bytes 10248192 | tf_op jit(solution)/shard_map/cqhd,ckhd->chqk/dot_general | solution.py:80
  294.8 11.7 %multiply_bitcast_fusion = f32[8,256,6,1,128]{4,1,2,0,3:T(8,128)} fusion(f32[8,6,64,256]{3,2,1,0:T(8,128)} %get-tuple-element.7, f32[8,6,64]{2,1,0:T(8,128)S(1)} %get-tuple-element.6, bf16[8,64,6,128]{3,2,1,0:T(8,128)(2,1)} %reshape.57, f32[8,6,64]{2,1,0:T(8,128)S(1)} %get-tuple-element.4, f32[8,6,256,64]{2,3,1,0:T(8,128)S(1)} %fusion.4), kind=kOutput, calls=%fused_computation.9 | convolution fusion | flops 208407808 | bytes 13393920 | tf_op jit(solution)/shard_map/chqk,cqhd->ckhd/dot_general | solution.py:86
  306.5 10.9 %pad_maximum_fusion = f32[8,256,6,2,128]{4,1,2,0,3:T(8,128)} fusion(f32[8,256,6,1,128]{4,1,2,0,3:T(8,128)} %convolution_bitcast_fusion, f32[8,256,6,1,128]{4,1,2,0,3:T(8,128)} %multiply_bitcast_fusion), kind=kLoop, calls=%fused_computation.5 | loop fusion | flops 3145728 | bytes 25165824 | tf_op jit(solution)/shard_map/stack | solution.py:89
  317.4 22.2 %copy.84 = f32[8,256,6,2,128]{4,3,2,1,0:T(2,128)} copy(f32[8,256,6,2,128]{4,1,2,0,3:T(8,128)} %pad_maximum_fusion) | data formatting | bytes 25165824 | tf_op jit(solution)/shard_map/stack | solution.py:89
  339.6 21.3 %reshape.60 = f32[16,196608]{1,0:T(8,128)} reshape(f32[8,256,6,2,128]{4,3,2,1,0:T(2,128)} %copy.84) | data formatting | bytes 25165824 | tf_op jit(solution)/shard_map/reshape | solution.py:89
  360.9 10.9 %fusion.1 = bf16[16,1,196608]{2,0,1:T(8,128)(2,1)} fusion(f32[16,196608]{1,0:T(8,128)} %reshape.60, s32[16]{0:T(128)S(1)} %reshape.53), kind=kOutput, calls=%fused_computation.3 | convolution fusion | flops 607125760 | bytes 18874432 | tf_op jit(solution)/shard_map/dot_general | solution.py:90
  371.8 0.5 broadcast.20
  372.3 8.8 %reduce.4 = bf16[16,196608]{1,0:T(8,128)(2,1)} reduce(bf16[16,1,196608]{2,0,1:T(8,128)(2,1)} %fusion.1, bf16[]{:T(256)} %broadcast.20), dimensions={1}, to_apply=%copy.85.reduce_sub_computation | reduce | bytes 12582914 | tf_op jit(solution)/shard_map/all_to_all | solution.py:97
  381.2 9.3 %reshape.67 = bf16[16,2,98304]{2,1,0:T(2,128)(2,1)} reshape(bf16[16,196608]{1,0:T(8,128)(2,1)} %reduce.4) | data formatting | bytes 12582912
  390.5 7.2 %all-to-all-start = ((bf16[16,2,98304]{2,1,0:T(2,128)(2,1)}), bf16[16,2,98304]{2,1,0:T(2,128)(2,1)}, u32[]{:S(2)}, u32[]{:S(2)}) async-start(bf16[16,2,98304]{2,1,0:T(2,128)(2,1)} %reshape.67), calls=%async_computation.1 | async-start | bytes 12582912 | tf_op jit(solution)/shard_map/all_to_all | solution.py:97
  397.7 0.1 copy.79
  397.9 0.1 copy.78
  398.0 0.1 broadcast_in_dim.14
  398.1 0.1 eq.60
  398.1 0.2 select_reduce_fusion
  398.3 0.2 dynamic-slice_reduce_fusion
  398.5 0.1 fusion.22
  398.6 0.2 dynamic-slice_reduce_fusion.1
  398.8 107.1 %all-to-all-done = bf16[16,2,98304]{2,1,0:T(2,128)(2,1)} async-done(((bf16[16,2,98304]{2,1,0:T(2,128)(2,1)}), bf16[16,2,98304]{2,1,0:T(2,128)(2,1)}, u32[]{:S(2)}, u32[]{:S(2)}) %all-to-all-start) | async-done | bytes 6291488 | tf_op jit(solution)/shard_map/all_to_all | solution.py:97
  505.9 14.3 %reshape.68 = bf16[16,1,196608]{2,1,0:T(2,128)(2,1)} reshape(bf16[16,2,98304]{2,1,0:T(2,128)(2,1)} %all-to-all-done) | data formatting | bytes 12582912
  520.2 12.8 %convolution_convert_fusion.2 = bf16[2,196608]{1,0:T(2,128)(2,1)S(1)} fusion(bf16[16,1,196608]{2,1,0:T(2,128)(2,1)} %reshape.68, s32[16]{0:T(128)S(1)} %dynamic-slice_reduce_fusion, pred[16]{0:T(512)(128)(4,1)S(1)} %dynamic-slice_reduce_fusion.1), kind=kOutput, calls=%fused_computation.4 | convolution fusion | flops 12976192 | bytes 7077968 | tf_op jit(solution)/shard_map/dot_general | solution.py:98
  533.1 1.6 reshape.61
  (15 shorter events, 0.2 us)
Async XLA Ops:
  7.2 89.8 %all-reduce.2.cloned.1.call-start = ((), (), s32[]{:S(2)}) async-start(), calls=%async_computation.2 | async-start | bytes 12582912 | tf_op jit(solution)/shard_map/psum | solution.py:22
  7.9 92.6 %copy-start.2 = (s32[128,2]{0,1:T(2,128)S(1)}, s32[128,2]{0,1:T(2,128)}, u32[]{:S(2)}) copy-start(s32[128,2]{0,1:T(2,128)} %param.11) | copy-start | bytes 3076
  7.9 92.6 %copy-start.3 = (s32[128,2]{0,1:T(2,128)S(1)}, s32[128,2]{0,1:T(2,128)}, u32[]{:S(2)}) copy-start(s32[128,2]{0,1:T(2,128)} %param.10) | copy-start | bytes 3076
  7.9 93.0 %copy-start.1 = (bf16[512,768]{1,0:T(8,128)(2,1)S(1)}, bf16[512,768]{1,0:T(8,128)(2,1)}, u32[]{:S(2)}) copy-start(bf16[512,768]{1,0:T(8,128)(2,1)} %param.7) | copy-start | bytes 2359300
  7.9 179.8 %all-gather.6.cloned.1.call-start = ((), (), s32[]{:S(2)}) async-start(), calls=%async_computation.5 | async-start | bytes 13369344 | tf_op jit(solution)/shard_map/all_gather | solution.py:45
  99.7 161.2 %all-gather.4.cloned.1.call-start = ((), (), s32[]{:S(2)}) async-start(), calls=%async_computation.4 | async-start | bytes 9437184 | tf_op jit(solution)/shard_map/all_gather | solution.py:71
  100.4 434.3 %reduce-scatter.2.cloned.1.call-start = ((), (), s32[]{:S(2)}) async-start(), calls=%async_computation.3 | async-start | bytes 9437184 | tf_op jit(solution)/shard_map/reduce_scatter | solution.py:67
  219.3 13.7 %copy-start = (bf16[8,64,6,128]{3,2,1,0:T(8,128)(2,1)S(1)}, bf16[8,64,6,128]{3,2,1,0:T(8,128)(2,1)}, u32[]{:S(2)}) copy-start(bf16[8,64,6,128]{3,2,1,0:T(8,128)(2,1)} %reshape.57) | copy-start | bytes 2359300
  390.5 115.4 %all-to-all-start = ((bf16[16,2,98304]{2,1,0:T(2,128)(2,1)}), bf16[16,2,98304]{2,1,0:T(2,128)(2,1)}, u32[]{:S(2)}, u32[]{:S(2)}) async-start(bf16[16,2,98304]{2,1,0:T(2,128)(2,1)} %reshape.67), calls=%async_computation.1 | async-start | bytes 12582912 | tf_op jit(solution)/shard_map/all_to_all | solution.py:97
Sparse Core Ops, SparseCore 0:
  10.4 86.5 all-reduce.1
  99.8 87.8 all-gather.5
  189.4 51.1 all-gather.3
  261.0 53.9 reduce-scatter.1
where the time goes:
time: 549 us; the launch traced here: 541 us
  waiting for transfers between devices  283 us (52%)
  local copies, waits for them, and re-layouts  113 us (21%)
  matrix products  101 us (18%)
  other arithmetic  23.6 us (4%)
  between operations  14.1 us (3%)
  starting transfers between devices  7.38 us (1%)
    all_to_all x1, waiting for transfers between devices, local(): lax.all_to_all(per_owner, 'dp', split_axis=0, concat_axis=0, tiled=True)  107 us
    psum x1, waiting for transfers between devices, local(): summed = lax.psum(local_partial, 'tensor').astype(jnp.float32)  89 us
    all_gather x1, waiting for transfers between devices, local(): everyone = lax.all_gather(share_blocks, 'dp', axis=0, tiled=True)  85 us
    unnamed x14, local copies, waits for them, and re-layouts  36.7 us
    another operation x1, local copies, waits for them, and re-layouts, local(): jnp.stack([grad_keys, grad_values], axis=3).reshape(read_count, block_width)  22.2 us
    reshape x1, local copies, waits for them, and re-layouts, local(): jnp.stack([grad_keys, grad_values], axis=3).reshape(read_count, block_width)  21.3 us
    slice x1, local copies, waits for them, and re-layouts, local(): keys = layout[:, :, :, 0]  13.7 us
    dot_general x1, matrix products, local(): lax.dot_general(lax.all_gather(d_out, 'tensor', axis=1, tiled=True), w_ou...  13.5 us
  transfers between devices with their start and end apart: 5, of which 3 were waited for; matrix products, arithmetic and copies ran while one was open for 43% of the time, Pallas kernels for 0%

commit v1 on v0

v1 whole, which is shorter than its diff:
```python
import functools

import jax
import jax.numpy as jnp
from jax import lax
from jax.experimental import pallas as pl
from jax.experimental.pallas import tpu as pltpu
from jax.sharding import PartitionSpec as P

HD = 128
SPAN = 64
NBR_LEN = 128
NB_DEV = 2


def attention_kernel(heads, q_ref, kv_ref, g_ref, att_ref, dkv_ref):
    factor = HD ** (-0.5)
    for h in range(heads):
        cols = slice(h * HD, (h + 1) * HD)
        kcols = slice(2 * h * HD, 2 * h * HD + HD)
        vcols = slice(2 * h * HD + HD, 2 * (h + 1) * HD)
        q = q_ref[:, cols]
        g = g_ref[:, cols]
        k = jnp.concatenate([kv_ref[0, :, kcols], kv_ref[1, :, kcols]], axis=0)
        v = jnp.concatenate([kv_ref[0, :, vcols], kv_ref[1, :, vcols]], axis=0)
        scores = (
            lax.dot_general(q, k, (((1,), (1,)), ((), ())), preferred_element_type=jnp.float32)
            * factor
        )
        top = jnp.max(scores, axis=-1, keepdims=True)
        expo = jnp.exp(scores - top)
        probs = expo / jnp.sum(expo, axis=-1, keepdims=True)
        probs_low = probs.astype(jnp.bfloat16)
        attended = jnp.dot(probs_low, v, preferred_element_type=jnp.float32)
        att_ref[:, cols] = attended.astype(att_ref.dtype)
        grad_values = lax.dot_general(
            probs_low, g, (((0,), (0,)), ((), ())), preferred_element_type=jnp.float32
        )
        grad_probs = lax.dot_general(
            g, v, (((1,), (1,)), ((), ())), preferred_element_type=jnp.float32
        )
        grad_scores = probs * (grad_probs - jnp.sum(probs * grad_probs, axis=-1, keepdims=True))
        grad_scores = grad_scores.astype(jnp.bfloat16)
        grad_keys = (
            lax.dot_general(
                grad_scores, q, (((0,), (0,)), ((), ())), preferred_element_type=jnp.float32
            )
            * factor
        )
        dkv_ref[0, :, kcols] = grad_keys[:NBR_LEN]
        dkv_ref[1, :, kcols] = grad_keys[NBR_LEN:]
        dkv_ref[0, :, vcols] = grad_values[:NBR_LEN]
        dkv_ref[1, :, vcols] = grad_values[NBR_LEN:]


def attention(queries, neighbours, grad_attended):
    rows, width = queries.shape
    spans = rows // SPAN
    heads = width // HD
    kv_width = neighbours.shape[2]
    return pl.pallas_call(
        functools.partial(attention_kernel, heads),
        grid=(spans,),
        in_specs=[
            pl.BlockSpec((SPAN, width), lambda c: (c, 0)),
            pl.BlockSpec((2, NBR_LEN, kv_width), lambda c: (c, 0, 0)),
            pl.BlockSpec((SPAN, width), lambda c: (c, 0)),
        ],
        out_specs=[
            pl.BlockSpec((SPAN, width), lambda c: (c, 0)),
            pl.BlockSpec((2, NBR_LEN, kv_width), lambda c: (c, 0, 0)),
        ],
        out_shape=[
            jax.ShapeDtypeStruct((rows, width), jnp.bfloat16),
            jax.ShapeDtypeStruct(neighbours.shape, jnp.float32),
        ],
    )(queries, neighbours, grad_attended)


def local(kv_part, queries, w_out, d_out, nbr_owner, nbr_slot):
    dp_count = lax.axis_size("dp")
    reader = lax.axis_index("dp")
    head_width = w_out.shape[0]
    share_width = 2 * head_width
    span_count = queries.shape[0] // SPAN
    read_count = 2 * span_count
    block_width = NBR_LEN * share_width
    shares = lax.psum_scatter(kv_part[0], "tensor", scatter_dimension=1, tiled=True)
    share_blocks = shares.reshape(NB_DEV, NBR_LEN, share_width)
    owner_ids = jnp.arange(dp_count, dtype=jnp.int32)
    slot_ids = jnp.arange(NB_DEV, dtype=jnp.int32)
    owner_hits = nbr_owner[:, :, None] == owner_ids[None, None, :]
    per_reader = owner_hits.reshape(dp_count, read_count, dp_count)
    reads_from = jnp.any(per_reader, axis=1)
    slot_from = jnp.max(jnp.where(per_reader, nbr_slot.reshape(dp_count, read_count, 1), 0), axis=1)
    my_owner = lax.dynamic_slice_in_dim(nbr_owner, reader * span_count, span_count, 0).reshape(
        read_count
    )
    my_slot = lax.dynamic_slice_in_dim(nbr_slot, reader * span_count, span_count, 0).reshape(
        read_count
    )
    read_table = (my_owner[:, None] == owner_ids[None, :]).astype(jnp.float32)
    serving = lax.dynamic_index_in_dim(reads_from, reader, 1, False)
    serving_slot = lax.dynamic_index_in_dim(slot_from, reader, 1, False)
    owner_select = ((serving_slot[:, None] == slot_ids[None, :]) & serving[:, None]).astype(
        jnp.bfloat16
    )
    everyone = lax.all_gather(share_blocks, "dp", axis=0, tiled=True)
    neighbours = jnp.take(everyone, my_owner * NB_DEV + my_slot, axis=0)
    grad_attended = lax.dot_general(
        lax.all_gather(d_out, "tensor", axis=1, tiled=True),
        w_out,
        (((1,), (1,)), ((), ())),
        preferred_element_type=jnp.float32,
    ).astype(jnp.bfloat16)
    attended, grad_blocks = attention(queries, neighbours, grad_attended)
    partial_out = jnp.dot(attended, w_out, preferred_element_type=jnp.float32)
    mixed = lax.psum_scatter(
        partial_out.astype(jnp.bfloat16), "tensor", scatter_dimension=1, tiled=True
    )
    per_owner = lax.dot_general(
        read_table,
        grad_blocks.reshape(read_count, block_width),
        (((0,), (0,)), ((), ())),
        precision=lax.Precision.HIGHEST,
        preferred_element_type=jnp.float32,
    ).astype(jnp.bfloat16)
    returned = lax.all_to_all(per_owner, "dp", split_axis=0, concat_axis=0, tiled=True)
    owner_grad = lax.dot_general(
        owner_select, returned, (((0,), (0,)), ((), ())), preferred_element_type=jnp.float32
    )
    d_kv = owner_grad.astype(jnp.bfloat16).reshape(NB_DEV * NBR_LEN, share_width)
    return (mixed, d_kv)


def solution(mesh):
    placed = (
        P("tensor", "dp", None),
        P("dp", "tensor"),
        P("tensor", None),
        P("dp", "tensor"),
        P(),
        P(),
    )
    return jax.shard_map(
        local,
        mesh=mesh,
        in_specs=placed,
        out_specs=(P("dp", "tensor"), P("dp", "tensor")),
        check_vma=False,
    )
```

time: 549 us -> 445 us (0.81); the launches traced: 541 us -> 445 us
  local copies, waits for them, and re-layouts: 113 us -> 51.6 us
  matrix products: 101 us -> 50.9 us
  Pallas kernels: 0 us -> 24.4 us
  other arithmetic: 23.6 us -> 16.1 us
    psum x1 -> x0, waiting for transfers between devices: 89 us -> none  [local(): summed = lax.psum(local_partial, 'tensor').astype(jnp.float32)]
    dot_general x7 -> x1, matrix products: 60.9 us -> 11.1 us  [local(): lax.dot_general(read_table, grad_blocks.reshape(read_count, block_width),...]
    all_gather x1, waiting for transfers between devices: 0.02 us -> 49.8 us  [local(): lax.all_gather(d_out, 'tensor', axis=1, tiled=True)]
    reduce_scatter x0 -> x1, waiting for transfers between devices: none -> 46.5 us  [local(): lax.psum_scatter(kv_part[0], 'tensor', scatter_dimension=1, tiled=True)]
    reshape x4 -> x0, local copies, waits for them, and re-layouts: 36 us -> none  [the longest x1 21.3 us: local(): jnp.stack([grad_keys, grad_values], axis=3).reshape(read_count, block_width)]
    pallas_call x0 -> x1, Pallas kernels: none -> 24.4 us  [attention(): pl.pallas_call(functools.partial(attention_kernel, heads), grid=(spans,),...]
    another operation x1 -> x0, local copies, waits for them, and re-layouts: 22.2 us -> none  [local(): jnp.stack([grad_keys, grad_values], axis=3).reshape(read_count, block_width)]
    slice x1 -> x0, local copies, waits for them, and re-layouts: 13.7 us -> none  [local(): keys = layout[:, :, :, 0]]
  transfers between devices with their start and end apart: 5 -> 5, of which waited for: 3 -> 4; matrix products, arithmetic and copies ran while one was open for 43% -> 20% of each run, Pallas kernels for 0% -> 0%
where the time goes in v1:
time: 445 us
  waiting for transfers between devices  280 us (63%)
  local copies, waits for them, and re-layouts  51.6 us (12%)
  matrix products  50.9 us (11%)
  Pallas kernels  24.4 us (5%)
  other arithmetic  16.1 us (4%)
  between operations  13.8 us (3%)
  starting transfers between devices  7.51 us (2%)
    all_to_all x1, waiting for transfers between devices, local(): lax.all_to_all(per_owner, 'dp', split_axis=0, concat_axis=0, tiled=True)  105 us
    all_gather x1, waiting for transfers between devices, local(): everyone = lax.all_gather(share_blocks, 'dp', axis=0, tiled=True)  77.1 us
    all_gather x1, waiting for transfers between devices, local(): lax.all_gather(d_out, 'tensor', axis=1, tiled=True)  49.8 us
    reduce_scatter x1, waiting for transfers between devices, local(): lax.psum_scatter(kv_part[0], 'tensor', scatter_dimension=1, tiled=True)  46.5 us
    unnamed x9, local copies, waits for them, and re-layouts  40.3 us
    pallas_call x1, Pallas kernels, attention(): pl.pallas_call(functools.partial(attention_kernel, heads), grid=(spans,),...  24.4 us
    dot_general x1, matrix products, local(): partial_out = jnp.dot(attended, w_out, preferred_element_type=jnp.float32)  13.5 us
    dot_general x1, matrix products, local(): lax.dot_general(lax.all_gather(d_out, 'tensor', axis=1, tiled=True), w_ou...  13.5 us
  transfers between devices with their start and end apart: 5, of which 4 were waited for; matrix products, arithmetic and copies ran while one was open for 20% of the time, Pallas kernels for 0%

profile of v1, /device:TPU:28, one launch (start us, length us, event | category | flops | bytes accessed | tf_op | source)
XLA Modules:
  0.0 444.6 jit_solution(7498770549964050256)
XLA Ops:
  7.2 0.0 reduce-scatter.3.cloned.1.call-start
  7.2 0.7 reduce-scatter.3.cloned.1.call-update
  7.9 0.0 all-gather.5.cloned.1.call-start
  7.9 0.7 all-gather.5.cloned.1.call-update
  8.6 0.0 all-gather.3.cloned.1.call-start
  8.7 46.5 %reduce-scatter.3.cloned.1.call-done = bf16[256,1536]{1,0:T(8,128)(2,1)} async-done(((bf16[256,12288]{1,0:T(8,128)(2,1)}), bf16[256,1536]{1,0:T(8,128)(2,1)}) %reduce-scatter.3.cloned.1.call-update) | async-done | bytes 786448 | tf_op jit(solution)/shard_map/reduce_scatter | solution.py:88
  55.2 0.0 all-gather.3.cloned.1.call-update
  55.2 0.0 reduce-scatter.5.cloned.1.call-start
  55.3 0.8 multiply_add_fusion
  56.0 0.1 copy.34
  56.1 0.1 reshape.68
  56.2 0.1 copy.35
  56.3 0.1 reshape.69
  56.4 0.1 copy.36
  56.4 0.1 add.50
  56.6 49.8 %all-gather.5.cloned.1.call-done = bf16[512,8192]{1,0:T(8,128)(2,1)} async-done(((bf16[512,1024]{1,0:T(8,128)(2,1)}), bf16[512,8192]{1,0:T(8,128)(2,1)}) %all-gather.5.cloned.1.call-update) | async-done | bytes 8388624 | tf_op jit(solution)/shard_map/all_gather | solution.py:111
  106.4 13.5 %convolution_convert_fusion.3.g_ref = bf16[512,768]{1,0:T(8,128)(2,1)} fusion(bf16[512,8192]{1,0:T(8,128)(2,1)} %all-gather.5.cloned.1.call-done, bf16[768,8192]{1,0:T(8,128)(2,1)} %param.8), kind=kOutput, calls=%fused_computation.8 | convolution fusion | flops 6442844160 | bytes 21757952 | tf_op jit(solution)/shard_map/dot_general | solution.py:110
  119.9 77.1 %all-gather.3.cloned.1.call-done = bf16[32,128,1536]{2,1,0:T(8,128)(2,1)} async-done(((bf16[2,128,1536]{2,1,0:T(8,128)(2,1)}), bf16[32,128,1536]{2,1,0:T(8,128)(2,1)}) %all-gather.3.cloned.1.call-update) | async-done | bytes 12582928 | tf_op jit(solution)/shard_map/all_gather | solution.py:108
  197.0 8.1 %gather_fusion = bf16[16,128,1536]{2,1,0:T(8,128)(2,1)} fusion(bf16[32,128,1536]{2,1,0:T(8,128)(2,1)} %all-gather.3.cloned.1.call-done, s32[1024]{0:T(1024)S(1)} %pad_clamp_fusion), kind=kCustom, calls=%fused_computation | custom fusion | bytes 12582976 | tf_op jit(solution)/shard_map/jit(_take)/gather | solution.py:109
  205.1 6.1 %broadcast_select_fusion.kv_ref = bf16[16,128,1536]{2,1,0:T(8,128)(2,1)} fusion(bf16[16,128,1536]{2,1,0:T(8,128)(2,1)} %gather_fusion, pred[16]{0:T(512)(128)(4,1)S(1)} %compare_and_fusion), kind=kLoop, calls=%fused_computation.7 | loop fusion | flops 3145728 | bytes 12582928 | tf_op jit(solution)/shard_map/jit(_take)/select_n | solution.py:109
  211.2 24.4 %shard_map.77 = (bf16[512,768]{1,0:T(8,128)(2,1)}, f32[16,128,1536]{2,1,0:T(8,128)}) custom-call(bf16[512,768]{1,0:T(8,128)(2,1)} %q_ref.1, bf16[16,128,1536]{2,1,0:T(8,128)(2,1)} %broadcast_select_fusion.kv_ref, bf16[512,768]{1,0:T(8,128)(2,1)} %convolution_convert_fusion.3.g_ref), custom_call_target="tpu_custom_call" | custom-call | tf_op jit(solution)/shard_map/pallas_call | solution.py:61
  235.6 13.5 %convolution_convert_fusion.2 = bf16[512,8192]{1,0:T(8,128)(2,1)} fusion(bf16[512,768]{1,0:T(8,128)(2,1)} %get-tuple-element.4, bf16[768,8192]{1,0:T(8,128)(2,1)} %param.8), kind=kOutput, calls=%fused_computation.4 | convolution fusion | flops 6446645248 | bytes 21757952 | tf_op jit(solution)/shard_map/dot_general | solution.py:117
  249.2 0.0 reduce-scatter.5.cloned.1.call-update
  249.2 16.3 %copy.41 = f32[2,8,128,1536]{3,1,2,0:T(8,128)} copy(f32[2,8,128,1536]{3,2,1,0:T(8,128)} %bitcast.17) | data formatting | bytes 25165824
  265.5 11.1 %fusion = bf16[16,1,196608]{2,0,1:T(8,128)(2,1)} fusion(f32[16,196608]{1,0:T(8,128)} %bitcast.16, s32[16]{0:T(128)S(1)} %reshape.68), kind=kOutput, calls=%fused_computation.2 | convolution fusion | flops 607125760 | bytes 18874432 | tf_op jit(solution)/shard_map/dot_general | solution.py:121
  276.6 0.5 broadcast.60
  277.1 9.0 %reduce.4 = bf16[16,196608]{1,0:T(8,128)(2,1)} reduce(bf16[16,1,196608]{2,0,1:T(8,128)(2,1)} %fusion, bf16[]{:T(256)} %broadcast.60), dimensions={1}, to_apply=%copy.39.reduce_sub_computation | reduce | bytes 12582914 | tf_op jit(solution)/shard_map/all_to_all | solution.py:128
  286.1 9.4 %reshape.83 = bf16[16,2,98304]{2,1,0:T(2,128)(2,1)} reshape(bf16[16,196608]{1,0:T(8,128)(2,1)} %reduce.4) | data formatting | bytes 12582912
  295.5 0.0 copy-start
  295.5 0.0 copy-start.1
  295.5 7.4 %all-to-all-start = ((bf16[16,2,98304]{2,1,0:T(2,128)(2,1)}), bf16[16,2,98304]{2,1,0:T(2,128)(2,1)}, u32[]{:S(2)}, u32[]{:S(2)}) async-start(bf16[16,2,98304]{2,1,0:T(2,128)(2,1)} %reshape.83), calls=%async_computation.2 | async-start | bytes 12582912 | tf_op jit(solution)/shard_map/all_to_all | solution.py:128
  302.9 0.0 copy-done
  302.9 0.1 copy.37
  303.0 0.0 copy-done.1
  303.0 0.1 copy.38
  303.1 0.1 eq.44
  303.2 0.1 broadcast_in_dim.32
  303.3 0.2 select_reduce_fusion
  303.4 0.2 dynamic-slice_reduce_fusion
  303.6 0.1 fusion.3
  303.8 0.2 dynamic-slice_reduce_fusion.1
  303.9 105.4 %all-to-all-done = bf16[16,2,98304]{2,1,0:T(2,128)(2,1)} async-done(((bf16[16,2,98304]{2,1,0:T(2,128)(2,1)}), bf16[16,2,98304]{2,1,0:T(2,128)(2,1)}, u32[]{:S(2)}, u32[]{:S(2)}) %all-to-all-start) | async-done | bytes 6291488 | tf_op jit(solution)/shard_map/all_to_all | solution.py:128
  409.3 14.3 %reshape.84 = bf16[16,1,196608]{2,1,0:T(2,128)(2,1)} reshape(bf16[16,2,98304]{2,1,0:T(2,128)(2,1)} %all-to-all-done) | data formatting | bytes 12582912
  423.6 12.8 %convolution_convert_fusion.1 = bf16[2,196608]{1,0:T(2,128)(2,1)S(1)} fusion(bf16[16,1,196608]{2,1,0:T(2,128)(2,1)} %reshape.84, s32[16]{0:T(128)S(1)} %dynamic-slice_reduce_fusion, pred[16]{0:T(512)(128)(4,1)S(1)} %dynamic-slice_reduce_fusion.1), kind=kOutput, calls=%fused_computation.3 | convolution fusion | flops 12976192 | bytes 7077968 | tf_op jit(solution)/shard_map/dot_general | solution.py:129
  436.5 1.6 reshape.72
  438.1 0.0 reduce-scatter.5.cloned.1.call-done
  (3 shorter events, 0.0 us)
Async XLA Ops:
  7.2 48.0 %reduce-scatter.3.cloned.1.call-start = ((), (), s32[]{:S(2)}) async-start(), calls=%async_computation.3 | async-start | bytes 7077888 | tf_op jit(solution)/shard_map/reduce_scatter | solution.py:88
  7.9 98.5 %all-gather.5.cloned.1.call-start = ((), (), s32[]{:S(2)}) async-start(), calls=%async_computation.5 | async-start | bytes 9437184 | tf_op jit(solution)/shard_map/all_gather | solution.py:111
  8.6 188.3 %all-gather.3.cloned.1.call-start = ((), (), s32[]{:S(2)}) async-start(), calls=%async_computation.4 | async-start | bytes 13369344 | tf_op jit(solution)/shard_map/all_gather | solution.py:108
  55.2 382.9 %reduce-scatter.5.cloned.1.call-start = ((), (), s32[]{:S(2)}) async-start(), calls=%async_computation.6 | async-start | bytes 9437184 | tf_op jit(solution)/shard_map/reduce_scatter | solution.py:118
  295.5 7.4 %copy-start = (s32[128,2]{0,1:T(2,128)S(1)}, s32[128,2]{0,1:T(2,128)}, u32[]{:S(2)}) copy-start(s32[128,2]{0,1:T(2,128)} %param.10) | copy-start | bytes 3076
  295.5 7.5 %copy-start.1 = (s32[128,2]{0,1:T(2,128)S(1)}, s32[128,2]{0,1:T(2,128)}, u32[]{:S(2)}) copy-start(s32[128,2]{0,1:T(2,128)} %param.11) | copy-start | bytes 3076
  295.5 113.8 %all-to-all-start = ((bf16[16,2,98304]{2,1,0:T(2,128)(2,1)}), bf16[16,2,98304]{2,1,0:T(2,128)(2,1)}, u32[]{:S(2)}, u32[]{:S(2)}) async-start(bf16[16,2,98304]{2,1,0:T(2,128)(2,1)} %reshape.83), calls=%async_computation.2 | async-start | bytes 12582912 | tf_op jit(solution)/shard_map/all_to_all | solution.py:128
Sparse Core Ops, SparseCore 0:
  10.4 44.7 reduce-scatter.2
  56.9 49.4 all-gather.4
  108.6 88.3 all-gather.2
  249.3 53.9 reduce-scatter.4

commit v2 on v1

v2 whole, which is shorter than its diff:
```python
import functools

import jax
import jax.numpy as jnp
from jax import lax
from jax.experimental import pallas as pl
from jax.experimental.pallas import tpu as pltpu
from jax.sharding import PartitionSpec as P

HD = 128
SPAN = 64
NBR_LEN = 128
NB_DEV = 2


def attention_kernel(heads, owner_ref, pick_ref, q_ref, first_ref, second_ref, g_ref, att_ref, out_ref, acc_ref):
    factor = HD ** (-0.5)
    span = pl.program_id(0)

    @pl.when(span == 0)
    def _():
        acc_ref[...] = jnp.zeros_like(acc_ref)

    first = owner_ref[2 * span]
    second = owner_ref[2 * span + 1]
    for h in range(heads):
        cols = slice(h * HD, (h + 1) * HD)
        kcols = slice(2 * h * HD, 2 * h * HD + HD)
        vcols = slice(2 * h * HD + HD, 2 * (h + 1) * HD)
        q = q_ref[:, cols]
        g = g_ref[:, cols]
        k = jnp.concatenate([first_ref[0, :, kcols], second_ref[0, :, kcols]], axis=0)
        v = jnp.concatenate([first_ref[0, :, vcols], second_ref[0, :, vcols]], axis=0)
        scores = (
            lax.dot_general(q, k, (((1,), (1,)), ((), ())), preferred_element_type=jnp.float32)
            * factor
        )
        top = jnp.max(scores, axis=-1, keepdims=True)
        expo = jnp.exp(scores - top)
        probs = expo / jnp.sum(expo, axis=-1, keepdims=True)
        probs_low = probs.astype(jnp.bfloat16)
        attended = jnp.dot(probs_low, v, preferred_element_type=jnp.float32)
        att_ref[:, cols] = attended.astype(att_ref.dtype)
        grad_values = lax.dot_general(
            probs_low, g, (((0,), (0,)), ((), ())), preferred_element_type=jnp.float32
        )
        grad_probs = lax.dot_general(
            g, v, (((1,), (1,)), ((), ())), preferred_element_type=jnp.float32
        )
        grad_scores = probs * (grad_probs - jnp.sum(probs * grad_probs, axis=-1, keepdims=True))
        grad_scores = grad_scores.astype(jnp.bfloat16)
        grad_keys = (
            lax.dot_general(
                grad_scores, q, (((0,), (0,)), ((), ())), preferred_element_type=jnp.float32
            )
            * factor
        )
        acc_ref[first, :, kcols] += grad_keys[:NBR_LEN]
        acc_ref[second, :, kcols] += grad_keys[NBR_LEN:]
        acc_ref[first, :, vcols] += grad_values[:NBR_LEN]
        acc_ref[second, :, vcols] += grad_values[NBR_LEN:]

    @pl.when(span == pl.num_programs(0) - 1)
    def _():
        out_ref[...] = acc_ref[...].astype(out_ref.dtype)


def attention(owners, picks, queries, everyone, grad_attended, owner_count):
    rows, width = queries.shape
    spans = rows // SPAN
    heads = width // HD
    kv_width = everyone.shape[2]
    grid_spec = pltpu.PrefetchScalarGridSpec(
        num_scalar_prefetch=2,
        grid=(spans,),
        in_specs=[
            pl.BlockSpec((SPAN, width), lambda c, o, n: (c, 0)),
            pl.BlockSpec((1, NBR_LEN, kv_width), lambda c, o, n: (n[2 * c], 0, 0)),
            pl.BlockSpec((1, NBR_LEN, kv_width), lambda c, o, n: (n[2 * c + 1], 0, 0)),
            pl.BlockSpec((SPAN, width), lambda c, o, n: (c, 0)),
        ],
        out_specs=[
            pl.BlockSpec((SPAN, width), lambda c, o, n: (c, 0)),
            pl.BlockSpec((owner_count, NBR_LEN, kv_width), lambda c, o, n: (0, 0, 0)),
        ],
        scratch_shapes=[pltpu.VMEM((owner_count, NBR_LEN, kv_width), jnp.float32)],
    )
    return pl.pallas_call(
        functools.partial(attention_kernel, heads),
        grid_spec=grid_spec,
        out_shape=[
            jax.ShapeDtypeStruct((rows, width), jnp.bfloat16),
            jax.ShapeDtypeStruct((owner_count, NBR_LEN, kv_width), jnp.bfloat16),
        ],
        compiler_params=pltpu.CompilerParams(
            dimension_semantics=("arbitrary",), vmem_limit_bytes=56 * 1024 * 1024
        ),
    )(owners, picks, queries, everyone, everyone, grad_attended)


def slot_sum_kernel(readers, select_ref, returned_ref, out_ref):
    for slot in range(NB_DEV):
        total = returned_ref[0].astype(jnp.float32) * select_ref[0, slot]
        for r in range(1, readers):
            total = total + returned_ref[r].astype(jnp.float32) * select_ref[r, slot]
        out_ref[slot] = total.astype(out_ref.dtype)


def slot_sum(select, returned):
    readers, length, width = returned.shape
    tile = 256
    return pl.pallas_call(
        functools.partial(slot_sum_kernel, readers),
        grid=(width // tile,),
        in_specs=[
            pl.BlockSpec(memory_space=pltpu.SMEM),
            pl.BlockSpec((readers, length, tile), lambda j: (0, 0, j)),
        ],
        out_specs=pl.BlockSpec((NB_DEV, length, tile), lambda j: (0, 0, j)),
        out_shape=jax.ShapeDtypeStruct((NB_DEV, length, width), jnp.bfloat16),
    )(select, returned)


def local(kv_part, queries, w_out, d_out, nbr_owner, nbr_slot):
    dp_count = lax.axis_size("dp")
    reader = lax.axis_index("dp")
    head_width = w_out.shape[0]
    share_width = 2 * head_width
    span_count = queries.shape[0] // SPAN
    read_count = 2 * span_count
    shares = lax.psum_scatter(kv_part[0], "tensor", scatter_dimension=1, tiled=True)
    share_blocks = shares.reshape(NB_DEV, NBR_LEN, share_width)
    owner_ids = jnp.arange(dp_count, dtype=jnp.int32)
    slot_ids = jnp.arange(NB_DEV, dtype=jnp.int32)
    owner_hits = nbr_owner[:, :, None] == owner_ids[None, None, :]
    per_reader = owner_hits.reshape(dp_count, read_count, dp_count)
    reads_from = jnp.any(per_reader, axis=1)
    slot_from = jnp.max(jnp.where(per_reader, nbr_slot.reshape(dp_count, read_count, 1), 0), axis=1)
    my_owner = lax.dynamic_slice_in_dim(nbr_owner, reader * span_count, span_count, 0).reshape(
        read_count
    )
    my_slot = lax.dynamic_slice_in_dim(nbr_slot, reader * span_count, span_count, 0).reshape(
        read_count
    )
    serving = lax.dynamic_index_in_dim(reads_from, reader, 1, False)
    serving_slot = lax.dynamic_index_in_dim(slot_from, reader, 1, False)
    owner_select = ((serving_slot[:, None] == slot_ids[None, :]) & serving[:, None]).astype(
        jnp.float32
    )
    everyone = lax.all_gather(share_blocks, "dp", axis=0, tiled=True)
    picks = my_owner * NB_DEV + my_slot
    tensor_count = lax.axis_size("tensor")
    spread = jnp.broadcast_to(d_out[None], (tensor_count,) + d_out.shape)
    gathered = lax.all_to_all(spread, "tensor", split_axis=0, concat_axis=0, tiled=True)
    grad_attended = jnp.einsum(
        "tqc,htc->qh",
        gathered,
        w_out.reshape(head_width, tensor_count, d_out.shape[1]),
        preferred_element_type=jnp.float32,
    ).astype(jnp.bfloat16)
    attended, per_owner = attention(my_owner, picks, queries, everyone, grad_attended, dp_count)
    partial_out = jnp.dot(attended, w_out, preferred_element_type=jnp.float32)
    mixed = lax.psum_scatter(
        partial_out.astype(jnp.bfloat16), "tensor", scatter_dimension=1, tiled=True
    )
    returned = lax.all_to_all(per_owner, "dp", split_axis=0, concat_axis=0, tiled=True)
    owner_grad = slot_sum(owner_select, returned)
    d_kv = owner_grad.reshape(NB_DEV * NBR_LEN, share_width)
    return (mixed, d_kv)


def solution(mesh):
    placed = (
        P("tensor", "dp", None),
        P("dp", "tensor"),
        P("tensor", None),
        P("dp", "tensor"),
        P(),
        P(),
    )
    return jax.shard_map(
        local,
        mesh=mesh,
        in_specs=placed,
        out_specs=(P("dp", "tensor"), P("dp", "tensor")),
        check_vma=False,
    )
```

time: 445 us -> 341 us (0.77)
  local copies, waits for them, and re-layouts: 51.6 us -> 6.77 us
  waiting for transfers between devices: 280 us -> 244 us
  matrix products: 50.9 us -> 27.1 us
  other arithmetic: 16.1 us -> 1.54 us
  Pallas kernels: 24.4 us -> 35 us
  starting transfers between devices: 7.51 us -> 12.5 us
    all_to_all x0 -> x1, waiting for transfers between devices: none -> 93.6 us  [local(): lax.all_to_all(spread, 'tensor', split_axis=0, concat_axis=0, tiled=True)]
    all_gather x1, waiting for transfers between devices: 77.1 us -> 0.01 us  [local(): everyone = lax.all_gather(share_blocks, 'dp', axis=0, tiled=True)]
    all_gather x1 -> x0, waiting for transfers between devices: 49.8 us -> none  [local(): lax.all_gather(d_out, 'tensor', axis=1, tiled=True)]
    unnamed x9 -> x8, local copies, waits for them, and re-layouts: 40.3 us -> 0.24 us
    dot_general x3 -> x1, matrix products: 37.4 us -> 13.5 us  [local(): jnp.einsum('tqc,htc->qh', gathered, w_out.reshape(head_width, tensor_coun...]
    pallas_call x1 -> x2, Pallas kernels: 24.4 us -> 35 us  [the longest x1 28.5 us: attention(): pl.pallas_call(functools.partial(attention_kernel, heads), grid_spec=grid...]
    all_to_all x1 -> x0, other arithmetic: 9 us -> none  [local(): lax.all_to_all(per_owner, 'dp', split_axis=0, concat_axis=0, tiled=True)]
    gather x1 -> x0, local copies, waits for them, and re-layouts: 8.14 us -> none  [local(): neighbours = jnp.take(everyone, my_owner * NB_DEV + my_slot, axis=0)]
  transfers between devices with their start and end apart: 5 -> 5, of which waited for: 4 -> 3; matrix products, arithmetic and copies ran while one was open for 20% -> 6% of each run, Pallas kernels for 0% -> 2%
where the time goes in v2:
time: 341 us
  waiting for transfers between devices  244 us (72%)
  Pallas kernels  35 us (10%)
  matrix products  27.1 us (8%)
  between operations  13.8 us (4%)
  starting transfers between devices  12.5 us (4%)
  local copies, waits for them, and re-layouts  6.77 us (2%)
    all_to_all x1, waiting for transfers between devices, local(): lax.all_to_all(per_owner, 'dp', split_axis=0, concat_axis=0, tiled=True)  102 us
    all_to_all x1, waiting for transfers between devices, local(): lax.all_to_all(spread, 'tensor', split_axis=0, concat_axis=0, tiled=True)  93.6 us
    reduce_scatter x1, waiting for transfers between devices, local(): lax.psum_scatter(kv_part[0], 'tensor', scatter_dimension=1, tiled=True)  47.2 us
    pallas_call x1, Pallas kernels, attention(): pl.pallas_call(functools.partial(attention_kernel, heads), grid_spec=grid...  28.5 us
    dot_general x1, matrix products, local(): partial_out = jnp.dot(attended, w_out, preferred_element_type=jnp.float32)  13.6 us
    dot_general x1, matrix products, local(): jnp.einsum('tqc,htc->qh', gathered, w_out.reshape(head_width, tensor_coun...  13.5 us
    all_to_all x1, starting transfers between devices, local(): lax.all_to_all(per_owner, 'dp', split_axis=0, concat_axis=0, tiled=True)  7.25 us
  transfers between devices with their start and end apart: 5, of which 3 were waited for; matrix products, arithmetic and copies ran while one was open for 6% of the time, Pallas kernels for 2%

profile of v2, /device:TPU:28, one launch (start us, length us, event | category | flops | bytes accessed | tf_op | source)
XLA Modules:
  0.0 340.6 jit_solution(1480793557869925454)
XLA Ops:
  7.2 0.0 reduce-scatter.3.cloned.1.call-start
  7.2 0.7 reduce-scatter.3.cloned.1.call-update
  7.9 0.0 all-gather.2.cloned.1.call-start
  7.9 47.2 %reduce-scatter.3.cloned.1.call-done = bf16[256,1536]{1,0:T(8,128)(2,1)} async-done(((bf16[256,12288]{1,0:T(8,128)(2,1)}), bf16[256,1536]{1,0:T(8,128)(2,1)}) %reduce-scatter.3.cloned.1.call-update) | async-done | bytes 786448 | tf_op jit(solution)/shard_map/reduce_scatter | solution.py:131
  55.2 0.0 all-gather.2.cloned.1.call-update
  55.2 5.6 %broadcast_in_dim.16 = bf16[8,512,1024]{2,1,0:T(8,128)(2,1)} broadcast(bf16[512,1024]{1,0:T(8,128)(2,1)} %param.9), dimensions={1,2} | broadcast | bytes 9437184 | tf_op jit(solution)/shard_map/broadcast_in_dim | solution.py:153
  60.8 0.0 copy-start
  60.8 0.0 copy-start.1
  60.8 5.1 %all-to-all-start = ((bf16[8,512,1024]{2,1,0:T(8,128)(2,1)}), bf16[8,512,1024]{2,1,0:T(8,128)(2,1)}, u32[]{:S(2)}, u32[]{:S(2)}) async-start(bf16[8,512,1024]{2,1,0:T(8,128)(2,1)} %broadcast_in_dim.16), calls=%async_computation.1 | async-start | bytes 16777216 | tf_op jit(solution)/shard_map/all_to_all | solution.py:154
  66.0 0.0 reduce-scatter.5.cloned.1.call-start
  66.0 0.0 copy-done
  66.0 0.0 copy-done.1
  66.0 0.1 constant_dynamic-slice_fusion
  66.1 0.1 copy.26
  66.2 0.1 reshape.26.owner_ref
  66.3 0.0 copy-start.2
  66.3 0.1 copy.27
  66.4 0.1 reshape.27
  66.4 0.6 multiply_add_fusion.pick_ref
  67.0 93.6 %all-to-all-done = bf16[8,512,1024]{2,1,0:T(8,128)(2,1)} async-done(((bf16[8,512,1024]{2,1,0:T(8,128)(2,1)}), bf16[8,512,1024]{2,1,0:T(8,128)(2,1)}, u32[]{:S(2)}, u32[]{:S(2)}) %all-to-all-start) | async-done | bytes 8388640 | tf_op jit(solution)/shard_map/all_to_all | solution.py:154
  160.6 13.5 %bitcast_convert_fusion.g_ref = bf16[512,768]{1,0:T(8,128)(2,1)} fusion(bf16[8,512,1024]{2,1,0:T(8,128)(2,1)} %all-to-all-done, bf16[96,8,8,1024]{3,2,1,0:T(8,128)(2,1)} %bitcast.17), kind=kOutput, calls=%fused_computation.4 | convolution fusion | flops 6442844160 | bytes 21757952 | tf_op jit(solution)/shard_map/tqc,htc->qh/dot_general | solution.py:155
  174.1 0.0 copy-done.2
  174.1 0.0 all-gather.2.cloned.1.call-done.first_ref.second_ref
  174.1 28.5 %shard_map.77 = (bf16[512,768]{1,0:T(8,128)(2,1)}, bf16[16,128,1536]{2,1,0:T(8,128)(2,1)}) custom-call(s32[16]{0:T(128)} %copy-done.2, s32[16]{0:T(128)} %multiply_add_fusion.pick_ref, bf16[512,768]{1,0:T(8,128)(2,1)} %q_ref.1, bf16[32,128,1536]{2,1,0:T(8,128)(2,1)} %all-gather.2.cloned.1.call-done.first_ref.second_ref, ...), custom_call_target="tpu_custom_call" | custom-call | tf_op jit(solution)/shard_map/pallas_call | solution.py:88
  202.6 13.6 %convolution_convert_fusion = bf16[512,8192]{1,0:T(8,128)(2,1)} fusion(bf16[512,768]{1,0:T(8,128)(2,1)} %get-tuple-element.4, bf16[768,8192]{1,0:T(8,128)(2,1)} %param.8), kind=kOutput, calls=%fused_computation.3 | convolution fusion | flops 6446645248 | bytes 21757952 | tf_op jit(solution)/shard_map/dot_general | solution.py:162
  216.2 0.0 reduce-scatter.5.cloned.1.call-update
  216.2 7.2 %all-to-all-start.1 = ((bf16[16,128,1536]{2,1,0:T(8,128)(2,1)}), bf16[16,128,1536]{2,1,0:T(8,128)(2,1)}, u32[]{:S(2)}, u32[]{:S(2)}) async-start(bf16[16,128,1536]{2,1,0:T(8,128)(2,1)} %get-tuple-element.5), calls=%async_computation.3 | async-start | bytes 12582912 | tf_op jit(solution)/shard_map/all_to_all | solution.py:166
  223.5 0.1 copy.29
  223.6 0.1 copy.30
  223.7 0.1 eq.31
  223.8 0.1 broadcast_in_dim.26
  223.9 0.2 select_reduce_fusion
  224.0 0.2 dynamic-slice_reduce_fusion
  224.2 0.1 fusion.5
  224.3 0.2 dynamic-slice_reduce_fusion.1
  224.5 0.7 fusion.7.select_ref
  225.2 102.4 %all-to-all-done.1.returned_ref = bf16[16,128,1536]{2,1,0:T(8,128)(2,1)} async-done(((bf16[16,128,1536]{2,1,0:T(8,128)(2,1)}), bf16[16,128,1536]{2,1,0:T(8,128)(2,1)}, u32[]{:S(2)}, u32[]{:S(2)}) %all-to-all-start.1) | async-done | bytes 6291488 | tf_op jit(solution)/shard_map/all_to_all | solution.py:166
  327.6 6.5 %shard_map.78 = bf16[2,128,1536]{2,1,0:T(8,128)(2,1)} custom-call(f32[16,2]{1,0:T(8,128)} %fusion.7.select_ref, bf16[16,128,1536]{2,1,0:T(8,128)(2,1)} %all-to-all-done.1.returned_ref), custom_call_target="tpu_custom_call" | custom-call | tf_op jit(solution)/shard_map/pallas_call | solution.py:112
  334.1 0.0 reduce-scatter.5.cloned.1.call-done
Async XLA Ops:
  7.2 48.0 %reduce-scatter.3.cloned.1.call-start = ((), (), s32[]{:S(2)}) async-start(), calls=%async_computation.4 | async-start | bytes 7077888 | tf_op jit(solution)/shard_map/reduce_scatter | solution.py:131
  7.9 166.2 %all-gather.2.cloned.1.call-start = ((), (), s32[]{:S(2)}) async-start(), calls=%async_computation.5 | async-start | bytes 13369344 | tf_op jit(solution)/shard_map/all_gather | solution.py:150
  60.8 5.2 %copy-start = (s32[128,2]{0,1:T(2,128)S(1)}, s32[128,2]{0,1:T(2,128)}, u32[]{:S(2)}) copy-start(s32[128,2]{0,1:T(2,128)} %param.10) | copy-start | bytes 3076
  60.8 5.2 %copy-start.1 = (s32[128,2]{0,1:T(2,128)S(1)}, s32[128,2]{0,1:T(2,128)}, u32[]{:S(2)}) copy-start(s32[128,2]{0,1:T(2,128)} %param.11) | copy-start | bytes 3076
  60.8 99.8 %all-to-all-start = ((bf16[8,512,1024]{2,1,0:T(8,128)(2,1)}), bf16[8,512,1024]{2,1,0:T(8,128)(2,1)}, u32[]{:S(2)}, u32[]{:S(2)}) async-start(bf16[8,512,1024]{2,1,0:T(8,128)(2,1)} %broadcast_in_dim.16), calls=%async_computation.1 | async-start | bytes 16777216 | tf_op jit(solution)/shard_map/all_to_all | solution.py:154
  66.0 268.1 %reduce-scatter.5.cloned.1.call-start = ((), (), s32[]{:S(2)}) async-start(), calls=%async_computation.6 | async-start | bytes 9437184 | tf_op jit(solution)/shard_map/reduce_scatter | solution.py:163
  66.3 107.8 %copy-start.2 = (s32[16]{0:T(128)}, s32[16]{0:T(128)S(1)}, u32[]{:S(2)}) copy-start(s32[16]{0:T(128)S(1)} %reshape.26.owner_ref) | copy-start | bytes 196
  216.2 111.4 %all-to-all-start.1 = ((bf16[16,128,1536]{2,1,0:T(8,128)(2,1)}), bf16[16,128,1536]{2,1,0:T(8,128)(2,1)}, u32[]{:S(2)}, u32[]{:S(2)}) async-start(bf16[16,128,1536]{2,1,0:T(8,128)(2,1)} %get-tuple-element.5), calls=%async_computation.3 | async-start | bytes 12582912 | tf_op jit(solution)/shard_map/all_to_all | solution.py:166
Sparse Core Ops, SparseCore 0:
  10.4 44.7 reduce-scatter.2
  57.4 87.8 all-gather.1
  216.3 51.9 reduce-scatter.4

commit v3 on v2

--- a/solution.py
+++ b/solution.py
@@ -119,6 +119,46 @@
         out_specs=pl.BlockSpec((NB_DEV, length, tile), lambda j: (0, 0, j)),
         out_shape=jax.ShapeDtypeStruct((NB_DEV, length, width), jnp.bfloat16),
     )(select, returned)
+
+
+def exchange_kernel(x_ref, y_ref, send_sems, recv_sems, local_sem):
+    count = lax.axis_size("dp")
+    me = lax.axis_index("dp")
+    column = lax.axis_index("tensor")
+    copies = []
+    for step in range(1, count):
+        peer = lax.rem(me + step, count)
+        copy = pltpu.make_async_remote_copy(
+            src_ref=x_ref.at[peer],
+            dst_ref=y_ref.at[me],
+            send_sem=send_sems.at[step],
+            recv_sem=recv_sems.at[step],
+            device_id=(peer, column),
+            device_id_type=pl.DeviceIdType.MESH,
+        )
+        copy.start()
+        copies.append(copy)
+    own = pltpu.make_async_copy(x_ref.at[me], y_ref.at[me], local_sem)
+    own.start()
+    own.wait()
+    for copy in copies:
+        copy.wait()
+
+
+def exchange(blocks):
+    count = blocks.shape[0]
+    return pl.pallas_call(
+        exchange_kernel,
+        in_specs=[pl.BlockSpec(memory_space=pl.ANY)],
+        out_specs=pl.BlockSpec(memory_space=pl.ANY),
+        out_shape=jax.ShapeDtypeStruct(blocks.shape, blocks.dtype),
+        scratch_shapes=[
+            pltpu.SemaphoreType.DMA((count,)),
+            pltpu.SemaphoreType.DMA((count,)),
+            pltpu.SemaphoreType.DMA,
+        ],
+        compiler_params=pltpu.CompilerParams(has_side_effects=True),
+    )(blocks)
 
 
 def local(kv_part, queries, w_out, d_out, nbr_owner, nbr_slot):
@@ -147,15 +187,13 @@
     owner_select = ((serving_slot[:, None] == slot_ids[None, :]) & serving[:, None]).astype(
         jnp.float32
     )
-    everyone = lax.all_gather(share_blocks, "dp", axis=0, tiled=True)
-    picks = my_owner * NB_DEV + my_slot
-    tensor_count = lax.axis_size("tensor")
-    spread = jnp.broadcast_to(d_out[None], (tensor_count,) + d_out.shape)
-    gathered = lax.all_to_all(spread, "tensor", split_axis=0, concat_axis=0, tiled=True)
-    grad_attended = jnp.einsum(
-        "tqc,htc->qh",
-        gathered,
-        w_out.reshape(head_width, tensor_count, d_out.shape[1]),
+    outgoing = jnp.take(share_blocks, serving_slot, axis=0, mode="clip")
+    everyone = exchange(outgoing)
+    picks = my_owner
+    grad_attended = lax.dot_general(
+        lax.all_gather(d_out, "tensor", axis=1, tiled=True),
+        w_out,
+        (((1,), (1,)), ((), ())),
         preferred_element_type=jnp.float32,
     ).astype(jnp.bfloat16)
     attended, per_owner = attention(my_owner, picks, queries, everyone, grad_attended, dp_count)
@@ -163,7 +201,7 @@
     mixed = lax.psum_scatter(
         partial_out.astype(jnp.bfloat16), "tensor", scatter_dimension=1, tiled=True
     )
-    returned = lax.all_to_all(per_owner, "dp", split_axis=0, concat_axis=0, tiled=True)
+    returned = exchange(per_owner)
     owner_grad = slot_sum(owner_select, returned)
     d_kv = owner_grad.reshape(NB_DEV * NBR_LEN, share_width)
     return (mixed, d_kv)

time: 341 us -> 435 us (1.28)
  Pallas kernels: 35 us -> 340 us
  waiting for transfers between devices: 244 us -> 44.3 us
  starting transfers between devices: 12.5 us -> 0.11 us
    pallas_call x0 -> x2, Pallas kernels: none -> 305 us  [exchange(): pl.pallas_call(exchange_kernel, in_specs=[pl.BlockSpec(memory_space=pl.AN...]
    all_to_all x2 -> x0, waiting for transfers between devices: 196 us -> none  [the longest x1 102 us: local(): lax.all_to_all(per_owner, 'dp', split_axis=0, concat_axis=0, tiled=True)]
    all_to_all x2 -> x0, starting transfers between devices: 12.4 us -> none  [the longest x1 7.25 us: local(): lax.all_to_all(per_owner, 'dp', split_axis=0, concat_axis=0, tiled=True)]
    broadcast_in_dim x1 -> x0, local copies, waits for them, and re-layouts: 5.6 us -> none  [local(): spread = jnp.broadcast_to(d_out[None], (tensor_count,) + d_out.shape)]
    gather x0 -> x1, local copies, waits for them, and re-layouts: none -> 4.79 us  [local(): outgoing = jnp.take(share_blocks, serving_slot, axis=0, mode='clip')]
  transfers between devices with their start and end apart: 5 -> 3, of which waited for: 3 -> 1; matrix products, arithmetic and copies ran while one was open for 6% -> 2% of each run, Pallas kernels for 2% -> 72%
where the time goes in v3:
time: 435 us
  Pallas kernels  340 us (78%)
  waiting for transfers between devices  44.3 us (10%)
  matrix products  27.1 us (6%)
  between operations  13.8 us (3%)
  local copies, waits for them, and re-layouts  8.36 us (2%)
    pallas_call x2, Pallas kernels, exchange(): pl.pallas_call(exchange_kernel, in_specs=[pl.BlockSpec(memory_space=pl.AN...  305 us
    reduce_scatter x1, waiting for transfers between devices, local(): lax.psum_scatter(kv_part[0], 'tensor', scatter_dimension=1, tiled=True)  42.9 us
    pallas_call x1, Pallas kernels, attention(): pl.pallas_call(functools.partial(attention_kernel, heads), grid_spec=grid...  28.7 us
    dot_general x1, matrix products, local(): partial_out = jnp.dot(attended, w_out, preferred_element_type=jnp.float32)  13.6 us
    dot_general x1, matrix products, local(): lax.dot_general(lax.all_gather(d_out, 'tensor', axis=1, tiled=True), w_ou...  13.5 us
  transfers between devices with their start and end apart: 3, of which 1 were waited for; matrix products, arithmetic and copies ran while one was open for 2% of the time, Pallas kernels for 72%

profile of v3, /device:TPU:28, one launch (start us, length us, event | category | flops | bytes accessed | tf_op | source)
XLA Modules:
  0.0 434.7 jit_solution(10974046712137319439)
XLA Ops:
  7.2 0.0 reduce-scatter.3.cloned.1.call-start
  7.2 0.7 reduce-scatter.3.cloned.1.call-update
  7.9 0.0 all-gather.2.cloned.1.call-start
  7.9 0.7 all-gather.2.cloned.1.call-update
  8.6 0.0 reduce-scatter.5.cloned.1.call-start
  8.7 0.8 copy.16
  9.5 0.8 constant_dynamic-slice_fusion
  10.2 0.1 copy.15
  10.3 0.6 reshape.19.owner_ref.pick_ref
  10.9 0.8 copy.17
  11.7 0.1 broadcast_in_dim.21
  11.8 0.1 eq.31
  11.9 0.2 select_reduce_fusion
  12.1 0.2 dynamic-slice_reduce_fusion
  12.3 42.9 %reduce-scatter.3.cloned.1.call-done = bf16[256,1536]{1,0:T(8,128)(2,1)} async-done(((bf16[256,12288]{1,0:T(8,128)(2,1)}), bf16[256,1536]{1,0:T(8,128)(2,1)}) %reduce-scatter.3.cloned.1.call-update) | async-done | bytes 786448 | tf_op jit(solution)/shard_map/reduce_scatter | solution.py:171
  55.2 4.8 %gather_fusion = bf16[16,128,1536]{2,1,0:T(8,128)(2,1)} fusion(bf16[2,128,1536]{2,1,0:T(8,128)(2,1)} %bitcast.7, s32[1024]{0:T(1024)S(1)} %pad_clamp_fusion), kind=kCustom, calls=%fused_computation | custom fusion | bytes 12582976 | tf_op jit(solution)/shard_map/jit(_take)/gather | solution.py:190
  60.0 151.6 %shard_map.77.first_ref.second_ref = bf16[16,128,1536]{2,1,0:T(8,128)(2,1)} custom-call(bf16[16,128,1536]{2,1,0:T(8,128)(2,1)} %gather_fusion), custom_call_target="tpu_custom_call" | custom-call | tf_op jit(solution)/shard_map/pallas_call | solution.py:150
  211.5 0.0 all-gather.2.cloned.1.call-done
  211.6 13.5 %convolution_convert_fusion.1.g_ref = bf16[512,768]{1,0:T(8,128)(2,1)} fusion(bf16[512,8192]{1,0:T(8,128)(2,1)} %all-gather.2.cloned.1.call-done, bf16[768,8192]{1,0:T(8,128)(2,1)} %param.8), kind=kOutput, calls=%fused_computation.2 | convolution fusion | flops 6442844160 | bytes 21757952 | tf_op jit(solution)/shard_map/dot_general | solution.py:193
  225.1 28.7 %shard_map.78 = (bf16[512,768]{1,0:T(8,128)(2,1)}, bf16[16,128,1536]{2,1,0:T(8,128)(2,1)}) custom-call(s32[16]{0:T(128)} %reshape.19.owner_ref.pick_ref, s32[16]{0:T(128)} %reshape.19.owner_ref.pick_ref, bf16[512,768]{1,0:T(8,128)(2,1)} %q_ref.1, bf16[16,128,1536]{2,1,0:T(8,128)(2,1)} %shard_map.77.first_ref.second_ref, ...), custom_call_target="tpu_custom_call" | custom-call | tf_op jit(solution)/shard_map/pallas_call | solution.py:88
  253.8 13.6 %convolution_convert_fusion = bf16[512,8192]{1,0:T(8,128)(2,1)} fusion(bf16[512,768]{1,0:T(8,128)(2,1)} %get-tuple-element.4, bf16[768,8192]{1,0:T(8,128)(2,1)} %param.8), kind=kOutput, calls=%fused_computation.1 | convolution fusion | flops 6446645248 | bytes 21757952 | tf_op jit(solution)/shard_map/dot_general | solution.py:200
  267.3 0.0 reduce-scatter.5.cloned.1.call-update
  267.4 0.1 fusion
  267.5 0.2 dynamic-slice_reduce_fusion.1
  267.7 0.7 fusion.2.select_ref
  268.3 153.3 %shard_map.79.returned_ref = bf16[16,128,1536]{2,1,0:T(8,128)(2,1)} custom-call(bf16[16,128,1536]{2,1,0:T(8,128)(2,1)} %get-tuple-element.5.x_ref), custom_call_target="tpu_custom_call" | custom-call | tf_op jit(solution)/shard_map/pallas_call | solution.py:150
  421.7 6.5 %shard_map.80 = bf16[2,128,1536]{2,1,0:T(8,128)(2,1)} custom-call(f32[16,2]{1,0:T(8,128)} %fusion.2.select_ref, bf16[16,128,1536]{2,1,0:T(8,128)(2,1)} %shard_map.79.returned_ref), custom_call_target="tpu_custom_call" | custom-call | tf_op jit(solution)/shard_map/pallas_call | solution.py:112
  428.2 0.0 reduce-scatter.5.cloned.1.call-done
  (1 shorter events, 0.0 us)
Async XLA Ops:
  7.2 48.0 %reduce-scatter.3.cloned.1.call-start = ((), (), s32[]{:S(2)}) async-start(), calls=%async_computation.2 | async-start | bytes 7077888 | tf_op jit(solution)/shard_map/reduce_scatter | solution.py:171
  7.9 203.7 %all-gather.2.cloned.1.call-start = ((), (), s32[]{:S(2)}) async-start(), calls=%async_computation.3 | async-start | bytes 9437184 | tf_op jit(solution)/shard_map/all_gather | solution.py:194
  8.6 419.5 %reduce-scatter.5.cloned.1.call-start = ((), (), s32[]{:S(2)}) async-start(), calls=%async_computation.4 | async-start | bytes 9437184 | tf_op jit(solution)/shard_map/reduce_scatter | solution.py:201
Sparse Core Ops, SparseCore 0:
  10.4 44.7 reduce-scatter.2
  56.9 49.4 all-gather.1
  267.5 53.9 reduce-scatter.4

commit v4 on v2

--- a/solution.py
+++ b/solution.py
@@ -150,12 +150,29 @@
     everyone = lax.all_gather(share_blocks, "dp", axis=0, tiled=True)
     picks = my_owner * NB_DEV + my_slot
     tensor_count = lax.axis_size("tensor")
-    spread = jnp.broadcast_to(d_out[None], (tensor_count,) + d_out.shape)
-    gathered = lax.all_to_all(spread, "tensor", split_axis=0, concat_axis=0, tiled=True)
+    column = lax.axis_index("tensor")
+    direction = 1 - 2 * (column % 2)
+    ring = [(t, (t + 2 * (1 - 2 * (t % 2))) % tensor_count) for t in range(tensor_count)]
+    swap = [(t, t ^ 1) for t in range(tensor_count)]
+    hops = tensor_count // 2
+    mine = [d_out]
+    for _ in range(hops - 1):
+        mine.append(lax.ppermute(mine[-1], "tensor", ring))
+    theirs = [lax.ppermute(block, "tensor", swap) for block in mine]
+    steps = jnp.arange(hops, dtype=jnp.int32)
+    slot_block = jnp.concatenate(
+        [
+            (column - 2 * direction * steps) % tensor_count,
+            ((column ^ 1) + 2 * direction * steps) % tensor_count,
+        ]
+    )
+    w_slots = jnp.take(
+        w_out.reshape(head_width, tensor_count, d_out.shape[1]), slot_block, axis=1, mode="clip"
+    )
     grad_attended = jnp.einsum(
         "tqc,htc->qh",
-        gathered,
-        w_out.reshape(head_width, tensor_count, d_out.shape[1]),
+        jnp.stack(mine + theirs),
+        w_slots,
         preferred_element_type=jnp.float32,
     ).astype(jnp.bfloat16)
     attended, per_owner = attention(my_owner, picks, queries, everyone, grad_attended, dp_count)

time: 341 us -> 324 us (0.950)
  waiting for transfers between devices: 244 us -> 180 us
  local copies, waits for them, and re-layouts: 6.77 us -> 54.9 us
    all_to_all x1 -> x0, waiting for transfers between devices: 93.6 us -> none  [local(): lax.all_to_all(spread, 'tensor', split_axis=0, concat_axis=0, tiled=True)]
    unnamed x8 -> x18, local copies, waits for them, and re-layouts: 0.24 us -> 25.7 us
    ppermute x0 -> x7, waiting for transfers between devices: none -> 25.4 us  [the longest x3 25.4 us: local(): mine.append(lax.ppermute(mine[-1], 'tensor', ring))]
    reshape x0 -> x1, local copies, waits for them, and re-layouts: none -> 15.9 us  [local(): w_out.reshape(head_width, tensor_count, d_out.shape[1])]
    gather x0 -> x1, local copies, waits for them, and re-layouts: none -> 11.4 us  [local(): jnp.take(w_out.reshape(head_width, tensor_count, d_out.shape[1]), slot_bl...]
    broadcast_in_dim x1 -> x0, local copies, waits for them, and re-layouts: 5.6 us -> none  [local(): spread = jnp.broadcast_to(d_out[None], (tensor_count,) + d_out.shape)]
    all_to_all x1 -> x0, starting transfers between devices: 5.14 us -> none  [local(): lax.all_to_all(spread, 'tensor', split_axis=0, concat_axis=0, tiled=True)]
    all_to_all x1, waiting for transfers between devices: 102 us -> 107 us  [local(): lax.all_to_all(per_owner, 'dp', split_axis=0, concat_axis=0, tiled=True)]
  transfers between devices with their start and end apart: 5 -> 11, of which waited for: 3 -> 4; matrix products, arithmetic and copies ran while one was open for 6% -> 22% of each run, Pallas kernels for 2% -> 2%
where the time goes in v4:
time: 324 us; the launch traced here: 323 us
  waiting for transfers between devices  180 us (56%)
  local copies, waits for them, and re-layouts  54.9 us (17%)
  Pallas kernels  35 us (11%)
  matrix products  27.1 us (8%)
  between operations  13.8 us (4%)
  starting transfers between devices  10.9 us (3%)
    all_to_all x1, waiting for transfers between devices, local(): lax.all_to_all(per_owner, 'dp', split_axis=0, concat_axis=0, tiled=True)  107 us
    reduce_scatter x1, waiting for transfers between devices, local(): lax.psum_scatter(kv_part[0], 'tensor', scatter_dimension=1, tiled=True)  47.2 us
    pallas_call x1, Pallas kernels, attention(): pl.pallas_call(functools.partial(attention_kernel, heads), grid_spec=grid...  28.5 us
    unnamed x18, local copies, waits for them, and re-layouts  25.7 us
    ppermute x3, waiting for transfers between devices, local(): mine.append(lax.ppermute(mine[-1], 'tensor', ring))  25.4 us
    reshape x1, local copies, waits for them, and re-layouts, local(): w_out.reshape(head_width, tensor_count, d_out.shape[1])  15.9 us
    dot_general x1, matrix products, local(): partial_out = jnp.dot(attended, w_out, preferred_element_type=jnp.float32)  13.6 us
    dot_general x1, matrix products, local(): jnp.einsum('tqc,htc->qh', jnp.stack(mine + theirs), w_slots, preferred_el...  13.5 us
  transfers between devices with their start and end apart: 11, of which 4 were waited for; matrix products, arithmetic and copies ran while one was open for 22% of the time, Pallas kernels for 2%

profile of v4, /device:TPU:28, one launch (start us, length us, event | category | flops | bytes accessed | tf_op | source)
XLA Modules:
  0.0 323.3 jit_solution(1691240529859115954)
XLA Ops:
  7.2 0.0 reduce-scatter.3.cloned.1.call-start
  7.2 0.7 reduce-scatter.3.cloned.1.call-update
  7.9 0.0 all-gather.2.cloned.1.call-start
  7.9 47.2 %reduce-scatter.3.cloned.1.call-done = bf16[256,1536]{1,0:T(8,128)(2,1)} async-done(((bf16[256,12288]{1,0:T(8,128)(2,1)}), bf16[256,1536]{1,0:T(8,128)(2,1)}) %reduce-scatter.3.cloned.1.call-update) | async-done | bytes 786448 | tf_op jit(solution)/shard_map/reduce_scatter | solution.py:131
  55.2 0.0 all-gather.2.cloned.1.call-update
  55.2 0.0 reduce-scatter.5.cloned.1.call-start
  55.3 0.1 collective-permute-start
  55.3 16.2 %collective-permute-done = bf16[512,1024]{1,0:T(8,128)(2,1)S(1)} collective-permute-done((bf16[512,1024]{1,0:T(8,128)(2,1)}, bf16[512,1024]{1,0:T(8,128)(2,1)S(1)}, u32[]{:S(2)}, u32[]{:S(2)}) %collective-permute-start) | collective-permute-done | bytes 1048608 | tf_op jit(solution)/shard_map/ppermute | solution.py:160
  71.5 0.0 collective-permute-start.1
  71.5 0.4 collective-permute-start.3
  71.9 16.7 %copy.34 = bf16[768,8192]{0,1:T(8,128)(2,1)} copy(bf16[768,8192]{1,0:T(8,128)(2,1)} %param.8) | data formatting | bytes 25165824 | tf_op args[2]
  88.6 15.9 %copy.35 = bf16[768,8,1024]{2,0,1:T(8,128)(2,1)} copy(bf16[768,8,1024]{0,2,1:T(8,128)(2,1)} %bitcast.30) | data formatting | bytes 25165824 | tf_op jit(solution)/shard_map/reshape | solution.py:170
  104.5 0.1 constant_dynamic-slice_fusion
  104.6 0.1 copy.32
  104.7 0.1 reshape.25.owner_ref
  104.8 0.1 copy.33
  104.8 0.1 reshape.26
  105.0 0.1 pad_add_fusion
  105.0 11.4 %gather_fusion = bf16[8,768,1024]{2,1,0:T(8,128)(2,1)} fusion(bf16[768,8,1024]{2,0,1:T(8,128)(2,1)} %copy.35, s32[1024]{0:T(1024)S(1)} %pad_clamp_fusion), kind=kCustom, calls=%fused_computation | custom fusion | bytes 25165856 | tf_op jit(solution)/shard_map/jit(_take)/gather | solution.py:169
  116.5 1.1 bitcast_dynamic-update-slice_fusion.7
  117.6 0.5 multiply_add_fusion.pick_ref
  118.1 3.1 collective-permute-start.4
  121.2 1.0 bitcast_dynamic-update-slice_fusion.6
  122.2 0.0 collective-permute-start.5
  122.2 1.1 bitcast_dynamic-update-slice_fusion.5
  123.3 9.2 %collective-permute-done.2 = bf16[512,1024]{1,0:T(8,128)(2,1)S(1)} collective-permute-done((bf16[512,1024]{1,0:T(8,128)(2,1)S(1)}, bf16[512,1024]{1,0:T(8,128)(2,1)S(1)}, u32[]{:S(2)}, u32[]{:S(2)}) %collective-permute-start.2) | collective-permute-done | bytes 1048608 | tf_op jit(solution)/shard_map/ppermute | solution.py:160
  132.5 0.0 collective-permute-start.6
  132.5 1.1 bitcast_dynamic-update-slice_fusion.4
  133.6 2.3 bitcast_dynamic-update-slice_fusion.3
  135.9 1.1 bitcast_dynamic-update-slice_fusion.2
  136.9 1.1 bitcast_dynamic-update-slice_fusion.1
  138.0 1.0 bitcast_dynamic-update-slice_fusion
  139.1 13.5 %bitcast_convert_fusion.g_ref = bf16[512,768]{1,0:T(8,128)(2,1)} fusion(bf16[8,512,1024]{2,1,0:T(8,128)(2,1)} %bitcast_dynamic-update-slice_fusion, bf16[8,768,1024]{2,1,0:T(8,128)(2,1)} %gather_fusion), kind=kOutput, calls=%fused_computation.4 | convolution fusion | flops 6442844160 | bytes 21757952 | tf_op jit(solution)/shard_map/tqc,htc->qh/dot_general | solution.py:172
  152.6 28.5 %shard_map.77 = (bf16[512,768]{1,0:T(8,128)(2,1)}, bf16[16,128,1536]{2,1,0:T(8,128)(2,1)}) custom-call(s32[16]{0:T(128)} %copy-done.3, s32[16]{0:T(128)} %multiply_add_fusion.pick_ref, bf16[512,768]{1,0:T(8,128)(2,1)} %q_ref.1, bf16[32,128,1536]{2,1,0:T(8,128)(2,1)} %all-gather.2.cloned.1.call-done.first_ref.second_ref, ...), custom_call_target="tpu_custom_call" | custom-call | tf_op jit(solution)/shard_map/pallas_call | solution.py:88
  181.1 13.6 %convolution_convert_fusion = bf16[512,8192]{1,0:T(8,128)(2,1)} fusion(bf16[512,768]{1,0:T(8,128)(2,1)} %get-tuple-element.4, bf16[768,8192]{1,0:T(8,128)(2,1)} %param.8), kind=kOutput, calls=%fused_computation.3 | convolution fusion | flops 6446645248 | bytes 21757952 | tf_op jit(solution)/shard_map/dot_general | solution.py:179
  194.7 0.0 reduce-scatter.5.cloned.1.call-update
  194.7 7.2 %all-to-all-start = ((bf16[16,128,1536]{2,1,0:T(8,128)(2,1)}), bf16[16,128,1536]{2,1,0:T(8,128)(2,1)}, u32[]{:S(2)}, u32[]{:S(2)}) async-start(bf16[16,128,1536]{2,1,0:T(8,128)(2,1)} %get-tuple-element.5), calls=%async_computation.2 | async-start | bytes 12582912 | tf_op jit(solution)/shard_map/all_to_all | solution.py:183
  202.0 0.1 copy.36
  202.1 0.1 copy.37
  202.2 0.1 eq.36
  202.3 0.1 broadcast_in_dim.24
  202.3 0.2 select_reduce_fusion
  202.5 0.2 dynamic-slice_reduce_fusion
  202.7 0.1 fusion.4
  202.8 0.2 dynamic-slice_reduce_fusion.1
  203.0 0.7 fusion.6.select_ref
  203.7 106.6 %all-to-all-done.returned_ref = bf16[16,128,1536]{2,1,0:T(8,128)(2,1)} async-done(((bf16[16,128,1536]{2,1,0:T(8,128)(2,1)}), bf16[16,128,1536]{2,1,0:T(8,128)(2,1)}, u32[]{:S(2)}, u32[]{:S(2)}) %all-to-all-start) | async-done | bytes 6291488 | tf_op jit(solution)/shard_map/all_to_all | solution.py:183
  310.3 6.5 %shard_map.78 = bf16[2,128,1536]{2,1,0:T(8,128)(2,1)} custom-call(f32[16,2]{1,0:T(8,128)} %fusion.6.select_ref, bf16[16,128,1536]{2,1,0:T(8,128)(2,1)} %all-to-all-done.returned_ref), custom_call_target="tpu_custom_call" | custom-call | tf_op jit(solution)/shard_map/pallas_call | solution.py:112
  (18 shorter events, 0.1 us)
Async XLA Ops:
  7.2 48.0 %reduce-scatter.3.cloned.1.call-start = ((), (), s32[]{:S(2)}) async-start(), calls=%async_computation.3 | async-start | bytes 7077888 | tf_op jit(solution)/shard_map/reduce_scatter | solution.py:131
  7.9 144.7 %all-gather.2.cloned.1.call-start = ((), (), s32[]{:S(2)}) async-start(), calls=%async_computation.4 | async-start | bytes 13369344 | tf_op jit(solution)/shard_map/all_gather | solution.py:150
  55.2 261.6 %reduce-scatter.5.cloned.1.call-start = ((), (), s32[]{:S(2)}) async-start(), calls=%async_computation.5 | async-start | bytes 9437184 | tf_op jit(solution)/shard_map/reduce_scatter | solution.py:180
  55.3 16.3 %collective-permute-start = (bf16[512,1024]{1,0:T(8,128)(2,1)}, bf16[512,1024]{1,0:T(8,128)(2,1)S(1)}, u32[]{:S(2)}, u32[]{:S(2)}) collective-permute-start(bf16[512,1024]{1,0:T(8,128)(2,1)} %param.9), channel_id=1, source_target_pairs={{0,2},{1,7},{2,4},{3,1},{4,6},{5,3},{6,0},{7,5},{8,10},{9,15},{10,... | collective-permute-start | bytes 3145736 | tf_op jit(solution)/shard_map/ppermute | solution.py:160
  71.5 44.9 %collective-permute-start.1 = (bf16[512,1024]{1,0:T(8,128)(2,1)S(1)}, bf16[512,1024]{1,0:T(8,128)(2,1)S(1)}, u32[]{:S(2)}, u32[]{:S(2)}) collective-permute-start(bf16[512,1024]{1,0:T(8,128)(2,1)S(1)} %collective-permute-done), channel_id=1, source_target_pairs={{0,2},{1,7},{2,4},{3,1},{4,6},{5,3},{6,0},{7,5},{8,10},{9,15},{10,... | collective-permute-start | bytes 3145736 | tf_op jit(solution)/shard_map/ppermute | solution.py:160
  71.5 62.0 %collective-permute-start.3 = (bf16[512,1024]{1,0:T(8,128)(2,1)}, bf16[512,1024]{1,0:T(8,128)(2,1)}, u32[]{:S(2)}, u32[]{:S(2)}) collective-permute-start(bf16[512,1024]{1,0:T(8,128)(2,1)} %param.9), channel_id=1, source_target_pairs={{0,1},{1,0},{2,3},{3,2},{4,5},{5,4},{6,7},{7,6},{8,9},{9,8},{10,11... | collective-permute-start | bytes 3145736 | tf_op jit(solution)/shard_map/ppermute | solution.py:161
  88.6 15.9 %copy-start.1 = (s32[128,2]{0,1:T(2,128)S(1)}, s32[128,2]{0,1:T(2,128)}, u32[]{:S(2)}) copy-start(s32[128,2]{0,1:T(2,128)} %param.10) | copy-start | bytes 3076
  88.6 15.9 %copy-start.2 = (s32[128,2]{0,1:T(2,128)S(1)}, s32[128,2]{0,1:T(2,128)}, u32[]{:S(2)}) copy-start(s32[128,2]{0,1:T(2,128)} %param.11) | copy-start | bytes 3076
  104.8 12.8 %copy-start.3 = (s32[16]{0:T(128)}, s32[16]{0:T(128)S(1)}, u32[]{:S(2)}) copy-start(s32[16]{0:T(128)S(1)} %reshape.25.owner_ref) | copy-start | bytes 196
  105.0 11.4 %copy-start = (bf16[512,1024]{1,0:T(8,128)(2,1)S(1)}, bf16[512,1024]{1,0:T(8,128)(2,1)}, u32[]{:S(2)}) copy-start(bf16[512,1024]{1,0:T(8,128)(2,1)} %param.9) | copy-start | bytes 3145732
  116.5 16.0 %collective-permute-start.2 = (bf16[512,1024]{1,0:T(8,128)(2,1)S(1)}, bf16[512,1024]{1,0:T(8,128)(2,1)S(1)}, u32[]{:S(2)}, u32[]{:S(2)}) collective-permute-start(bf16[512,1024]{1,0:T(8,128)(2,1)S(1)} %collective-permute-done.1), channel_id=1, source_target_pairs={{0,2},{1,7},{2,4},{3,1},{4,6},{5,3},{6,0},{7,5},{8,10},{9,15},{10,... | collective-permute-start | bytes 3145736 | tf_op jit(solution)/shard_map/ppermute | solution.py:160
  118.1 17.8 %collective-permute-start.4 = (bf16[512,1024]{1,0:T(8,128)(2,1)S(1)}, bf16[512,1024]{1,0:T(8,128)(2,1)S(1)}, u32[]{:S(2)}, u32[]{:S(2)}) collective-permute-start(bf16[512,1024]{1,0:T(8,128)(2,1)S(1)} %collective-permute-done), channel_id=1, source_target_pairs={{0,1},{1,0},{2,3},{3,2},{4,5},{5,4},{6,7},{7,6},{8,9},{9,8},{10,11... | collective-permute-start | bytes 3145736 | tf_op jit(solution)/shard_map/ppermute | solution.py:161
  122.2 14.7 %collective-permute-start.5 = (bf16[512,1024]{1,0:T(8,128)(2,1)S(1)}, bf16[512,1024]{1,0:T(8,128)(2,1)S(1)}, u32[]{:S(2)}, u32[]{:S(2)}) collective-permute-start(bf16[512,1024]{1,0:T(8,128)(2,1)S(1)} %collective-permute-done.1), channel_id=1, source_target_pairs={{0,1},{1,0},{2,3},{3,2},{4,5},{5,4},{6,7},{7,6},{8,9},{9,8},{10,11... | collective-permute-start | bytes 3145736 | tf_op jit(solution)/shard_map/ppermute | solution.py:161
  132.5 5.5 %collective-permute-start.6 = (bf16[512,1024]{1,0:T(8,128)(2,1)S(1)}, bf16[512,1024]{1,0:T(8,128)(2,1)S(1)}, u32[]{:S(2)}, u32[]{:S(2)}) collective-permute-start(bf16[512,1024]{1,0:T(8,128)(2,1)S(1)} %collective-permute-done.2), channel_id=1, source_target_pairs={{0,1},{1,0},{2,3},{3,2},{4,5},{5,4},{6,7},{7,6},{8,9},{9,8},{10,11... | collective-permute-start | bytes 3145736 | tf_op jit(solution)/shard_map/ppermute | solution.py:161
  194.7 115.6 %all-to-all-start = ((bf16[16,128,1536]{2,1,0:T(8,128)(2,1)}), bf16[16,128,1536]{2,1,0:T(8,128)(2,1)}, u32[]{:S(2)}, u32[]{:S(2)}) async-start(bf16[16,128,1536]{2,1,0:T(8,128)(2,1)} %get-tuple-element.5), calls=%async_computation.2 | async-start | bytes 12582912 | tf_op jit(solution)/shard_map/all_to_all | solution.py:183
Sparse Core Ops, SparseCore 0:
  10.4 44.7 reduce-scatter.2
  57.4 87.8 all-gather.1
  194.8 53.1 reduce-scatter.4

commit v5 on v4

--- a/solution.py
+++ b/solution.py
@@ -98,29 +98,6 @@
     )(owners, picks, queries, everyone, everyone, grad_attended)
 
 
-def slot_sum_kernel(readers, select_ref, returned_ref, out_ref):
-    for slot in range(NB_DEV):
-        total = returned_ref[0].astype(jnp.float32) * select_ref[0, slot]
-        for r in range(1, readers):
-            total = total + returned_ref[r].astype(jnp.float32) * select_ref[r, slot]
-        out_ref[slot] = total.astype(out_ref.dtype)
-
-
-def slot_sum(select, returned):
-    readers, length, width = returned.shape
-    tile = 256
-    return pl.pallas_call(
-        functools.partial(slot_sum_kernel, readers),
-        grid=(width // tile,),
-        in_specs=[
-            pl.BlockSpec(memory_space=pltpu.SMEM),
-            pl.BlockSpec((readers, length, tile), lambda j: (0, 0, j)),
-        ],
-        out_specs=pl.BlockSpec((NB_DEV, length, tile), lambda j: (0, 0, j)),
-        out_shape=jax.ShapeDtypeStruct((NB_DEV, length, width), jnp.bfloat16),
-    )(select, returned)
-
-
 def local(kv_part, queries, w_out, d_out, nbr_owner, nbr_slot):
     dp_count = lax.axis_size("dp")
     reader = lax.axis_index("dp")
@@ -134,18 +111,12 @@
     slot_ids = jnp.arange(NB_DEV, dtype=jnp.int32)
     owner_hits = nbr_owner[:, :, None] == owner_ids[None, None, :]
     per_reader = owner_hits.reshape(dp_count, read_count, dp_count)
-    reads_from = jnp.any(per_reader, axis=1)
     slot_from = jnp.max(jnp.where(per_reader, nbr_slot.reshape(dp_count, read_count, 1), 0), axis=1)
     my_owner = lax.dynamic_slice_in_dim(nbr_owner, reader * span_count, span_count, 0).reshape(
         read_count
     )
     my_slot = lax.dynamic_slice_in_dim(nbr_slot, reader * span_count, span_count, 0).reshape(
         read_count
-    )
-    serving = lax.dynamic_index_in_dim(reads_from, reader, 1, False)
-    serving_slot = lax.dynamic_index_in_dim(slot_from, reader, 1, False)
-    owner_select = ((serving_slot[:, None] == slot_ids[None, :]) & serving[:, None]).astype(
-        jnp.float32
     )
     everyone = lax.all_gather(share_blocks, "dp", axis=0, tiled=True)
     picks = my_owner * NB_DEV + my_slot
@@ -176,13 +147,41 @@
         preferred_element_type=jnp.float32,
     ).astype(jnp.bfloat16)
     attended, per_owner = attention(my_owner, picks, queries, everyone, grad_attended, dp_count)
-    partial_out = jnp.dot(attended, w_out, preferred_element_type=jnp.float32)
-    mixed = lax.psum_scatter(
-        partial_out.astype(jnp.bfloat16), "tensor", scatter_dimension=1, tiled=True
-    )
-    returned = lax.all_to_all(per_owner, "dp", split_axis=0, concat_axis=0, tiled=True)
-    owner_grad = slot_sum(owner_select, returned)
+    partial_out = jnp.dot(attended, w_out, preferred_element_type=jnp.float32).astype(
+        jnp.bfloat16
+    )
+    slot_mask = lax.dynamic_index_in_dim(slot_from, reader, 0, False)[:, None] == slot_ids[None, :]
+    expanded = jnp.where(slot_mask[:, :, None, None], per_owner[:, None], jnp.zeros_like(per_owner[:, None]))
+    owner_grad = lax.psum_scatter(
+        expanded.reshape(dp_count * NB_DEV, NBR_LEN, share_width),
+        "dp",
+        scatter_dimension=0,
+        tiled=True,
+    )
     d_kv = owner_grad.reshape(NB_DEV * NBR_LEN, share_width)
+    cycle = list(range(0, tensor_count, 2)) + list(range(tensor_count - 1, 0, -2))
+    position_of = [cycle.index(t) for t in range(tensor_count)]
+    rightward = [(cycle[p], cycle[(p + 1) % tensor_count]) for p in range(tensor_count)]
+    leftward = [(cycle[p], cycle[(p - 1) % tensor_count]) for p in range(tensor_count)]
+    cycle_table = jnp.array(cycle, dtype=jnp.int32)
+    position = jnp.array(position_of, dtype=jnp.int32)[column]
+    block_width = partial_out.shape[1] // tensor_count
+    half = block_width // 2
+
+    def piece(offset, part):
+        block = cycle_table[(position + offset) % tensor_count]
+        return lax.dynamic_slice_in_dim(partial_out, block * block_width + part * half, half, 1)
+
+    halves = []
+    for part, perm, sign in ((0, rightward, -1), (1, leftward, 1)):
+        acc = piece(sign, part)
+        for step in range(tensor_count - 1):
+            arrived = lax.ppermute(acc, "tensor", perm)
+            acc = (
+                arrived.astype(jnp.float32) + piece(sign * (step + 2), part).astype(jnp.float32)
+            ).astype(jnp.bfloat16)
+        halves.append(acc)
+    mixed = jnp.concatenate(halves, axis=1)
     return (mixed, d_kv)
 
 

time: 324 us -> 337 us (1.040)
  waiting for transfers between devices: 180 us -> 150 us
  between operations: 13.8 us -> 33.8 us
  other arithmetic: 1.54 us -> 20.8 us
  Pallas kernels: 35 us -> 28.5 us
  local copies, waits for them, and re-layouts: 54.9 us -> 60.1 us
  starting transfers between devices: 10.9 us -> 15.8 us
    all_to_all x1 -> x0, waiting for transfers between devices: 107 us -> none  [local(): lax.all_to_all(per_owner, 'dp', split_axis=0, concat_axis=0, tiled=True)]
    ppermute x0 -> x14, waiting for transfers between devices: none -> 76.1 us  [local(): arrived = lax.ppermute(acc, 'tensor', perm)]
    ppermute x0 -> x14, starting transfers between devices: none -> 12.1 us  [local(): arrived = lax.ppermute(acc, 'tensor', perm)]
    convert_element_type x1 -> x7, other arithmetic: 0.68 us -> 10.5 us  [local(): acc = (arrived.astype(jnp.float32) + piece(sign * (step + 2), part).astyp...]
    select_n x0 -> x1, other arithmetic: none -> 8.41 us  [local(): jnp.where(slot_mask[:, :, None, None], per_owner[:, None], jnp.zeros_like...]
    all_to_all x1 -> x0, starting transfers between devices: 7.24 us -> none  [local(): lax.all_to_all(per_owner, 'dp', split_axis=0, concat_axis=0, tiled=True)]
    pallas_call x1 -> x0, Pallas kernels: 6.46 us -> none  [slot_sum(): pl.pallas_call(functools.partial(slot_sum_kernel, readers), grid=(width /...]
    unnamed x18 -> x26, local copies, waits for them, and re-layouts: 25.7 us -> 29.4 us
  transfers between devices with their start and end apart: 11 -> 24, of which waited for: 4 -> 14; matrix products, arithmetic and copies ran while one was open for 22% -> 28% of each run, Pallas kernels for 2% -> 0%
where the time goes in v5:
time: 337 us; the launch traced here: 334 us
  waiting for transfers between devices  150 us (45%)
  local copies, waits for them, and re-layouts  60.1 us (18%)
  between operations  33.8 us (10%)
  Pallas kernels  28.5 us (8%)
  matrix products  25.7 us (8%)
  other arithmetic  20.8 us (6%)
  starting transfers between devices  15.8 us (5%)
    ppermute x14, waiting for transfers between devices, local(): arrived = lax.ppermute(acc, 'tensor', perm)  76.1 us
    reduce_scatter x1, waiting for transfers between devices, local(): lax.psum_scatter(kv_part[0], 'tensor', scatter_dimension=1, tiled=True)  47.2 us
    unnamed x26, local copies, waits for them, and re-layouts  29.4 us
    pallas_call x1, Pallas kernels, attention(): pl.pallas_call(functools.partial(attention_kernel, heads), grid_spec=grid...  28.5 us
    ppermute x3, waiting for transfers between devices, local(): mine.append(lax.ppermute(mine[-1], 'tensor', ring))  25.5 us
    reshape x1, local copies, waits for them, and re-layouts, local(): w_out.reshape(head_width, tensor_count, d_out.shape[1])  15.9 us
    dot_general x1, matrix products, local(): jnp.einsum('tqc,htc->qh', jnp.stack(mine + theirs), w_slots, preferred_el...  13.5 us
    dot_general x1, matrix products, local(): jnp.dot(attended, w_out, preferred_element_type=jnp.float32)  12.1 us
  transfers between devices with their start and end apart: 24, of which 14 were waited for; matrix products, arithmetic and copies ran while one was open for 28% of the time, Pallas kernels for 0%

profile of v5, /device:TPU:28, one launch (start us, length us, event | category | flops | bytes accessed | tf_op | source)
XLA Modules:
  0.0 334.2 jit_solution(3179988900769308740)
XLA Ops:
  7.2 0.7 reduce-scatter.3.cloned.1.call-update
  7.9 47.2 %reduce-scatter.3.cloned.1.call-done = bf16[256,1536]{1,0:T(8,128)(2,1)} async-done(((bf16[256,12288]{1,0:T(8,128)(2,1)}), bf16[256,1536]{1,0:T(8,128)(2,1)}) %reduce-scatter.3.cloned.1.call-update) | async-done | bytes 786448 | tf_op jit(solution)/shard_map/reduce_scatter | solution.py:108
  55.3 16.2 %collective-permute-done = bf16[512,1024]{1,0:T(8,128)(2,1)S(1)} collective-permute-done((bf16[512,1024]{1,0:T(8,128)(2,1)}, bf16[512,1024]{1,0:T(8,128)(2,1)S(1)}, u32[]{:S(2)}, u32[]{:S(2)}) %collective-permute-start) | collective-permute-done | bytes 1048608 | tf_op jit(solution)/shard_map/ppermute | solution.py:131
  71.9 16.8 %copy.30 = bf16[768,8192]{0,1:T(8,128)(2,1)} copy(bf16[768,8192]{1,0:T(8,128)(2,1)} %param.10) | data formatting | bytes 25165824 | tf_op args[2]
  88.7 15.9 %copy.31 = bf16[768,8,1024]{2,0,1:T(8,128)(2,1)} copy(bf16[768,8,1024]{0,2,1:T(8,128)(2,1)} %bitcast.74) | data formatting | bytes 25165824 | tf_op jit(solution)/shard_map/reshape | solution.py:141
  105.9 11.5 %gather_fusion = bf16[8,768,1024]{2,1,0:T(8,128)(2,1)} fusion(bf16[768,8,1024]{2,0,1:T(8,128)(2,1)} %copy.31, s32[1024]{0:T(1024)S(1)} %pad_clamp_fusion), kind=kCustom, calls=%fused_computation | custom fusion | bytes 25165856 | tf_op jit(solution)/shard_map/jit(_take)/gather | solution.py:140
  117.4 1.0 bitcast_dynamic-update-slice_fusion.7
  118.9 3.1 collective-permute-start.4
  122.1 1.1 bitcast_dynamic-update-slice_fusion.6
  123.1 1.0 bitcast_dynamic-update-slice_fusion.5
  124.2 9.3 %collective-permute-done.2 = bf16[512,1024]{1,0:T(8,128)(2,1)S(1)} collective-permute-done((bf16[512,1024]{1,0:T(8,128)(2,1)S(1)}, bf16[512,1024]{1,0:T(8,128)(2,1)S(1)}, u32[]{:S(2)}, u32[]{:S(2)}) %collective-permute-start.2) | collective-permute-done | bytes 1048608 | tf_op jit(solution)/shard_map/ppermute | solution.py:131
  133.4 1.1 bitcast_dynamic-update-slice_fusion.4
  134.5 2.3 bitcast_dynamic-update-slice_fusion.3
  136.8 1.1 bitcast_dynamic-update-slice_fusion.2
  137.8 1.0 bitcast_dynamic-update-slice_fusion.1
  138.9 1.1 bitcast_dynamic-update-slice_fusion
  140.0 13.5 %bitcast_convert_fusion.g_ref = bf16[512,768]{1,0:T(8,128)(2,1)} fusion(bf16[8,512,1024]{2,1,0:T(8,128)(2,1)} %bitcast_dynamic-update-slice_fusion, bf16[8,768,1024]{2,1,0:T(8,128)(2,1)} %gather_fusion), kind=kOutput, calls=%fused_computation.5 | convolution fusion | flops 6442844160 | bytes 21757952 | tf_op jit(solution)/shard_map/tqc,htc->qh/dot_general | solution.py:143
  153.5 28.5 %shard_map.95 = (bf16[512,768]{1,0:T(8,128)(2,1)}, bf16[16,128,1536]{2,1,0:T(8,128)(2,1)}) custom-call(s32[16]{0:T(128)} %copy-done.5, s32[16]{0:T(128)} %multiply_add_fusion.pick_ref, bf16[512,768]{1,0:T(8,128)(2,1)} %q_ref.1, bf16[32,128,1536]{2,1,0:T(8,128)(2,1)} %all-gather.2.cloned.1.call-done.first_ref.second_ref, ...), custom_call_target="tpu_custom_call" | custom-call | tf_op jit(solution)/shard_map/pallas_call | solution.py:88
  182.0 8.4 %bitcast_select_fusion = bf16[32,128,1536]{2,1,0:T(8,128)(2,1)} fusion(pred[32]{0:T(512)(128)(4,1)S(1)} %eq.67, bf16[16,128,1536]{2,1,0:T(8,128)(2,1)} %get-tuple-element.5), kind=kLoop, calls=%fused_computation.1 | loop fusion | flops 6291456 | bytes 18874400 | tf_op jit(solution)/shard_map/jit(_where)/select_n | solution.py:154
  190.5 0.6 copy-done.7
  201.7 0.8 fusion.7
  203.8 12.1 %convolution_convert_fusion = bf16[512,8192]{1,0:T(8,128)(2,1)S(1)} fusion(bf16[512,768]{1,0:T(8,128)(2,1)S(1)} %copy-done.6, bf16[768,8192]{1,0:T(8,128)(2,1)} %param.10), kind=kOutput, calls=%fused_computation.4 | convolution fusion | flops 6446645248 | bytes 21757952 | tf_op jit(solution)/shard_map/dot_general | solution.py:150
  215.9 3.2 copy-done
  219.7 1.5 collective-permute-start.7
  222.5 11.1 %collective-permute-done.14 = bf16[512,512]{1,0:T(8,128)(2,1)S(1)} collective-permute-done((bf16[512,512]{1,0:T(8,128)(2,1)S(1)}, bf16[512,512]{1,0:T(8,128)(2,1)S(1)}, u32[]{:S(2)}, u32[]{:S(2)}) %collective-permute-start.14) | collective-permute-done | bytes 524320 | tf_op jit(solution)/shard_map/ppermute | solution.py:179
  233.6 1.5 add_convert_fusion.13
  235.2 2.0 collective-permute-start.8
  238.4 11.2 %collective-permute-done.15 = bf16[512,512]{1,0:T(8,128)(2,1)S(1)} collective-permute-done((bf16[512,512]{1,0:T(8,128)(2,1)S(1)}, bf16[512,512]{1,0:T(8,128)(2,1)S(1)}, u32[]{:S(2)}, u32[]{:S(2)}) %collective-permute-start.15) | collective-permute-done | bytes 524320 | tf_op jit(solution)/shard_map/ppermute | solution.py:179
  249.7 1.5 add_convert_fusion.12
  251.2 2.0 collective-permute-start.9
  254.4 11.1 %collective-permute-done.16 = bf16[512,512]{1,0:T(8,128)(2,1)S(1)} collective-permute-done((bf16[512,512]{1,0:T(8,128)(2,1)S(1)}, bf16[512,512]{1,0:T(8,128)(2,1)S(1)}, u32[]{:S(2)}, u32[]{:S(2)}) %collective-permute-start.16) | collective-permute-done | bytes 524320 | tf_op jit(solution)/shard_map/ppermute | solution.py:179
  265.5 1.5 add_convert_fusion.11
  268.7 10.7 %collective-permute-done.10 = bf16[512,512]{1,0:T(8,128)(2,1)S(1)} collective-permute-done((bf16[512,512]{1,0:T(8,128)(2,1)S(1)}, bf16[512,512]{1,0:T(8,128)(2,1)S(1)}, u32[]{:S(2)}, u32[]{:S(2)}) %collective-permute-start.10) | collective-permute-done | bytes 524320 | tf_op jit(solution)/shard_map/ppermute | solution.py:179
  279.4 1.0 collective-permute-done.17
  280.5 1.5 add_convert_fusion.10
  282.0 1.5 collective-permute-start.11
  284.7 10.4 %collective-permute-done.11 = bf16[512,512]{1,0:T(8,128)(2,1)S(1)} collective-permute-done((bf16[512,512]{1,0:T(8,128)(2,1)S(1)}, bf16[512,512]{1,0:T(8,128)(2,1)S(1)}, u32[]{:S(2)}, u32[]{:S(2)}) %collective-permute-start.11) | collective-permute-done | bytes 524320 | tf_op jit(solution)/shard_map/ppermute | solution.py:179
  295.2 0.7 collective-permute-done.18
  295.9 1.5 add_convert_fusion.9
  297.4 1.8 collective-permute-start.12
  300.5 9.7 %collective-permute-done.12 = bf16[512,512]{1,0:T(8,128)(2,1)S(1)} collective-permute-done((bf16[512,512]{1,0:T(8,128)(2,1)S(1)}, bf16[512,512]{1,0:T(8,128)(2,1)S(1)}, u32[]{:S(2)}, u32[]{:S(2)}) %collective-permute-start.12) | collective-permute-done | bytes 524320 | tf_op jit(solution)/shard_map/ppermute | solution.py:179
  310.1 0.7 collective-permute-done.19
  310.8 1.5 add_convert_fusion.8
  312.3 2.1 collective-permute-start.13
  315.7 8.8 %collective-permute-done.13 = bf16[512,512]{1,0:T(8,128)(2,1)S(1)} collective-permute-done((bf16[512,512]{1,0:T(8,128)(2,1)S(1)}, bf16[512,512]{1,0:T(8,128)(2,1)S(1)}, u32[]{:S(2)}, u32[]{:S(2)}) %collective-permute-start.13) | collective-permute-done | bytes 524320 | tf_op jit(solution)/shard_map/ppermute | solution.py:179
  324.5 0.7 collective-permute-done.20
  325.1 1.5 add_convert_fusion.7
  326.6 1.1 pad_maximum_fusion
  (62 shorter events, 4.2 us)
Async XLA Ops:
  7.2 48.0 %reduce-scatter.3.cloned.1.call-start = ((), (), s32[]{:S(2)}) async-start(), calls=%async_computation.2 | async-start | bytes 7077888 | tf_op jit(solution)/shard_map/reduce_scatter | solution.py:108
  7.9 145.6 %all-gather.2.cloned.1.call-start = ((), (), s32[]{:S(2)}) async-start(), calls=%async_computation.3 | async-start | bytes 13369344 | tf_op jit(solution)/shard_map/all_gather | solution.py:121
  55.2 272.5 %reduce-scatter.5.cloned.1.call-start = ((), (), s32[]{:S(2)}) async-start(), calls=%async_computation.4 | async-start | bytes 13369344 | tf_op jit(solution)/shard_map/reduce_scatter | solution.py:155
  55.3 16.3 %collective-permute-start = (bf16[512,1024]{1,0:T(8,128)(2,1)}, bf16[512,1024]{1,0:T(8,128)(2,1)S(1)}, u32[]{:S(2)}, u32[]{:S(2)}) collective-permute-start(bf16[512,1024]{1,0:T(8,128)(2,1)} %param.11), channel_id=1, source_target_pairs={{0,2},{1,7},{2,4},{3,1},{4,6},{5,3},{6,0},{7,5},{8,10},{9,15},{10,... | collective-permute-start | bytes 3145736 | tf_op jit(solution)/shard_map/ppermute | solution.py:131
  71.5 45.9 %collective-permute-start.1 = (bf16[512,1024]{1,0:T(8,128)(2,1)S(1)}, bf16[512,1024]{1,0:T(8,128)(2,1)S(1)}, u32[]{:S(2)}, u32[]{:S(2)}) collective-permute-start(bf16[512,1024]{1,0:T(8,128)(2,1)S(1)} %collective-permute-done), channel_id=1, source_target_pairs={{0,2},{1,7},{2,4},{3,1},{4,6},{5,3},{6,0},{7,5},{8,10},{9,15},{10,... | collective-permute-start | bytes 3145736 | tf_op jit(solution)/shard_map/ppermute | solution.py:131
  71.5 63.0 %collective-permute-start.3 = (bf16[512,1024]{1,0:T(8,128)(2,1)}, bf16[512,1024]{1,0:T(8,128)(2,1)}, u32[]{:S(2)}, u32[]{:S(2)}) collective-permute-start(bf16[512,1024]{1,0:T(8,128)(2,1)} %param.11), channel_id=1, source_target_pairs={{0,1},{1,0},{2,3},{3,2},{4,5},{5,4},{6,7},{7,6},{8,9},{9,8},{10,11... | collective-permute-start | bytes 3145736 | tf_op jit(solution)/shard_map/ppermute | solution.py:132
  88.7 15.9 %copy-start.3 = (s32[128,2]{0,1:T(2,128)S(1)}, s32[128,2]{0,1:T(2,128)}, u32[]{:S(2)}) copy-start(s32[128,2]{0,1:T(2,128)} %param.13) | copy-start | bytes 3076
  88.7 16.1 %copy-start.4 = (s32[128,2]{0,1:T(2,128)S(1)}, s32[128,2]{0,1:T(2,128)}, u32[]{:S(2)}) copy-start(s32[128,2]{0,1:T(2,128)} %param.12) | copy-start | bytes 3076
  105.1 13.4 %copy-start.5 = (s32[16]{0:T(128)}, s32[16]{0:T(128)S(1)}, u32[]{:S(2)}) copy-start(s32[16]{0:T(128)S(1)} %reshape.148.owner_ref) | copy-start | bytes 196
  105.9 11.5 %copy-start.1 = (bf16[512,1024]{1,0:T(8,128)(2,1)S(1)}, bf16[512,1024]{1,0:T(8,128)(2,1)}, u32[]{:S(2)}) copy-start(bf16[512,1024]{1,0:T(8,128)(2,1)} %param.11) | copy-start | bytes 3145732
  117.4 16.0 %collective-permute-start.2 = (bf16[512,1024]{1,0:T(8,128)(2,1)S(1)}, bf16[512,1024]{1,0:T(8,128)(2,1)S(1)}, u32[]{:S(2)}, u32[]{:S(2)}) collective-permute-start(bf16[512,1024]{1,0:T(8,128)(2,1)S(1)} %collective-permute-done.1), channel_id=1, source_target_pairs={{0,2},{1,7},{2,4},{3,1},{4,6},{5,3},{6,0},{7,5},{8,10},{9,15},{10,... | collective-permute-start | bytes 3145736 | tf_op jit(solution)/shard_map/ppermute | solution.py:131
  118.9 17.8 %collective-permute-start.4 = (bf16[512,1024]{1,0:T(8,128)(2,1)S(1)}, bf16[512,1024]{1,0:T(8,128)(2,1)S(1)}, u32[]{:S(2)}, u32[]{:S(2)}) collective-permute-start(bf16[512,1024]{1,0:T(8,128)(2,1)S(1)} %collective-permute-done), channel_id=1, source_target_pairs={{0,1},{1,0},{2,3},{3,2},{4,5},{5,4},{6,7},{7,6},{8,9},{9,8},{10,11... | collective-permute-start | bytes 3145736 | tf_op jit(solution)/shard_map/ppermute | solution.py:132
  123.1 14.7 %collective-permute-start.5 = (bf16[512,1024]{1,0:T(8,128)(2,1)S(1)}, bf16[512,1024]{1,0:T(8,128)(2,1)S(1)}, u32[]{:S(2)}, u32[]{:S(2)}) collective-permute-start(bf16[512,1024]{1,0:T(8,128)(2,1)S(1)} %collective-permute-done.1), channel_id=1, source_target_pairs={{0,1},{1,0},{2,3},{3,2},{4,5},{5,4},{6,7},{7,6},{8,9},{9,8},{10,11... | collective-permute-start | bytes 3145736 | tf_op jit(solution)/shard_map/ppermute | solution.py:132
  133.4 5.5 %collective-permute-start.6 = (bf16[512,1024]{1,0:T(8,128)(2,1)S(1)}, bf16[512,1024]{1,0:T(8,128)(2,1)S(1)}, u32[]{:S(2)}, u32[]{:S(2)}) collective-permute-start(bf16[512,1024]{1,0:T(8,128)(2,1)S(1)} %collective-permute-done.2), channel_id=1, source_target_pairs={{0,1},{1,0},{2,3},{3,2},{4,5},{5,4},{6,7},{7,6},{8,9},{9,8},{10,11... | collective-permute-start | bytes 3145736 | tf_op jit(solution)/shard_map/ppermute | solution.py:132
  190.4 0.7 copy-start.7
  190.4 11.3 %copy-start.2 = (s32[8]{0:T(128)S(1)}, s32[8]{0:T(128)}, u32[]{:S(2)}) copy-start(s32[8]{0:T(128)} %constant.215.clone) | copy-start | bytes 100
  190.4 13.3 %copy-start.6 = (bf16[512,768]{1,0:T(8,128)(2,1)S(1)}, bf16[512,768]{1,0:T(8,128)(2,1)}, u32[]{:S(2)}) copy-start(bf16[512,768]{1,0:T(8,128)(2,1)} %get-tuple-element.4) | copy-start | bytes 2359300
  215.9 3.2 copy-start
  219.2 14.4 %collective-permute-start.14 = (bf16[512,512]{1,0:T(8,128)(2,1)S(1)}, bf16[512,512]{1,0:T(8,128)(2,1)S(1)}, u32[]{:S(2)}, u32[]{:S(2)}) collective-permute-start(bf16[512,512]{1,0:T(8,128)(2,1)S(1)} %get-tuple-element.21), channel_id=1, source_target_pairs={{0,1},{2,0},{4,2},{6,4},{7,6},{5,7},{3,5},{1,3},{8,9},{10,8},{12,1... | collective-permute-start | bytes 1572872 | tf_op jit(solution)/shard_map/ppermute | solution.py:179
  219.7 13.9 %collective-permute-start.7 = (bf16[512,512]{1,0:T(8,128)(2,1)S(1)}, bf16[512,512]{1,0:T(8,128)(2,1)S(1)}, u32[]{:S(2)}, u32[]{:S(2)}) collective-permute-start(bf16[512,512]{1,0:T(8,128)(2,1)S(1)} %get-tuple-element.20), channel_id=1, source_target_pairs={{0,2},{2,4},{4,6},{6,7},{7,5},{5,3},{3,1},{1,0},{8,10},{10,12},{12... | collective-permute-start | bytes 1572872 | tf_op jit(solution)/shard_map/ppermute | solution.py:179
  235.1 14.5 %collective-permute-start.15 = (bf16[512,512]{1,0:T(8,128)(2,1)S(1)}, bf16[512,512]{1,0:T(8,128)(2,1)S(1)}, u32[]{:S(2)}, u32[]{:S(2)}) collective-permute-start(bf16[512,512]{1,0:T(8,128)(2,1)S(1)} %get-tuple-element.19), channel_id=1, source_target_pairs={{0,1},{2,0},{4,2},{6,4},{7,6},{5,7},{3,5},{1,3},{8,9},{10,8},{12,1... | collective-permute-start | bytes 1572872 | tf_op jit(solution)/shard_map/ppermute | solution.py:179
  235.2 14.5 %collective-permute-start.8 = (bf16[512,512]{1,0:T(8,128)(2,1)S(1)}, bf16[512,512]{1,0:T(8,128)(2,1)S(1)}, u32[]{:S(2)}, u32[]{:S(2)}) collective-permute-start(bf16[512,512]{1,0:T(8,128)(2,1)S(1)} %get-tuple-element.18), channel_id=1, source_target_pairs={{0,2},{2,4},{4,6},{6,7},{7,5},{5,3},{3,1},{1,0},{8,10},{10,12},{12... | collective-permute-start | bytes 1572872 | tf_op jit(solution)/shard_map/ppermute | solution.py:179
  251.2 14.3 %collective-permute-start.16 = (bf16[512,512]{1,0:T(8,128)(2,1)S(1)}, bf16[512,512]{1,0:T(8,128)(2,1)S(1)}, u32[]{:S(2)}, u32[]{:S(2)}) collective-permute-start(bf16[512,512]{1,0:T(8,128)(2,1)S(1)} %get-tuple-element.17), channel_id=1, source_target_pairs={{0,1},{2,0},{4,2},{6,4},{7,6},{5,7},{3,5},{1,3},{8,9},{10,8},{12,1... | collective-permute-start | bytes 1572872 | tf_op jit(solution)/shard_map/ppermute | solution.py:179
  251.2 14.3 %collective-permute-start.9 = (bf16[512,512]{1,0:T(8,128)(2,1)S(1)}, bf16[512,512]{1,0:T(8,128)(2,1)S(1)}, u32[]{:S(2)}, u32[]{:S(2)}) collective-permute-start(bf16[512,512]{1,0:T(8,128)(2,1)S(1)} %get-tuple-element.16), channel_id=1, source_target_pairs={{0,2},{2,4},{4,6},{6,7},{7,5},{5,3},{3,1},{1,0},{8,10},{10,12},{12... | collective-permute-start | bytes 1572872 | tf_op jit(solution)/shard_map/ppermute | solution.py:179
  267.0 12.5 %collective-permute-start.10 = (bf16[512,512]{1,0:T(8,128)(2,1)S(1)}, bf16[512,512]{1,0:T(8,128)(2,1)S(1)}, u32[]{:S(2)}, u32[]{:S(2)}) collective-permute-start(bf16[512,512]{1,0:T(8,128)(2,1)S(1)} %get-tuple-element.14), channel_id=1, source_target_pairs={{0,2},{2,4},{4,6},{6,7},{7,5},{5,3},{3,1},{1,0},{8,10},{10,12},{12... | collective-permute-start | bytes 1572872 | tf_op jit(solution)/shard_map/ppermute | solution.py:179
  267.3 13.2 %collective-permute-start.17 = (bf16[512,512]{1,0:T(8,128)(2,1)S(1)}, bf16[512,512]{1,0:T(8,128)(2,1)S(1)}, u32[]{:S(2)}, u32[]{:S(2)}) collective-permute-start(bf16[512,512]{1,0:T(8,128)(2,1)S(1)} %get-tuple-element.15), channel_id=1, source_target_pairs={{0,1},{2,0},{4,2},{6,4},{7,6},{5,7},{3,5},{1,3},{8,9},{10,8},{12,1... | collective-permute-start | bytes 1572872 | tf_op jit(solution)/shard_map/ppermute | solution.py:179
  282.0 13.2 %collective-permute-start.11 = (bf16[512,512]{1,0:T(8,128)(2,1)S(1)}, bf16[512,512]{1,0:T(8,128)(2,1)S(1)}, u32[]{:S(2)}, u32[]{:S(2)}) collective-permute-start(bf16[512,512]{1,0:T(8,128)(2,1)S(1)} %get-tuple-element.12), channel_id=1, source_target_pairs={{0,2},{2,4},{4,6},{6,7},{7,5},{5,3},{3,1},{1,0},{8,10},{10,12},{12... | collective-permute-start | bytes 1572872 | tf_op jit(solution)/shard_map/ppermute | solution.py:179
  283.5 12.4 %collective-permute-start.18 = (bf16[512,512]{1,0:T(8,128)(2,1)S(1)}, bf16[512,512]{1,0:T(8,128)(2,1)S(1)}, u32[]{:S(2)}, u32[]{:S(2)}) collective-permute-start(bf16[512,512]{1,0:T(8,128)(2,1)S(1)} %get-tuple-element.13), channel_id=1, source_target_pairs={{0,1},{2,0},{4,2},{6,4},{7,6},{5,7},{3,5},{1,3},{8,9},{10,8},{12,1... | collective-permute-start | bytes 1572872 | tf_op jit(solution)/shard_map/ppermute | solution.py:179
  297.4 12.7 %collective-permute-start.12 = (bf16[512,512]{1,0:T(8,128)(2,1)S(1)}, bf16[512,512]{1,0:T(8,128)(2,1)S(1)}, u32[]{:S(2)}, u32[]{:S(2)}) collective-permute-start(bf16[512,512]{1,0:T(8,128)(2,1)S(1)} %get-tuple-element.10), channel_id=1, source_target_pairs={{0,2},{2,4},{4,6},{6,7},{7,5},{5,3},{3,1},{1,0},{8,10},{10,12},{12... | collective-permute-start | bytes 1572872 | tf_op jit(solution)/shard_map/ppermute | solution.py:179
  299.2 11.6 %collective-permute-start.19 = (bf16[512,512]{1,0:T(8,128)(2,1)S(1)}, bf16[512,512]{1,0:T(8,128)(2,1)S(1)}, u32[]{:S(2)}, u32[]{:S(2)}) collective-permute-start(bf16[512,512]{1,0:T(8,128)(2,1)S(1)} %get-tuple-element.11), channel_id=1, source_target_pairs={{0,1},{2,0},{4,2},{6,4},{7,6},{5,7},{3,5},{1,3},{8,9},{10,8},{12,1... | collective-permute-start | bytes 1572872 | tf_op jit(solution)/shard_map/ppermute | solution.py:179
  312.3 12.2 %collective-permute-start.13 = (bf16[512,512]{1,0:T(8,128)(2,1)S(1)}, bf16[512,512]{1,0:T(8,128)(2,1)S(1)}, u32[]{:S(2)}, u32[]{:S(2)}) collective-permute-start(bf16[512,512]{1,0:T(8,128)(2,1)S(1)} %get-tuple-element.8), channel_id=1, source_target_pairs={{0,2},{2,4},{4,6},{6,7},{7,5},{5,3},{3,1},{1,0},{8,10},{10,12},{12... | collective-permute-start | bytes 1572872 | tf_op jit(solution)/shard_map/ppermute | solution.py:179
  314.4 10.7 %collective-permute-start.20 = (bf16[512,512]{1,0:T(8,128)(2,1)S(1)}, bf16[512,512]{1,0:T(8,128)(2,1)S(1)}, u32[]{:S(2)}, u32[]{:S(2)}) collective-permute-start(bf16[512,512]{1,0:T(8,128)(2,1)S(1)} %get-tuple-element.9), channel_id=1, source_target_pairs={{0,1},{2,0},{4,2},{6,4},{7,6},{5,7},{3,5},{1,3},{8,9},{10,8},{12,1... | collective-permute-start | bytes 1572872 | tf_op jit(solution)/shard_map/ppermute | solution.py:179
Sparse Core Ops, SparseCore 0:
  10.4 44.7 reduce-scatter.2
  57.4 87.8 all-gather.1
  190.6 92.7 reduce-scatter.4

commit v6 on v4

--- a/solution.py
+++ b/solution.py
@@ -13,7 +13,8 @@
 NB_DEV = 2
 
 
-def attention_kernel(heads, owner_ref, pick_ref, q_ref, first_ref, second_ref, g_ref, att_ref, out_ref, acc_ref):
+def attention_kernel(heads, owner_ref, pick_ref, q_ref, first_ref, second_ref, g_ref, *rest):
+    att_ref, out_ref, acc_ref = rest[-3:]
     factor = HD ** (-0.5)
     span = pl.program_id(0)
 
@@ -65,23 +66,31 @@
         out_ref[...] = acc_ref[...].astype(out_ref.dtype)
 
 
-def attention(owners, picks, queries, everyone, grad_attended, owner_count):
-    rows, width = queries.shape
+def attention(owners, picks, queries, everyone, grad_attended, owner_count, chunk, chunks, prior):
+    rows, full_width = queries.shape
     spans = rows // SPAN
+    kv_width = everyone.shape[2]
+    width = kv_width // 2
     heads = width // HD
-    kv_width = everyone.shape[2]
+    in_specs = [
+        pl.BlockSpec((SPAN, width), lambda c, o, n: (c, chunk)),
+        pl.BlockSpec((1, NBR_LEN, kv_width), lambda c, o, n: (n[2 * c], 0, 0)),
+        pl.BlockSpec((1, NBR_LEN, kv_width), lambda c, o, n: (n[2 * c + 1], 0, 0)),
+        pl.BlockSpec((SPAN, width), lambda c, o, n: (c, chunk)),
+    ]
+    operands = [owners, picks, queries, everyone, everyone, grad_attended]
+    aliases = {}
+    if prior is not None:
+        in_specs += [pl.BlockSpec(memory_space=pl.ANY)] * 2
+        operands += list(prior)
+        aliases = {6: 0, 7: 1}
     grid_spec = pltpu.PrefetchScalarGridSpec(
         num_scalar_prefetch=2,
         grid=(spans,),
-        in_specs=[
-            pl.BlockSpec((SPAN, width), lambda c, o, n: (c, 0)),
-            pl.BlockSpec((1, NBR_LEN, kv_width), lambda c, o, n: (n[2 * c], 0, 0)),
-            pl.BlockSpec((1, NBR_LEN, kv_width), lambda c, o, n: (n[2 * c + 1], 0, 0)),
-            pl.BlockSpec((SPAN, width), lambda c, o, n: (c, 0)),
-        ],
+        in_specs=in_specs,
         out_specs=[
-            pl.BlockSpec((SPAN, width), lambda c, o, n: (c, 0)),
-            pl.BlockSpec((owner_count, NBR_LEN, kv_width), lambda c, o, n: (0, 0, 0)),
+            pl.BlockSpec((SPAN, width), lambda c, o, n: (c, chunk)),
+            pl.BlockSpec((owner_count, NBR_LEN, kv_width), lambda c, o, n: (0, 0, chunk)),
         ],
         scratch_shapes=[pltpu.VMEM((owner_count, NBR_LEN, kv_width), jnp.float32)],
     )
@@ -89,13 +98,14 @@
         functools.partial(attention_kernel, heads),
         grid_spec=grid_spec,
         out_shape=[
-            jax.ShapeDtypeStruct((rows, width), jnp.bfloat16),
-            jax.ShapeDtypeStruct((owner_count, NBR_LEN, kv_width), jnp.bfloat16),
+            jax.ShapeDtypeStruct((rows, full_width), jnp.bfloat16),
+            jax.ShapeDtypeStruct((owner_count, NBR_LEN, kv_width * chunks), jnp.bfloat16),
         ],
+        input_output_aliases=aliases,
         compiler_params=pltpu.CompilerParams(
-            dimension_semantics=("arbitrary",), vmem_limit_bytes=56 * 1024 * 1024
+            dimension_semantics=("arbitrary",), vmem_limit_bytes=48 * 1024 * 1024
         ),
-    )(owners, picks, queries, everyone, everyone, grad_attended)
+    )(*operands)
 
 
 def slot_sum_kernel(readers, select_ref, returned_ref, out_ref):
@@ -147,7 +157,6 @@
     owner_select = ((serving_slot[:, None] == slot_ids[None, :]) & serving[:, None]).astype(
         jnp.float32
     )
-    everyone = lax.all_gather(share_blocks, "dp", axis=0, tiled=True)
     picks = my_owner * NB_DEV + my_slot
     tensor_count = lax.axis_size("tensor")
     column = lax.axis_index("tensor")
@@ -166,16 +175,30 @@
             ((column ^ 1) + 2 * direction * steps) % tensor_count,
         ]
     )
-    w_slots = jnp.take(
-        w_out.reshape(head_width, tensor_count, d_out.shape[1]), slot_block, axis=1, mode="clip"
-    )
+    block_slot = jnp.argmax(
+        slot_block[None, :] == jnp.arange(tensor_count, dtype=jnp.int32)[:, None], axis=1
+    )
+    ordered = jnp.take(jnp.stack(mine + theirs), block_slot, axis=0, mode="clip")
     grad_attended = jnp.einsum(
         "tqc,htc->qh",
-        jnp.stack(mine + theirs),
-        w_slots,
+        ordered,
+        w_out.reshape(head_width, tensor_count, d_out.shape[1]),
         preferred_element_type=jnp.float32,
     ).astype(jnp.bfloat16)
-    attended, per_owner = attention(my_owner, picks, queries, everyone, grad_attended, dp_count)
+    chunks = 2
+    chunk_width = share_width // chunks
+    outputs = None
+    for chunk in range(chunks):
+        everyone = lax.all_gather(
+            share_blocks[:, :, chunk * chunk_width:(chunk + 1) * chunk_width],
+            "dp",
+            axis=0,
+            tiled=True,
+        )
+        outputs = attention(
+            my_owner, picks, queries, everyone, grad_attended, dp_count, chunk, chunks, outputs
+        )
+    attended, per_owner = outputs
     partial_out = jnp.dot(attended, w_out, preferred_element_type=jnp.float32)
     mixed = lax.psum_scatter(
         partial_out.astype(jnp.bfloat16), "tensor", scatter_dimension=1, tiled=True

time: 324 us -> 338 us (1.043)
  waiting for transfers between devices: 180 us -> 228 us
  local copies, waits for them, and re-layouts: 54.9 us -> 21 us
    all_gather x1 -> x2, waiting for transfers between devices: 0.01 us -> 31.7 us  [local(): lax.all_gather(share_blocks[:, :, chunk * chunk_width:(chunk + 1) * chunk...]
    ppermute x3, waiting for transfers between devices: 25.4 us -> 42.6 us  [local(): mine.append(lax.ppermute(mine[-1], 'tensor', ring))]
    unnamed x18 -> x17, local copies, waits for them, and re-layouts: 25.7 us -> 8.92 us
    reshape x1 -> x0, local copies, waits for them, and re-layouts: 15.9 us -> none  [local(): w_out.reshape(head_width, tensor_count, d_out.shape[1])]
    pallas_call x1 -> x2, Pallas kernels: 28.5 us -> 31.1 us  [attention(): pl.pallas_call(functools.partial(attention_kernel, heads), grid_spec=grid...]
  transfers between devices with their start and end apart: 11 -> 12, of which waited for: 4 -> 6; matrix products, arithmetic and copies ran while one was open for 22% -> 10% of each run, Pallas kernels for 2% -> 7%
where the time goes in v6:
time: 338 us; the launch traced here: 337 us
  waiting for transfers between devices  228 us (67%)
  Pallas kernels  37.5 us (11%)
  matrix products  26.6 us (8%)
  local copies, waits for them, and re-layouts  21 us (6%)
  between operations  13.9 us (4%)
  starting transfers between devices  8.51 us (3%)
    all_to_all x1, waiting for transfers between devices, local(): lax.all_to_all(per_owner, 'dp', split_axis=0, concat_axis=0, tiled=True)  105 us
    reduce_scatter x1, waiting for transfers between devices, local(): lax.psum_scatter(kv_part[0], 'tensor', scatter_dimension=1, tiled=True)  47.2 us
    ppermute x3, waiting for transfers between devices, local(): mine.append(lax.ppermute(mine[-1], 'tensor', ring))  42.6 us
    all_gather x2, waiting for transfers between devices, local(): lax.all_gather(share_blocks[:, :, chunk * chunk_width:(chunk + 1) * chunk...  31.7 us
    pallas_call x2, Pallas kernels, attention(): pl.pallas_call(functools.partial(attention_kernel, heads), grid_spec=grid...  31.1 us
    dot_general x1, matrix products, local(): partial_out = jnp.dot(attended, w_out, preferred_element_type=jnp.float32)  13.8 us
    dot_general x1, matrix products, local(): jnp.einsum('tqc,htc->qh', ordered, w_out.reshape(head_width, tensor_count...  12.8 us
    unnamed x17, local copies, waits for them, and re-layouts  8.92 us
  transfers between devices with their start and end apart: 12, of which 6 were waited for; matrix products, arithmetic and copies ran while one was open for 10% of the time, Pallas kernels for 7%

profile of v6, /device:TPU:28, one launch (start us, length us, event | category | flops | bytes accessed | tf_op | source)
XLA Modules:
  0.0 337.2 jit_solution(11736169094592636685)
XLA Ops:
  7.2 0.0 reduce-scatter.3.cloned.1.call-start
  7.2 0.7 reduce-scatter.3.cloned.1.call-update
  7.9 0.0 all-gather.5.cloned.1.call-start
  8.0 47.2 %reduce-scatter.3.cloned.1.call-done = bf16[256,1536]{1,0:T(8,128)(2,1)} async-done(((bf16[256,12288]{1,0:T(8,128)(2,1)}), bf16[256,1536]{1,0:T(8,128)(2,1)}) %reduce-scatter.3.cloned.1.call-update) | async-done | bytes 786448 | tf_op jit(solution)/shard_map/reduce_scatter | solution.py:141
  55.2 2.0 fusion.10
  57.3 0.0 all-gather.3.cloned.1.call-start
  57.3 0.7 all-gather.3.cloned.1.call-update
  58.0 0.0 reduce-scatter.5.cloned.1.call-start
  58.1 0.1 collective-permute-start
  58.2 16.0 %collective-permute-done = bf16[512,1024]{1,0:T(8,128)(2,1)S(1)} collective-permute-done((bf16[512,1024]{1,0:T(8,128)(2,1)S(1)}, bf16[512,1024]{1,0:T(8,128)(2,1)S(1)}, u32[]{:S(2)}, u32[]{:S(2)}) %collective-permute-start) | collective-permute-done | bytes 1048608 | tf_op jit(solution)/shard_map/ppermute | solution.py:169
  74.2 0.5 collective-permute-start.3
  74.7 0.1 constant_dynamic-slice_fusion
  74.8 0.1 copy.28
  74.8 0.1 reshape.26.owner_ref
  74.9 0.1 copy.29
  75.0 0.1 reshape.27
  75.1 0.1 pad_add_fusion
  75.2 0.7 iota_reduce_fusion
  75.9 14.3 %collective-permute-done.1 = bf16[512,1024]{1,0:T(8,128)(2,1)S(1)} collective-permute-done((bf16[512,1024]{1,0:T(8,128)(2,1)S(1)}, bf16[512,1024]{1,0:T(8,128)(2,1)S(1)}, u32[]{:S(2)}, u32[]{:S(2)}) %collective-permute-start.1) | collective-permute-done | bytes 1048608 | tf_op jit(solution)/shard_map/ppermute | solution.py:169
  90.2 1.0 bitcast_dynamic-update-slice_fusion.7
  91.2 1.1 bitcast_dynamic-update-slice_fusion.6
  92.3 0.5 collective-permute-start.5
  92.8 1.1 bitcast_dynamic-update-slice_fusion.5
  93.9 12.3 %collective-permute-done.2 = bf16[512,1024]{1,0:T(8,128)(2,1)S(1)} collective-permute-done((bf16[512,1024]{1,0:T(8,128)(2,1)S(1)}, bf16[512,1024]{1,0:T(8,128)(2,1)S(1)}, u32[]{:S(2)}, u32[]{:S(2)}) %collective-permute-start.2) | collective-permute-done | bytes 1048608 | tf_op jit(solution)/shard_map/ppermute | solution.py:169
  106.2 1.0 bitcast_dynamic-update-slice_fusion.4
  107.2 2.3 bitcast_dynamic-update-slice_fusion.3
  109.5 1.1 bitcast_dynamic-update-slice_fusion.2
  110.6 1.1 bitcast_dynamic-update-slice_fusion.1
  111.7 1.1 bitcast_dynamic-update-slice_fusion
  112.7 8.0 %gather_fusion = bf16[8,512,1024]{2,1,0:T(8,128)(2,1)} fusion(bf16[8,512,1024]{2,1,0:T(8,128)(2,1)} %bitcast_dynamic-update-slice_fusion, s32[1024]{0:T(1024)S(1)} %pad_clamp_fusion), kind=kCustom, calls=%fused_computation | custom fusion | bytes 16777248 | tf_op jit(solution)/shard_map/jit(_take)/gather | solution.py:181
  120.8 12.8 %bitcast_convert_fusion.g_ref = bf16[512,768]{1,0:T(8,128)(2,1)S(1)} fusion(bf16[8,512,1024]{2,1,0:T(8,128)(2,1)} %gather_fusion, bf16[96,8,8,1024]{3,2,1,0:T(8,128)(2,1)} %bitcast.33), kind=kOutput, calls=%fused_computation.5 | convolution fusion | flops 6442844160 | bytes 21757952 | tf_op jit(solution)/shard_map/tqc,htc->qh/dot_general | solution.py:182
  133.6 0.0 all-gather.5.cloned.1.call-done.first_ref.second_ref
  133.7 15.6 %shard_map.77 = (bf16[512,768]{1,0:T(8,128)(2,1)S(1)}, bf16[16,128,1536]{2,1,0:T(8,128)(2,1)}) custom-call(s32[16]{0:T(128)S(1)} %reshape.26.owner_ref, s32[16]{0:T(128)S(1)} %multiply_add_fusion.pick_ref, bf16[512,768]{1,0:T(8,128)(2,1)S(1)} %copy-done, bf16[32,128,768]{2,1,0:T(8,128)(2,1)} %all-gather.5.cloned.1.call-done.first_ref.second_ref, ...), custom_call_target="tpu_custom_call" | custom-call | tf_op jit(solution)/shard_map/pallas_call | solution.py:97
  149.2 31.7 %all-gather.3.cloned.1.call-done.first_ref.second_ref = bf16[32,128,768]{2,1,0:T(8,128)(2,1)} async-done(((bf16[2,128,768]{2,1,0:T(8,128)(2,1)}), bf16[32,128,768]{2,1,0:T(8,128)(2,1)}) %all-gather.3.cloned.1.call-update) | async-done | bytes 6291472 | tf_op jit(solution)/shard_map/all_gather | solution.py:192
  180.9 15.5 %shard_map.78 = (bf16[512,768]{1,0:T(8,128)(2,1)S(1)}, bf16[16,128,1536]{2,1,0:T(8,128)(2,1)}) custom-call(s32[16]{0:T(128)S(1)} %reshape.26.owner_ref, s32[16]{0:T(128)S(1)} %multiply_add_fusion.pick_ref, bf16[512,768]{1,0:T(8,128)(2,1)S(1)} %copy-done, ...), custom_call_target="tpu_custom_call", output_to_operand_aliasing={{0}: (6, {}), {1}: (7, {})} | custom-call | tf_op jit(solution)/shard_map/pallas_call | solution.py:97
  196.4 13.8 %convolution_convert_fusion = bf16[512,8192]{1,0:T(8,128)(2,1)} fusion(bf16[512,768]{1,0:T(8,128)(2,1)S(1)} %get-tuple-element.10, bf16[768,8192]{1,0:T(8,128)(2,1)} %param.8), kind=kOutput, calls=%fused_computation.4 | convolution fusion | flops 6446645248 | bytes 21757952 | tf_op jit(solution)/shard_map/dot_general | solution.py:202
  210.2 7.2 %all-to-all-start = ((bf16[16,128,1536]{2,1,0:T(8,128)(2,1)}), bf16[16,128,1536]{2,1,0:T(8,128)(2,1)}, u32[]{:S(2)}, u32[]{:S(2)}) async-start(bf16[16,128,1536]{2,1,0:T(8,128)(2,1)} %get-tuple-element.11), calls=%async_computation.2 | async-start | bytes 12582912 | tf_op jit(solution)/shard_map/all_to_all | solution.py:206
  217.5 0.1 copy.31
  217.6 0.1 copy.32
  217.7 0.1 eq.54
  217.8 0.1 broadcast_in_dim.26
  217.9 0.2 select_reduce_fusion
  218.0 0.2 dynamic-slice_reduce_fusion
  218.2 0.1 fusion.5
  218.3 0.2 dynamic-slice_reduce_fusion.1
  218.5 0.7 fusion.7.select_ref
  219.2 105.0 %all-to-all-done.returned_ref = bf16[16,128,1536]{2,1,0:T(8,128)(2,1)} async-done(((bf16[16,128,1536]{2,1,0:T(8,128)(2,1)}), bf16[16,128,1536]{2,1,0:T(8,128)(2,1)}, u32[]{:S(2)}, u32[]{:S(2)}) %all-to-all-start) | async-done | bytes 6291488 | tf_op jit(solution)/shard_map/all_to_all | solution.py:206
  324.2 6.5 %shard_map.79 = bf16[2,128,1536]{2,1,0:T(8,128)(2,1)} custom-call(f32[16,2]{1,0:T(8,128)} %fusion.7.select_ref, bf16[16,128,1536]{2,1,0:T(8,128)(2,1)} %all-to-all-done.returned_ref), custom_call_target="tpu_custom_call" | custom-call | tf_op jit(solution)/shard_map/pallas_call | solution.py:122
  (22 shorter events, 0.1 us)
Async XLA Ops:
  7.2 50.9 %copy-start.1 = (bf16[512,1024]{1,0:T(8,128)(2,1)S(1)}, bf16[512,1024]{1,0:T(8,128)(2,1)}, u32[]{:S(2)}) copy-start(bf16[512,1024]{1,0:T(8,128)(2,1)} %param.9) | copy-start | bytes 3145732
  7.2 67.5 %copy-start.2 = (s32[128,2]{0,1:T(2,128)S(1)}, s32[128,2]{0,1:T(2,128)}, u32[]{:S(2)}) copy-start(s32[128,2]{0,1:T(2,128)} %param.10) | copy-start | bytes 3076
  7.2 67.5 %copy-start.3 = (s32[128,2]{0,1:T(2,128)S(1)}, s32[128,2]{0,1:T(2,128)}, u32[]{:S(2)}) copy-start(s32[128,2]{0,1:T(2,128)} %param.11) | copy-start | bytes 3076
  7.2 48.0 %reduce-scatter.3.cloned.1.call-start = ((), (), s32[]{:S(2)}) async-start(), calls=%async_computation.3 | async-start | bytes 7077888 | tf_op jit(solution)/shard_map/reduce_scatter | solution.py:141
  7.9 125.7 %all-gather.5.cloned.1.call-start = ((), (), s32[]{:S(2)}) async-start(), calls=%async_computation.5 | async-start | bytes 6684672 | tf_op jit(solution)/shard_map/all_gather | solution.py:192
  57.3 123.7 %all-gather.3.cloned.1.call-start = ((), (), s32[]{:S(2)}) async-start(), calls=%async_computation.4 | async-start | bytes 6684672 | tf_op jit(solution)/shard_map/all_gather | solution.py:192
  58.0 272.6 %reduce-scatter.5.cloned.1.call-start = ((), (), s32[]{:S(2)}) async-start(), calls=%async_computation.6 | async-start | bytes 9437184 | tf_op jit(solution)/shard_map/reduce_scatter | solution.py:203
  58.1 16.1 %collective-permute-start = (bf16[512,1024]{1,0:T(8,128)(2,1)S(1)}, bf16[512,1024]{1,0:T(8,128)(2,1)S(1)}, u32[]{:S(2)}, u32[]{:S(2)}) collective-permute-start(bf16[512,1024]{1,0:T(8,128)(2,1)S(1)} %copy-done.1), channel_id=1, source_target_pairs={{0,2},{1,7},{2,4},{3,1},{4,6},{5,3},{6,0},{7,5},{8,10},{9,15},{10,... | collective-permute-start | bytes 3145736 | tf_op jit(solution)/shard_map/ppermute | solution.py:169
  74.2 16.0 %collective-permute-start.1 = (bf16[512,1024]{1,0:T(8,128)(2,1)S(1)}, bf16[512,1024]{1,0:T(8,128)(2,1)S(1)}, u32[]{:S(2)}, u32[]{:S(2)}) collective-permute-start(bf16[512,1024]{1,0:T(8,128)(2,1)S(1)} %collective-permute-done), channel_id=1, source_target_pairs={{0,2},{1,7},{2,4},{3,1},{4,6},{5,3},{6,0},{7,5},{8,10},{9,15},{10,... | collective-permute-start | bytes 3145736 | tf_op jit(solution)/shard_map/ppermute | solution.py:169
  74.2 33.1 %collective-permute-start.3 = (bf16[512,1024]{1,0:T(8,128)(2,1)S(1)}, bf16[512,1024]{1,0:T(8,128)(2,1)}, u32[]{:S(2)}, u32[]{:S(2)}) collective-permute-start(bf16[512,1024]{1,0:T(8,128)(2,1)S(1)} %copy-done.1), channel_id=1, source_target_pairs={{0,1},{1,0},{2,3},{3,2},{4,5},{5,4},{6,7},{7,6},{8,9},{9,8},{10,11... | collective-permute-start | bytes 3145736 | tf_op jit(solution)/shard_map/ppermute | solution.py:170
  90.2 16.0 %collective-permute-start.2 = (bf16[512,1024]{1,0:T(8,128)(2,1)S(1)}, bf16[512,1024]{1,0:T(8,128)(2,1)S(1)}, u32[]{:S(2)}, u32[]{:S(2)}) collective-permute-start(bf16[512,1024]{1,0:T(8,128)(2,1)S(1)} %collective-permute-done.1), channel_id=1, source_target_pairs={{0,2},{1,7},{2,4},{3,1},{4,6},{5,3},{6,0},{7,5},{8,10},{9,15},{10,... | collective-permute-start | bytes 3145736 | tf_op jit(solution)/shard_map/ppermute | solution.py:169
  91.2 18.3 %collective-permute-start.4 = (bf16[512,1024]{1,0:T(8,128)(2,1)S(1)}, bf16[512,1024]{1,0:T(8,128)(2,1)S(1)}, u32[]{:S(2)}, u32[]{:S(2)}) collective-permute-start(bf16[512,1024]{1,0:T(8,128)(2,1)S(1)} %collective-permute-done), channel_id=1, source_target_pairs={{0,1},{1,0},{2,3},{3,2},{4,5},{5,4},{6,7},{7,6},{8,9},{9,8},{10,11... | collective-permute-start | bytes 3145736 | tf_op jit(solution)/shard_map/ppermute | solution.py:170
  92.3 18.3 %collective-permute-start.5 = (bf16[512,1024]{1,0:T(8,128)(2,1)S(1)}, bf16[512,1024]{1,0:T(8,128)(2,1)S(1)}, u32[]{:S(2)}, u32[]{:S(2)}) collective-permute-start(bf16[512,1024]{1,0:T(8,128)(2,1)S(1)} %collective-permute-done.1), channel_id=1, source_target_pairs={{0,1},{1,0},{2,3},{3,2},{4,5},{5,4},{6,7},{7,6},{8,9},{9,8},{10,11... | collective-permute-start | bytes 3145736 | tf_op jit(solution)/shard_map/ppermute | solution.py:170
  106.2 5.5 %collective-permute-start.6 = (bf16[512,1024]{1,0:T(8,128)(2,1)S(1)}, bf16[512,1024]{1,0:T(8,128)(2,1)S(1)}, u32[]{:S(2)}, u32[]{:S(2)}) collective-permute-start(bf16[512,1024]{1,0:T(8,128)(2,1)S(1)} %collective-permute-done.2), channel_id=1, source_target_pairs={{0,1},{1,0},{2,3},{3,2},{4,5},{5,4},{6,7},{7,6},{8,9},{9,8},{10,11... | collective-permute-start | bytes 3145736 | tf_op jit(solution)/shard_map/ppermute | solution.py:170
  120.8 12.9 %copy-start = (bf16[512,768]{1,0:T(8,128)(2,1)S(1)}, bf16[512,768]{1,0:T(8,128)(2,1)}, u32[]{:S(2)}) copy-start(bf16[512,768]{1,0:T(8,128)(2,1)} %q_ref.3) | copy-start | bytes 2359300
  210.2 113.9 %all-to-all-start = ((bf16[16,128,1536]{2,1,0:T(8,128)(2,1)}), bf16[16,128,1536]{2,1,0:T(8,128)(2,1)}, u32[]{:S(2)}, u32[]{:S(2)}) async-start(bf16[16,128,1536]{2,1,0:T(8,128)(2,1)} %get-tuple-element.11), calls=%async_computation.2 | async-start | bytes 12582912 | tf_op jit(solution)/shard_map/all_to_all | solution.py:206
Sparse Core Ops, SparseCore 0:
  10.4 44.7 reduce-scatter.2
  58.0 59.2 all-gather.4
  120.0 60.9 all-gather.2
  210.4 53.9 reduce-scatter.4

commit v7 on v4

--- a/solution.py
+++ b/solution.py
@@ -21,44 +21,44 @@
     def _():
         acc_ref[...] = jnp.zeros_like(acc_ref)
 
-    first = owner_ref[2 * span]
-    second = owner_ref[2 * span + 1]
+    owners = (owner_ref[2 * span], owner_ref[2 * span + 1])
+    sources = (first_ref, second_ref)
+    nt = (((1,), (1,)), ((), ()))
+    tn = (((0,), (0,)), ((), ()))
     for h in range(heads):
         cols = slice(h * HD, (h + 1) * HD)
         kcols = slice(2 * h * HD, 2 * h * HD + HD)
         vcols = slice(2 * h * HD + HD, 2 * (h + 1) * HD)
         q = q_ref[:, cols]
         g = g_ref[:, cols]
-        k = jnp.concatenate([first_ref[0, :, kcols], second_ref[0, :, kcols]], axis=0)
-        v = jnp.concatenate([first_ref[0, :, vcols], second_ref[0, :, vcols]], axis=0)
-        scores = (
-            lax.dot_general(q, k, (((1,), (1,)), ((), ())), preferred_element_type=jnp.float32)
-            * factor
+        keys = [src[0, :, kcols] for src in sources]
+        values = [src[0, :, vcols] for src in sources]
+        scores = [
+            lax.dot_general(q, k, nt, preferred_element_type=jnp.float32) * factor for k in keys
+        ]
+        top = jnp.maximum(
+            jnp.max(scores[0], axis=-1, keepdims=True), jnp.max(scores[1], axis=-1, keepdims=True)
         )
-        top = jnp.max(scores, axis=-1, keepdims=True)
-        expo = jnp.exp(scores - top)
-        probs = expo / jnp.sum(expo, axis=-1, keepdims=True)
-        probs_low = probs.astype(jnp.bfloat16)
-        attended = jnp.dot(probs_low, v, preferred_element_type=jnp.float32)
+        expo = [jnp.exp(s - top) for s in scores]
+        total = jnp.sum(expo[0], axis=-1, keepdims=True) + jnp.sum(expo[1], axis=-1, keepdims=True)
+        probs = [e / total for e in expo]
+        probs_low = [p.astype(jnp.bfloat16) for p in probs]
+        attended = jnp.dot(probs_low[0], values[0], preferred_element_type=jnp.float32) + jnp.dot(
+            probs_low[1], values[1], preferred_element_type=jnp.float32
+        )
         att_ref[:, cols] = attended.astype(att_ref.dtype)
-        grad_values = lax.dot_general(
-            probs_low, g, (((0,), (0,)), ((), ())), preferred_element_type=jnp.float32
+        grad_probs = [lax.dot_general(g, v, nt, preferred_element_type=jnp.float32) for v in values]
+        inner = jnp.sum(probs[0] * grad_probs[0], axis=-1, keepdims=True) + jnp.sum(
+            probs[1] * grad_probs[1], axis=-1, keepdims=True
         )
-        grad_probs = lax.dot_general(
-            g, v, (((1,), (1,)), ((), ())), preferred_element_type=jnp.float32
-        )
-        grad_scores = probs * (grad_probs - jnp.sum(probs * grad_probs, axis=-1, keepdims=True))
-        grad_scores = grad_scores.astype(jnp.bfloat16)
-        grad_keys = (
-            lax.dot_general(
-                grad_scores, q, (((0,), (0,)), ((), ())), preferred_element_type=jnp.float32
+        for j in range(2):
+            grad_values = lax.dot_general(probs_low[j], g, tn, preferred_element_type=jnp.float32)
+            grad_scores = (probs[j] * (grad_probs[j] - inner)).astype(jnp.bfloat16)
+            grad_keys = (
+                lax.dot_general(grad_scores, q, tn, preferred_element_type=jnp.float32) * factor
             )
-            * factor
-        )
-        acc_ref[first, :, kcols] += grad_keys[:NBR_LEN]
-        acc_ref[second, :, kcols] += grad_keys[NBR_LEN:]
-        acc_ref[first, :, vcols] += grad_values[:NBR_LEN]
-        acc_ref[second, :, vcols] += grad_values[NBR_LEN:]
+            acc_ref[owners[j], :, kcols] += grad_keys
+            acc_ref[owners[j], :, vcols] += grad_values
 
     @pl.when(span == pl.num_programs(0) - 1)
     def _():
@@ -108,7 +108,7 @@
 
 def slot_sum(select, returned):
     readers, length, width = returned.shape
-    tile = 256
+    tile = 768
     return pl.pallas_call(
         functools.partial(slot_sum_kernel, readers),
         grid=(width // tile,),
@@ -166,13 +166,14 @@
             ((column ^ 1) + 2 * direction * steps) % tensor_count,
         ]
     )
-    w_slots = jnp.take(
-        w_out.reshape(head_width, tensor_count, d_out.shape[1]), slot_block, axis=1, mode="clip"
-    )
+    block_slot = jnp.argmax(
+        slot_block[None, :] == jnp.arange(tensor_count, dtype=jnp.int32)[:, None], axis=1
+    )
+    ordered = jnp.take(jnp.stack(mine + theirs), block_slot, axis=0, mode="clip")
     grad_attended = jnp.einsum(
         "tqc,htc->qh",
-        jnp.stack(mine + theirs),
-        w_slots,
+        ordered,
+        w_out.reshape(head_width, tensor_count, d_out.shape[1]),
         preferred_element_type=jnp.float32,
     ).astype(jnp.bfloat16)
     attended, per_owner = attention(my_owner, picks, queries, everyone, grad_attended, dp_count)

time: 324 us -> 324 us (level)
  local copies, waits for them, and re-layouts: 54.9 us -> 19.9 us
  waiting for transfers between devices: 180 us -> 208 us
  Pallas kernels: 35 us -> 44.2 us
    unnamed x18 -> x15, local copies, waits for them, and re-layouts: 25.7 us -> 8.96 us
    reshape x1 -> x0, local copies, waits for them, and re-layouts: 15.9 us -> none  [local(): w_out.reshape(head_width, tensor_count, d_out.shape[1])]
    ppermute x3, waiting for transfers between devices: 25.4 us -> 40.5 us  [local(): mine.append(lax.ppermute(mine[-1], 'tensor', ring))]
    all_gather x1, waiting for transfers between devices: 0.01 us -> 14.3 us  [local(): everyone = lax.all_gather(share_blocks, 'dp', axis=0, tiled=True)]
    pallas_call x1, Pallas kernels: 28.5 us -> 39.1 us  [attention(): pl.pallas_call(functools.partial(attention_kernel, heads), grid_spec=grid...]
  transfers between devices with their start and end apart: 11 -> 11, of which waited for: 4 -> 6; matrix products, arithmetic and copies ran while one was open for 22% -> 11% of each run, Pallas kernels for 2% -> 2%
where the time goes in v7:
time: 324 us
  waiting for transfers between devices  208 us (64%)
  Pallas kernels  44.2 us (14%)
  matrix products  27.4 us (8%)
  local copies, waits for them, and re-layouts  19.9 us (6%)
  between operations  13.8 us (4%)
  starting transfers between devices  8.31 us (3%)
    all_to_all x1, waiting for transfers between devices, local(): lax.all_to_all(per_owner, 'dp', split_axis=0, concat_axis=0, tiled=True)  105 us
    reduce_scatter x1, waiting for transfers between devices, local(): lax.psum_scatter(kv_part[0], 'tensor', scatter_dimension=1, tiled=True)  47.2 us
    ppermute x3, waiting for transfers between devices, local(): mine.append(lax.ppermute(mine[-1], 'tensor', ring))  40.5 us
    pallas_call x1, Pallas kernels, attention(): pl.pallas_call(functools.partial(attention_kernel, heads), grid_spec=grid...  39.1 us
    all_gather x1, waiting for transfers between devices, local(): everyone = lax.all_gather(share_blocks, 'dp', axis=0, tiled=True)  14.3 us
    dot_general x1, matrix products, local(): jnp.einsum('tqc,htc->qh', ordered, w_out.reshape(head_width, tensor_count...  13.8 us
    dot_general x1, matrix products, local(): partial_out = jnp.dot(attended, w_out, preferred_element_type=jnp.float32)  13.6 us
    unnamed x15, local copies, waits for them, and re-layouts  8.96 us
  transfers between devices with their start and end apart: 11, of which 6 were waited for; matrix products, arithmetic and copies ran while one was open for 11% of the time, Pallas kernels for 2%

profile of v7, /device:TPU:28, one launch (start us, length us, event | category | flops | bytes accessed | tf_op | source)
XLA Modules:
  0.0 323.5 jit_solution(15363632221783693778)
XLA Ops:
  7.2 0.0 reduce-scatter.3.cloned.1.call-start
  7.2 0.7 reduce-scatter.3.cloned.1.call-update
  7.9 0.0 all-gather.2.cloned.1.call-start
  7.9 47.2 %reduce-scatter.3.cloned.1.call-done = bf16[256,1536]{1,0:T(8,128)(2,1)} async-done(((bf16[256,12288]{1,0:T(8,128)(2,1)}), bf16[256,1536]{1,0:T(8,128)(2,1)}) %reduce-scatter.3.cloned.1.call-update) | async-done | bytes 786448 | tf_op jit(solution)/shard_map/reduce_scatter | solution.py:131
  55.2 0.0 all-gather.2.cloned.1.call-update
  55.2 0.0 reduce-scatter.5.cloned.1.call-start
  55.3 0.1 collective-permute-start
  55.3 16.2 %collective-permute-done = bf16[512,1024]{1,0:T(8,128)(2,1)S(1)} collective-permute-done((bf16[512,1024]{1,0:T(8,128)(2,1)}, bf16[512,1024]{1,0:T(8,128)(2,1)S(1)}, u32[]{:S(2)}, u32[]{:S(2)}) %collective-permute-start) | collective-permute-done | bytes 1048608 | tf_op jit(solution)/shard_map/ppermute | solution.py:160
  71.5 0.4 collective-permute-start.3
  71.9 0.8 constant_dynamic-slice_fusion
  72.7 0.1 copy.26
  72.8 0.1 reshape.26.owner_ref
  72.9 0.1 copy.27
  72.9 0.1 reshape.27
  73.0 0.1 pad_add_fusion
  73.1 0.6 iota_reduce_fusion
  73.8 13.8 %collective-permute-done.1 = bf16[512,1024]{1,0:T(8,128)(2,1)S(1)} collective-permute-done((bf16[512,1024]{1,0:T(8,128)(2,1)S(1)}, bf16[512,1024]{1,0:T(8,128)(2,1)S(1)}, u32[]{:S(2)}, u32[]{:S(2)}) %collective-permute-start.1) | collective-permute-done | bytes 1048608 | tf_op jit(solution)/shard_map/ppermute | solution.py:160
  87.6 2.3 bitcast_dynamic-update-slice_fusion.7
  89.9 0.6 multiply_add_fusion.pick_ref
  90.5 1.0 bitcast_dynamic-update-slice_fusion.6
  91.5 0.5 collective-permute-start.5
  92.0 1.0 bitcast_dynamic-update-slice_fusion.5
  93.1 10.5 %collective-permute-done.2 = bf16[512,1024]{1,0:T(8,128)(2,1)S(1)} collective-permute-done((bf16[512,1024]{1,0:T(8,128)(2,1)S(1)}, bf16[512,1024]{1,0:T(8,128)(2,1)S(1)}, u32[]{:S(2)}, u32[]{:S(2)}) %collective-permute-start.2) | collective-permute-done | bytes 1048608 | tf_op jit(solution)/shard_map/ppermute | solution.py:160
  103.6 1.1 bitcast_dynamic-update-slice_fusion.4
  104.6 1.1 bitcast_dynamic-update-slice_fusion.3
  105.7 1.1 bitcast_dynamic-update-slice_fusion.2
  106.8 1.1 bitcast_dynamic-update-slice_fusion.1
  107.9 1.1 bitcast_dynamic-update-slice_fusion
  108.9 8.2 %gather_fusion = bf16[8,512,1024]{2,1,0:T(8,128)(2,1)} fusion(bf16[8,512,1024]{2,1,0:T(8,128)(2,1)} %bitcast_dynamic-update-slice_fusion, s32[1024]{0:T(1024)S(1)} %pad_clamp_fusion), kind=kCustom, calls=%fused_computation | custom fusion | bytes 16777248 | tf_op jit(solution)/shard_map/jit(_take)/gather | solution.py:172
  117.2 13.8 %bitcast_convert_fusion.g_ref = bf16[512,768]{1,0:T(8,128)(2,1)} fusion(bf16[8,512,1024]{2,1,0:T(8,128)(2,1)} %gather_fusion, bf16[96,8,8,1024]{3,2,1,0:T(8,128)(2,1)} %bitcast.33), kind=kOutput, calls=%fused_computation.5 | convolution fusion | flops 6442844160 | bytes 21757952 | tf_op jit(solution)/shard_map/tqc,htc->qh/dot_general | solution.py:173
  131.0 14.3 %all-gather.2.cloned.1.call-done.first_ref.second_ref = bf16[32,128,1536]{2,1,0:T(8,128)(2,1)} async-done(((bf16[2,128,1536]{2,1,0:T(8,128)(2,1)}), bf16[32,128,1536]{2,1,0:T(8,128)(2,1)}) %all-gather.2.cloned.1.call-update) | async-done | bytes 12582928 | tf_op jit(solution)/shard_map/all_gather | solution.py:150
  145.3 39.1 %shard_map.77 = (bf16[512,768]{1,0:T(8,128)(2,1)}, bf16[16,128,1536]{2,1,0:T(8,128)(2,1)}) custom-call(s32[16]{0:T(128)} %copy-done.2, s32[16]{0:T(128)} %multiply_add_fusion.pick_ref, bf16[512,768]{1,0:T(8,128)(2,1)} %q_ref.1, bf16[32,128,1536]{2,1,0:T(8,128)(2,1)} %all-gather.2.cloned.1.call-done.first_ref.second_ref, ...), custom_call_target="tpu_custom_call" | custom-call | tf_op jit(solution)/shard_map/pallas_call | solution.py:88
  184.4 13.6 %convolution_convert_fusion = bf16[512,8192]{1,0:T(8,128)(2,1)} fusion(bf16[512,768]{1,0:T(8,128)(2,1)} %get-tuple-element.6, bf16[768,8192]{1,0:T(8,128)(2,1)} %param.8), kind=kOutput, calls=%fused_computation.4 | convolution fusion | flops 6446645248 | bytes 21757952 | tf_op jit(solution)/shard_map/dot_general | solution.py:180
  198.0 0.0 reduce-scatter.5.cloned.1.call-update
  198.0 0.0 copy-start
  198.0 0.0 copy-start.1
  198.0 7.2 %all-to-all-start = ((bf16[16,128,1536]{2,1,0:T(8,128)(2,1)}), bf16[16,128,1536]{2,1,0:T(8,128)(2,1)}, u32[]{:S(2)}, u32[]{:S(2)}) async-start(bf16[16,128,1536]{2,1,0:T(8,128)(2,1)} %get-tuple-element.7), calls=%async_computation.2 | async-start | bytes 12582912 | tf_op jit(solution)/shard_map/all_to_all | solution.py:184
  205.3 0.1 copy.29
  205.4 0.1 copy.30
  205.5 0.1 eq.54
  205.6 0.1 broadcast_in_dim.26
  205.7 0.2 select_reduce_fusion
  205.8 0.2 dynamic-slice_reduce_fusion
  206.0 0.1 fusion.5
  206.1 0.2 dynamic-slice_reduce_fusion.1
  206.3 0.7 fusion.7.select_ref
  207.0 104.9 %all-to-all-done.returned_ref = bf16[16,128,1536]{2,1,0:T(8,128)(2,1)} async-done(((bf16[16,128,1536]{2,1,0:T(8,128)(2,1)}), bf16[16,128,1536]{2,1,0:T(8,128)(2,1)}, u32[]{:S(2)}, u32[]{:S(2)}) %all-to-all-start) | async-done | bytes 6291488 | tf_op jit(solution)/shard_map/all_to_all | solution.py:184
  311.9 5.1 %shard_map.78 = bf16[2,128,1536]{2,1,0:T(8,128)(2,1)} custom-call(f32[16,2]{1,0:T(8,128)} %fusion.7.select_ref, bf16[16,128,1536]{2,1,0:T(8,128)(2,1)} %all-to-all-done.returned_ref), custom_call_target="tpu_custom_call" | custom-call | tf_op jit(solution)/shard_map/pallas_call | solution.py:112
  (15 shorter events, 0.0 us)
Async XLA Ops:
  7.2 48.0 %reduce-scatter.3.cloned.1.call-start = ((), (), s32[]{:S(2)}) async-start(), calls=%async_computation.3 | async-start | bytes 7077888 | tf_op jit(solution)/shard_map/reduce_scatter | solution.py:131
  7.9 137.4 %all-gather.2.cloned.1.call-start = ((), (), s32[]{:S(2)}) async-start(), calls=%async_computation.4 | async-start | bytes 13369344 | tf_op jit(solution)/shard_map/all_gather | solution.py:150
  55.2 261.8 %reduce-scatter.5.cloned.1.call-start = ((), (), s32[]{:S(2)}) async-start(), calls=%async_computation.5 | async-start | bytes 9437184 | tf_op jit(solution)/shard_map/reduce_scatter | solution.py:181
  55.3 16.3 %collective-permute-start = (bf16[512,1024]{1,0:T(8,128)(2,1)}, bf16[512,1024]{1,0:T(8,128)(2,1)S(1)}, u32[]{:S(2)}, u32[]{:S(2)}) collective-permute-start(bf16[512,1024]{1,0:T(8,128)(2,1)} %param.9), channel_id=1, source_target_pairs={{0,2},{1,7},{2,4},{3,1},{4,6},{5,3},{6,0},{7,5},{8,10},{9,15},{10,... | collective-permute-start | bytes 3145736 | tf_op jit(solution)/shard_map/ppermute | solution.py:160
  71.5 16.0 %collective-permute-start.1 = (bf16[512,1024]{1,0:T(8,128)(2,1)S(1)}, bf16[512,1024]{1,0:T(8,128)(2,1)S(1)}, u32[]{:S(2)}, u32[]{:S(2)}) collective-permute-start(bf16[512,1024]{1,0:T(8,128)(2,1)S(1)} %collective-permute-done), channel_id=1, source_target_pairs={{0,2},{1,7},{2,4},{3,1},{4,6},{5,3},{6,0},{7,5},{8,10},{9,15},{10,... | collective-permute-start | bytes 3145736 | tf_op jit(solution)/shard_map/ppermute | solution.py:160
  71.5 33.1 %collective-permute-start.3 = (bf16[512,1024]{1,0:T(8,128)(2,1)}, bf16[512,1024]{1,0:T(8,128)(2,1)S(1)}, u32[]{:S(2)}, u32[]{:S(2)}) collective-permute-start(bf16[512,1024]{1,0:T(8,128)(2,1)} %param.9), channel_id=1, source_target_pairs={{0,1},{1,0},{2,3},{3,2},{4,5},{5,4},{6,7},{7,6},{8,9},{9,8},{10,11... | collective-permute-start | bytes 3145736 | tf_op jit(solution)/shard_map/ppermute | solution.py:161
  72.9 36.1 %copy-start.2 = (s32[16]{0:T(128)}, s32[16]{0:T(128)S(1)}, u32[]{:S(2)}) copy-start(s32[16]{0:T(128)S(1)} %reshape.26.owner_ref) | copy-start | bytes 196
  87.6 16.0 %collective-permute-start.2 = (bf16[512,1024]{1,0:T(8,128)(2,1)S(1)}, bf16[512,1024]{1,0:T(8,128)(2,1)S(1)}, u32[]{:S(2)}, u32[]{:S(2)}) collective-permute-start(bf16[512,1024]{1,0:T(8,128)(2,1)S(1)} %collective-permute-done.1), channel_id=1, source_target_pairs={{0,2},{1,7},{2,4},{3,1},{4,6},{5,3},{6,0},{7,5},{8,10},{9,15},{10,... | collective-permute-start | bytes 3145736 | tf_op jit(solution)/shard_map/ppermute | solution.py:160
  90.5 15.2 %collective-permute-start.4 = (bf16[512,1024]{1,0:T(8,128)(2,1)S(1)}, bf16[512,1024]{1,0:T(8,128)(2,1)S(1)}, u32[]{:S(2)}, u32[]{:S(2)}) collective-permute-start(bf16[512,1024]{1,0:T(8,128)(2,1)S(1)} %collective-permute-done), channel_id=1, source_target_pairs={{0,1},{1,0},{2,3},{3,2},{4,5},{5,4},{6,7},{7,6},{8,9},{9,8},{10,11... | collective-permute-start | bytes 3145736 | tf_op jit(solution)/shard_map/ppermute | solution.py:161
  91.5 15.3 %collective-permute-start.5 = (bf16[512,1024]{1,0:T(8,128)(2,1)S(1)}, bf16[512,1024]{1,0:T(8,128)(2,1)S(1)}, u32[]{:S(2)}, u32[]{:S(2)}) collective-permute-start(bf16[512,1024]{1,0:T(8,128)(2,1)S(1)} %collective-permute-done.1), channel_id=1, source_target_pairs={{0,1},{1,0},{2,3},{3,2},{4,5},{5,4},{6,7},{7,6},{8,9},{9,8},{10,11... | collective-permute-start | bytes 3145736 | tf_op jit(solution)/shard_map/ppermute | solution.py:161
  103.6 4.3 %collective-permute-start.6 = (bf16[512,1024]{1,0:T(8,128)(2,1)S(1)}, bf16[512,1024]{1,0:T(8,128)(2,1)S(1)}, u32[]{:S(2)}, u32[]{:S(2)}) collective-permute-start(bf16[512,1024]{1,0:T(8,128)(2,1)S(1)} %collective-permute-done.2), channel_id=1, source_target_pairs={{0,1},{1,0},{2,3},{3,2},{4,5},{5,4},{6,7},{7,6},{8,9},{9,8},{10,11... | collective-permute-start | bytes 3145736 | tf_op jit(solution)/shard_map/ppermute | solution.py:161
  198.0 7.3 %copy-start = (s32[128,2]{0,1:T(2,128)S(1)}, s32[128,2]{0,1:T(2,128)}, u32[]{:S(2)}) copy-start(s32[128,2]{0,1:T(2,128)} %param.10) | copy-start | bytes 3076
  198.0 7.4 %copy-start.1 = (s32[128,2]{0,1:T(2,128)S(1)}, s32[128,2]{0,1:T(2,128)}, u32[]{:S(2)}) copy-start(s32[128,2]{0,1:T(2,128)} %param.11) | copy-start | bytes 3076
  198.0 113.9 %all-to-all-start = ((bf16[16,128,1536]{2,1,0:T(8,128)(2,1)}), bf16[16,128,1536]{2,1,0:T(8,128)(2,1)}, u32[]{:S(2)}, u32[]{:S(2)}) async-start(bf16[16,128,1536]{2,1,0:T(8,128)(2,1)} %get-tuple-element.7), calls=%async_computation.2 | async-start | bytes 12582912 | tf_op jit(solution)/shard_map/all_to_all | solution.py:184
Sparse Core Ops, SparseCore 0:
  10.4 44.7 reduce-scatter.2
  57.4 87.8 all-gather.1
  198.1 53.9 reduce-scatter.4

commit v8 on v4

--- a/solution.py
+++ b/solution.py
@@ -108,7 +108,7 @@
 
 def slot_sum(select, returned):
     readers, length, width = returned.shape
-    tile = 256
+    tile = 768
     return pl.pallas_call(
         functools.partial(slot_sum_kernel, readers),
         grid=(width // tile,),
@@ -166,13 +166,14 @@
             ((column ^ 1) + 2 * direction * steps) % tensor_count,
         ]
     )
-    w_slots = jnp.take(
-        w_out.reshape(head_width, tensor_count, d_out.shape[1]), slot_block, axis=1, mode="clip"
-    )
+    block_slot = jnp.argmax(
+        slot_block[None, :] == jnp.arange(tensor_count, dtype=jnp.int32)[:, None], axis=1
+    )
+    ordered = jnp.take(jnp.stack(mine + theirs), block_slot, axis=0, mode="clip")
     grad_attended = jnp.einsum(
         "tqc,htc->qh",
-        jnp.stack(mine + theirs),
-        w_slots,
+        ordered,
+        w_out.reshape(head_width, tensor_count, d_out.shape[1]),
         preferred_element_type=jnp.float32,
     ).astype(jnp.bfloat16)
     attended, per_owner = attention(my_owner, picks, queries, everyone, grad_attended, dp_count)

time: 324 us -> 313 us (0.966)
  local copies, waits for them, and re-layouts: 54.9 us -> 19.9 us
  waiting for transfers between devices: 180 us -> 208 us
    unnamed x18 -> x15, local copies, waits for them, and re-layouts: 25.7 us -> 8.96 us
    reshape x1 -> x0, local copies, waits for them, and re-layouts: 15.9 us -> none  [local(): w_out.reshape(head_width, tensor_count, d_out.shape[1])]
    ppermute x3, waiting for transfers between devices: 25.4 us -> 40.5 us  [local(): mine.append(lax.ppermute(mine[-1], 'tensor', ring))]
    all_gather x1, waiting for transfers between devices: 0.01 us -> 14.3 us  [local(): everyone = lax.all_gather(share_blocks, 'dp', axis=0, tiled=True)]
  transfers between devices with their start and end apart: 11 -> 11, of which waited for: 4 -> 6; matrix products, arithmetic and copies ran while one was open for 22% -> 11% of each run, Pallas kernels for 2% -> 2%
where the time goes in v8:
time: 313 us
  waiting for transfers between devices  208 us (66%)
  Pallas kernels  33.6 us (11%)
  matrix products  27.4 us (9%)
  local copies, waits for them, and re-layouts  19.9 us (6%)
  between operations  13.8 us (4%)
  starting transfers between devices  8.31 us (3%)
    all_to_all x1, waiting for transfers between devices, local(): lax.all_to_all(per_owner, 'dp', split_axis=0, concat_axis=0, tiled=True)  105 us
    reduce_scatter x1, waiting for transfers between devices, local(): lax.psum_scatter(kv_part[0], 'tensor', scatter_dimension=1, tiled=True)  47.2 us
    ppermute x3, waiting for transfers between devices, local(): mine.append(lax.ppermute(mine[-1], 'tensor', ring))  40.5 us
    pallas_call x1, Pallas kernels, attention(): pl.pallas_call(functools.partial(attention_kernel, heads), grid_spec=grid...  28.5 us
    all_gather x1, waiting for transfers between devices, local(): everyone = lax.all_gather(share_blocks, 'dp', axis=0, tiled=True)  14.3 us
    dot_general x1, matrix products, local(): jnp.einsum('tqc,htc->qh', ordered, w_out.reshape(head_width, tensor_count...  13.8 us
    dot_general x1, matrix products, local(): partial_out = jnp.dot(attended, w_out, preferred_element_type=jnp.float32)  13.6 us
    unnamed x15, local copies, waits for them, and re-layouts  8.96 us
  transfers between devices with their start and end apart: 11, of which 6 were waited for; matrix products, arithmetic and copies ran while one was open for 11% of the time, Pallas kernels for 2%

profile of v8, /device:TPU:28, one launch (start us, length us, event | category | flops | bytes accessed | tf_op | source)
XLA Modules:
  0.0 313.0 jit_solution(8006708684625473966)
XLA Ops:
  7.2 0.0 reduce-scatter.3.cloned.1.call-start
  7.2 0.7 reduce-scatter.3.cloned.1.call-update
  7.9 0.0 all-gather.2.cloned.1.call-start
  7.9 47.2 %reduce-scatter.3.cloned.1.call-done = bf16[256,1536]{1,0:T(8,128)(2,1)} async-done(((bf16[256,12288]{1,0:T(8,128)(2,1)}), bf16[256,1536]{1,0:T(8,128)(2,1)}) %reduce-scatter.3.cloned.1.call-update) | async-done | bytes 786448 | tf_op jit(solution)/shard_map/reduce_scatter | solution.py:131
  55.2 0.0 all-gather.2.cloned.1.call-update
  55.2 0.0 reduce-scatter.5.cloned.1.call-start
  55.3 0.1 collective-permute-start
  55.3 16.2 %collective-permute-done = bf16[512,1024]{1,0:T(8,128)(2,1)S(1)} collective-permute-done((bf16[512,1024]{1,0:T(8,128)(2,1)}, bf16[512,1024]{1,0:T(8,128)(2,1)S(1)}, u32[]{:S(2)}, u32[]{:S(2)}) %collective-permute-start) | collective-permute-done | bytes 1048608 | tf_op jit(solution)/shard_map/ppermute | solution.py:160
  71.5 0.4 collective-permute-start.3
  71.9 0.8 constant_dynamic-slice_fusion
  72.7 0.1 copy.26
  72.8 0.1 reshape.26.owner_ref
  72.9 0.1 copy.27
  72.9 0.1 reshape.27
  73.0 0.1 pad_add_fusion
  73.1 0.6 iota_reduce_fusion
  73.8 13.8 %collective-permute-done.1 = bf16[512,1024]{1,0:T(8,128)(2,1)S(1)} collective-permute-done((bf16[512,1024]{1,0:T(8,128)(2,1)S(1)}, bf16[512,1024]{1,0:T(8,128)(2,1)S(1)}, u32[]{:S(2)}, u32[]{:S(2)}) %collective-permute-start.1) | collective-permute-done | bytes 1048608 | tf_op jit(solution)/shard_map/ppermute | solution.py:160
  87.6 2.3 bitcast_dynamic-update-slice_fusion.7
  89.9 0.6 multiply_add_fusion.pick_ref
  90.5 1.0 bitcast_dynamic-update-slice_fusion.6
  91.5 0.5 collective-permute-start.5
  92.0 1.0 bitcast_dynamic-update-slice_fusion.5
  93.1 10.5 %collective-permute-done.2 = bf16[512,1024]{1,0:T(8,128)(2,1)S(1)} collective-permute-done((bf16[512,1024]{1,0:T(8,128)(2,1)S(1)}, bf16[512,1024]{1,0:T(8,128)(2,1)S(1)}, u32[]{:S(2)}, u32[]{:S(2)}) %collective-permute-start.2) | collective-permute-done | bytes 1048608 | tf_op jit(solution)/shard_map/ppermute | solution.py:160
  103.6 1.1 bitcast_dynamic-update-slice_fusion.4
  104.6 1.1 bitcast_dynamic-update-slice_fusion.3
  105.7 1.1 bitcast_dynamic-update-slice_fusion.2
  106.8 1.1 bitcast_dynamic-update-slice_fusion.1
  107.9 1.1 bitcast_dynamic-update-slice_fusion
  108.9 8.2 %gather_fusion = bf16[8,512,1024]{2,1,0:T(8,128)(2,1)} fusion(bf16[8,512,1024]{2,1,0:T(8,128)(2,1)} %bitcast_dynamic-update-slice_fusion, s32[1024]{0:T(1024)S(1)} %pad_clamp_fusion), kind=kCustom, calls=%fused_computation | custom fusion | bytes 16777248 | tf_op jit(solution)/shard_map/jit(_take)/gather | solution.py:172
  117.2 13.8 %bitcast_convert_fusion.g_ref = bf16[512,768]{1,0:T(8,128)(2,1)} fusion(bf16[8,512,1024]{2,1,0:T(8,128)(2,1)} %gather_fusion, bf16[96,8,8,1024]{3,2,1,0:T(8,128)(2,1)} %bitcast.33), kind=kOutput, calls=%fused_computation.5 | convolution fusion | flops 6442844160 | bytes 21757952 | tf_op jit(solution)/shard_map/tqc,htc->qh/dot_general | solution.py:173
  131.0 14.3 %all-gather.2.cloned.1.call-done.first_ref.second_ref = bf16[32,128,1536]{2,1,0:T(8,128)(2,1)} async-done(((bf16[2,128,1536]{2,1,0:T(8,128)(2,1)}), bf16[32,128,1536]{2,1,0:T(8,128)(2,1)}) %all-gather.2.cloned.1.call-update) | async-done | bytes 12582928 | tf_op jit(solution)/shard_map/all_gather | solution.py:150
  145.3 28.5 %shard_map.77 = (bf16[512,768]{1,0:T(8,128)(2,1)}, bf16[16,128,1536]{2,1,0:T(8,128)(2,1)}) custom-call(s32[16]{0:T(128)} %copy-done.2, s32[16]{0:T(128)} %multiply_add_fusion.pick_ref, bf16[512,768]{1,0:T(8,128)(2,1)} %q_ref.1, bf16[32,128,1536]{2,1,0:T(8,128)(2,1)} %all-gather.2.cloned.1.call-done.first_ref.second_ref, ...), custom_call_target="tpu_custom_call" | custom-call | tf_op jit(solution)/shard_map/pallas_call | solution.py:88
  173.8 13.6 %convolution_convert_fusion = bf16[512,8192]{1,0:T(8,128)(2,1)} fusion(bf16[512,768]{1,0:T(8,128)(2,1)} %get-tuple-element.6, bf16[768,8192]{1,0:T(8,128)(2,1)} %param.8), kind=kOutput, calls=%fused_computation.4 | convolution fusion | flops 6446645248 | bytes 21757952 | tf_op jit(solution)/shard_map/dot_general | solution.py:180
  187.4 0.0 reduce-scatter.5.cloned.1.call-update
  187.4 0.0 copy-start
  187.4 0.0 copy-start.1
  187.5 7.2 %all-to-all-start = ((bf16[16,128,1536]{2,1,0:T(8,128)(2,1)}), bf16[16,128,1536]{2,1,0:T(8,128)(2,1)}, u32[]{:S(2)}, u32[]{:S(2)}) async-start(bf16[16,128,1536]{2,1,0:T(8,128)(2,1)} %get-tuple-element.7), calls=%async_computation.2 | async-start | bytes 12582912 | tf_op jit(solution)/shard_map/all_to_all | solution.py:184
  194.7 0.1 copy.29
  194.8 0.1 copy.30
  194.9 0.1 eq.54
  195.0 0.1 broadcast_in_dim.26
  195.1 0.2 select_reduce_fusion
  195.3 0.2 dynamic-slice_reduce_fusion
  195.4 0.1 fusion.5
  195.6 0.2 dynamic-slice_reduce_fusion.1
  195.8 0.7 fusion.7.select_ref
  196.4 104.9 %all-to-all-done.returned_ref = bf16[16,128,1536]{2,1,0:T(8,128)(2,1)} async-done(((bf16[16,128,1536]{2,1,0:T(8,128)(2,1)}), bf16[16,128,1536]{2,1,0:T(8,128)(2,1)}, u32[]{:S(2)}, u32[]{:S(2)}) %all-to-all-start) | async-done | bytes 6291488 | tf_op jit(solution)/shard_map/all_to_all | solution.py:184
  301.3 5.1 %shard_map.78 = bf16[2,128,1536]{2,1,0:T(8,128)(2,1)} custom-call(f32[16,2]{1,0:T(8,128)} %fusion.7.select_ref, bf16[16,128,1536]{2,1,0:T(8,128)(2,1)} %all-to-all-done.returned_ref), custom_call_target="tpu_custom_call" | custom-call | tf_op jit(solution)/shard_map/pallas_call | solution.py:112
  (15 shorter events, 0.0 us)
Async XLA Ops:
  7.2 48.0 %reduce-scatter.3.cloned.1.call-start = ((), (), s32[]{:S(2)}) async-start(), calls=%async_computation.3 | async-start | bytes 7077888 | tf_op jit(solution)/shard_map/reduce_scatter | solution.py:131
  7.9 137.4 %all-gather.2.cloned.1.call-start = ((), (), s32[]{:S(2)}) async-start(), calls=%async_computation.4 | async-start | bytes 13369344 | tf_op jit(solution)/shard_map/all_gather | solution.py:150
  55.2 251.2 %reduce-scatter.5.cloned.1.call-start = ((), (), s32[]{:S(2)}) async-start(), calls=%async_computation.5 | async-start | bytes 9437184 | tf_op jit(solution)/shard_map/reduce_scatter | solution.py:181
  55.3 16.3 %collective-permute-start = (bf16[512,1024]{1,0:T(8,128)(2,1)}, bf16[512,1024]{1,0:T(8,128)(2,1)S(1)}, u32[]{:S(2)}, u32[]{:S(2)}) collective-permute-start(bf16[512,1024]{1,0:T(8,128)(2,1)} %param.9), channel_id=1, source_target_pairs={{0,2},{1,7},{2,4},{3,1},{4,6},{5,3},{6,0},{7,5},{8,10},{9,15},{10,... | collective-permute-start | bytes 3145736 | tf_op jit(solution)/shard_map/ppermute | solution.py:160
  71.5 16.0 %collective-permute-start.1 = (bf16[512,1024]{1,0:T(8,128)(2,1)S(1)}, bf16[512,1024]{1,0:T(8,128)(2,1)S(1)}, u32[]{:S(2)}, u32[]{:S(2)}) collective-permute-start(bf16[512,1024]{1,0:T(8,128)(2,1)S(1)} %collective-permute-done), channel_id=1, source_target_pairs={{0,2},{1,7},{2,4},{3,1},{4,6},{5,3},{6,0},{7,5},{8,10},{9,15},{10,... | collective-permute-start | bytes 3145736 | tf_op jit(solution)/shard_map/ppermute | solution.py:160
  71.5 33.1 %collective-permute-start.3 = (bf16[512,1024]{1,0:T(8,128)(2,1)}, bf16[512,1024]{1,0:T(8,128)(2,1)S(1)}, u32[]{:S(2)}, u32[]{:S(2)}) collective-permute-start(bf16[512,1024]{1,0:T(8,128)(2,1)} %param.9), channel_id=1, source_target_pairs={{0,1},{1,0},{2,3},{3,2},{4,5},{5,4},{6,7},{7,6},{8,9},{9,8},{10,11... | collective-permute-start | bytes 3145736 | tf_op jit(solution)/shard_map/ppermute | solution.py:161
  72.9 36.1 %copy-start.2 = (s32[16]{0:T(128)}, s32[16]{0:T(128)S(1)}, u32[]{:S(2)}) copy-start(s32[16]{0:T(128)S(1)} %reshape.26.owner_ref) | copy-start | bytes 196
  87.6 16.0 %collective-permute-start.2 = (bf16[512,1024]{1,0:T(8,128)(2,1)S(1)}, bf16[512,1024]{1,0:T(8,128)(2,1)S(1)}, u32[]{:S(2)}, u32[]{:S(2)}) collective-permute-start(bf16[512,1024]{1,0:T(8,128)(2,1)S(1)} %collective-permute-done.1), channel_id=1, source_target_pairs={{0,2},{1,7},{2,4},{3,1},{4,6},{5,3},{6,0},{7,5},{8,10},{9,15},{10,... | collective-permute-start | bytes 3145736 | tf_op jit(solution)/shard_map/ppermute | solution.py:160
  90.5 15.2 %collective-permute-start.4 = (bf16[512,1024]{1,0:T(8,128)(2,1)S(1)}, bf16[512,1024]{1,0:T(8,128)(2,1)S(1)}, u32[]{:S(2)}, u32[]{:S(2)}) collective-permute-start(bf16[512,1024]{1,0:T(8,128)(2,1)S(1)} %collective-permute-done), channel_id=1, source_target_pairs={{0,1},{1,0},{2,3},{3,2},{4,5},{5,4},{6,7},{7,6},{8,9},{9,8},{10,11... | collective-permute-start | bytes 3145736 | tf_op jit(solution)/shard_map/ppermute | solution.py:161
  91.5 15.3 %collective-permute-start.5 = (bf16[512,1024]{1,0:T(8,128)(2,1)S(1)}, bf16[512,1024]{1,0:T(8,128)(2,1)S(1)}, u32[]{:S(2)}, u32[]{:S(2)}) collective-permute-start(bf16[512,1024]{1,0:T(8,128)(2,1)S(1)} %collective-permute-done.1), channel_id=1, source_target_pairs={{0,1},{1,0},{2,3},{3,2},{4,5},{5,4},{6,7},{7,6},{8,9},{9,8},{10,11... | collective-permute-start | bytes 3145736 | tf_op jit(solution)/shard_map/ppermute | solution.py:161
  103.6 4.3 %collective-permute-start.6 = (bf16[512,1024]{1,0:T(8,128)(2,1)S(1)}, bf16[512,1024]{1,0:T(8,128)(2,1)S(1)}, u32[]{:S(2)}, u32[]{:S(2)}) collective-permute-start(bf16[512,1024]{1,0:T(8,128)(2,1)S(1)} %collective-permute-done.2), channel_id=1, source_target_pairs={{0,1},{1,0},{2,3},{3,2},{4,5},{5,4},{6,7},{7,6},{8,9},{9,8},{10,11... | collective-permute-start | bytes 3145736 | tf_op jit(solution)/shard_map/ppermute | solution.py:161
  187.4 7.3 %copy-start = (s32[128,2]{0,1:T(2,128)S(1)}, s32[128,2]{0,1:T(2,128)}, u32[]{:S(2)}) copy-start(s32[128,2]{0,1:T(2,128)} %param.10) | copy-start | bytes 3076
  187.4 7.4 %copy-start.1 = (s32[128,2]{0,1:T(2,128)S(1)}, s32[128,2]{0,1:T(2,128)}, u32[]{:S(2)}) copy-start(s32[128,2]{0,1:T(2,128)} %param.11) | copy-start | bytes 3076
  187.5 113.9 %all-to-all-start = ((bf16[16,128,1536]{2,1,0:T(8,128)(2,1)}), bf16[16,128,1536]{2,1,0:T(8,128)(2,1)}, u32[]{:S(2)}, u32[]{:S(2)}) async-start(bf16[16,128,1536]{2,1,0:T(8,128)(2,1)} %get-tuple-element.7), calls=%async_computation.2 | async-start | bytes 12582912 | tf_op jit(solution)/shard_map/all_to_all | solution.py:184
Sparse Core Ops, SparseCore 0:
  10.4 44.7 reduce-scatter.2
  57.4 87.8 all-gather.1
  187.6 53.9 reduce-scatter.4

commit v9 on v7

--- a/solution.py
+++ b/solution.py
@@ -13,80 +13,94 @@
 NB_DEV = 2
 
 
-def attention_kernel(heads, owner_ref, pick_ref, q_ref, first_ref, second_ref, g_ref, att_ref, out_ref, acc_ref):
+def attention_kernel(heads, per_step, owner_ref, pick_ref, q_ref, g_ref, *rest):
+    kv_refs = rest[: 2 * per_step]
+    att_ref, out_ref, acc_ref = rest[2 * per_step:]
     factor = HD ** (-0.5)
-    span = pl.program_id(0)
-
-    @pl.when(span == 0)
+    step = pl.program_id(0)
+
+    @pl.when(step == 0)
     def _():
         acc_ref[...] = jnp.zeros_like(acc_ref)
 
-    owners = (owner_ref[2 * span], owner_ref[2 * span + 1])
-    sources = (first_ref, second_ref)
-    nt = (((1,), (1,)), ((), ()))
-    tn = (((0,), (0,)), ((), ()))
-    for h in range(heads):
-        cols = slice(h * HD, (h + 1) * HD)
-        kcols = slice(2 * h * HD, 2 * h * HD + HD)
-        vcols = slice(2 * h * HD + HD, 2 * (h + 1) * HD)
-        q = q_ref[:, cols]
-        g = g_ref[:, cols]
-        keys = [src[0, :, kcols] for src in sources]
-        values = [src[0, :, vcols] for src in sources]
-        scores = [
-            lax.dot_general(q, k, nt, preferred_element_type=jnp.float32) * factor for k in keys
-        ]
-        top = jnp.maximum(
-            jnp.max(scores[0], axis=-1, keepdims=True), jnp.max(scores[1], axis=-1, keepdims=True)
-        )
-        expo = [jnp.exp(s - top) for s in scores]
-        total = jnp.sum(expo[0], axis=-1, keepdims=True) + jnp.sum(expo[1], axis=-1, keepdims=True)
-        probs = [e / total for e in expo]
-        probs_low = [p.astype(jnp.bfloat16) for p in probs]
-        attended = jnp.dot(probs_low[0], values[0], preferred_element_type=jnp.float32) + jnp.dot(
-            probs_low[1], values[1], preferred_element_type=jnp.float32
-        )
-        att_ref[:, cols] = attended.astype(att_ref.dtype)
-        grad_probs = [lax.dot_general(g, v, nt, preferred_element_type=jnp.float32) for v in values]
-        inner = jnp.sum(probs[0] * grad_probs[0], axis=-1, keepdims=True) + jnp.sum(
-            probs[1] * grad_probs[1], axis=-1, keepdims=True
-        )
-        for j in range(2):
-            grad_values = lax.dot_general(probs_low[j], g, tn, preferred_element_type=jnp.float32)
-            grad_scores = (probs[j] * (grad_probs[j] - inner)).astype(jnp.bfloat16)
+    for sub in range(per_step):
+        first_ref, second_ref = kv_refs[2 * sub], kv_refs[2 * sub + 1]
+        span = step * per_step + sub
+        first = owner_ref[2 * span]
+        second = owner_ref[2 * span + 1]
+        rows = slice(sub * SPAN, (sub + 1) * SPAN)
+        for h in range(heads):
+            cols = slice(h * HD, (h + 1) * HD)
+            kcols = slice(2 * h * HD, 2 * h * HD + HD)
+            vcols = slice(2 * h * HD + HD, 2 * (h + 1) * HD)
+            q = q_ref[rows, cols]
+            g = g_ref[rows, cols]
+            k = jnp.concatenate([first_ref[0, :, kcols], second_ref[0, :, kcols]], axis=0)
+            v = jnp.concatenate([first_ref[0, :, vcols], second_ref[0, :, vcols]], axis=0)
+            scores = (
+                lax.dot_general(q, k, (((1,), (1,)), ((), ())), preferred_element_type=jnp.float32)
+                * factor
+            )
+            top = jnp.max(scores, axis=-1, keepdims=True)
+            expo = jnp.exp(scores - top)
+            probs = expo / jnp.sum(expo, axis=-1, keepdims=True)
+            probs_low = probs.astype(jnp.bfloat16)
+            attended = jnp.dot(probs_low, v, preferred_element_type=jnp.float32)
+            att_ref[rows, cols] = attended.astype(att_ref.dtype)
+            grad_values = lax.dot_general(
+                probs_low, g, (((0,), (0,)), ((), ())), preferred_element_type=jnp.float32
+            )
+            grad_probs = lax.dot_general(
+                g, v, (((1,), (1,)), ((), ())), preferred_element_type=jnp.float32
+            )
+            grad_scores = probs * (
+                grad_probs - jnp.sum(probs * grad_probs, axis=-1, keepdims=True)
+            )
+            grad_scores = grad_scores.astype(jnp.bfloat16)
             grad_keys = (
-                lax.dot_general(grad_scores, q, tn, preferred_element_type=jnp.float32) * factor
-            )
-            acc_ref[owners[j], :, kcols] += grad_keys
-            acc_ref[owners[j], :, vcols] += grad_values
-
-    @pl.when(span == pl.num_programs(0) - 1)
+                lax.dot_general(
+                    grad_scores, q, (((0,), (0,)), ((), ())), preferred_element_type=jnp.float32
+                )
+                * factor
+            )
+            acc_ref[first, :, kcols] += grad_keys[:NBR_LEN]
+            acc_ref[second, :, kcols] += grad_keys[NBR_LEN:]
+            acc_ref[first, :, vcols] += grad_values[:NBR_LEN]
+            acc_ref[second, :, vcols] += grad_values[NBR_LEN:]
+
+    @pl.when(step == pl.num_programs(0) - 1)
     def _():
         out_ref[...] = acc_ref[...].astype(out_ref.dtype)
 
 
 def attention(owners, picks, queries, everyone, grad_attended, owner_count):
     rows, width = queries.shape
-    spans = rows // SPAN
+    per_step = 2
+    steps = rows // (SPAN * per_step)
     heads = width // HD
     kv_width = everyone.shape[2]
+
+    def neighbour_spec(index):
+        return pl.BlockSpec(
+            (1, NBR_LEN, kv_width), lambda c, o, n: (n[2 * per_step * c + index], 0, 0)
+        )
+
     grid_spec = pltpu.PrefetchScalarGridSpec(
         num_scalar_prefetch=2,
-        grid=(spans,),
+        grid=(steps,),
         in_specs=[
-            pl.BlockSpec((SPAN, width), lambda c, o, n: (c, 0)),
-            pl.BlockSpec((1, NBR_LEN, kv_width), lambda c, o, n: (n[2 * c], 0, 0)),
-            pl.BlockSpec((1, NBR_LEN, kv_width), lambda c, o, n: (n[2 * c + 1], 0, 0)),
-            pl.BlockSpec((SPAN, width), lambda c, o, n: (c, 0)),
-        ],
+            pl.BlockSpec((SPAN * per_step, width), lambda c, o, n: (c, 0)),
+            pl.BlockSpec((SPAN * per_step, width), lambda c, o, n: (c, 0)),
+        ]
+        + [neighbour_spec(index) for index in range(2 * per_step)],
         out_specs=[
-            pl.BlockSpec((SPAN, width), lambda c, o, n: (c, 0)),
+            pl.BlockSpec((SPAN * per_step, width), lambda c, o, n: (c, 0)),
             pl.BlockSpec((owner_count, NBR_LEN, kv_width), lambda c, o, n: (0, 0, 0)),
         ],
         scratch_shapes=[pltpu.VMEM((owner_count, NBR_LEN, kv_width), jnp.float32)],
     )
     return pl.pallas_call(
-        functools.partial(attention_kernel, heads),
+        functools.partial(attention_kernel, heads, per_step),
         grid_spec=grid_spec,
         out_shape=[
             jax.ShapeDtypeStruct((rows, width), jnp.bfloat16),
@@ -95,7 +109,7 @@
         compiler_params=pltpu.CompilerParams(
             dimension_semantics=("arbitrary",), vmem_limit_bytes=56 * 1024 * 1024
         ),
-    )(owners, picks, queries, everyone, everyone, grad_attended)
+    )(owners, picks, queries, grad_attended, *([everyone] * (2 * per_step)))
 
 
 def slot_sum_kernel(readers, select_ref, returned_ref, out_ref):

time: 324 us -> 312 us (0.963)
  Pallas kernels: 44.2 us -> 32 us
    pallas_call x1, Pallas kernels: 39.1 us -> 26.9 us  [attention(): pl.pallas_call(functools.partial(attention_kernel, heads, per_step), grid...]
  transfers between devices with their start and end apart: 11 -> 11, of which waited for: 6 -> 6; matrix products, arithmetic and copies ran while one was open for 11% -> 12% of each run, Pallas kernels for 2% -> 2%
where the time goes in v9:
time: 312 us; the launch traced here: 311 us
  waiting for transfers between devices  208 us (67%)
  Pallas kernels  32 us (10%)
  matrix products  27.4 us (9%)
  local copies, waits for them, and re-layouts  19.9 us (6%)
  between operations  13.8 us (4%)
  starting transfers between devices  8.32 us (3%)
    all_to_all x1, waiting for transfers between devices, local(): lax.all_to_all(per_owner, 'dp', split_axis=0, concat_axis=0, tiled=True)  105 us
    reduce_scatter x1, waiting for transfers between devices, local(): lax.psum_scatter(kv_part[0], 'tensor', scatter_dimension=1, tiled=True)  47.2 us
    ppermute x3, waiting for transfers between devices, local(): mine.append(lax.ppermute(mine[-1], 'tensor', ring))  40.5 us
    pallas_call x1, Pallas kernels, attention(): pl.pallas_call(functools.partial(attention_kernel, heads, per_step), grid...  26.9 us
    all_gather x1, waiting for transfers between devices, local(): everyone = lax.all_gather(share_blocks, 'dp', axis=0, tiled=True)  14.3 us
    dot_general x1, matrix products, local(): jnp.einsum('tqc,htc->qh', ordered, w_out.reshape(head_width, tensor_count...  13.8 us
    dot_general x1, matrix products, local(): partial_out = jnp.dot(attended, w_out, preferred_element_type=jnp.float32)  13.6 us
    unnamed x15, local copies, waits for them, and re-layouts  8.96 us
  transfers between devices with their start and end apart: 11, of which 6 were waited for; matrix products, arithmetic and copies ran while one was open for 12% of the time, Pallas kernels for 2%

profile of v9, /device:TPU:28, one launch (start us, length us, event | category | flops | bytes accessed | tf_op | source)
XLA Modules:
  0.0 311.4 jit_solution(16291492052471958628)
XLA Ops:
  7.2 0.0 reduce-scatter.3.cloned.1.call-start
  7.2 0.7 reduce-scatter.3.cloned.1.call-update
  7.9 0.0 all-gather.2.cloned.1.call-start
  7.9 47.2 %reduce-scatter.3.cloned.1.call-done = bf16[256,1536]{1,0:T(8,128)(2,1)} async-done(((bf16[256,12288]{1,0:T(8,128)(2,1)}), bf16[256,1536]{1,0:T(8,128)(2,1)}) %reduce-scatter.3.cloned.1.call-update) | async-done | bytes 786448 | tf_op jit(solution)/shard_map/reduce_scatter | solution.py:145
  55.2 0.0 all-gather.2.cloned.1.call-update
  55.2 0.0 reduce-scatter.5.cloned.1.call-start
  55.3 0.1 collective-permute-start
  55.3 16.2 %collective-permute-done = bf16[512,1024]{1,0:T(8,128)(2,1)S(1)} collective-permute-done((bf16[512,1024]{1,0:T(8,128)(2,1)}, bf16[512,1024]{1,0:T(8,128)(2,1)S(1)}, u32[]{:S(2)}, u32[]{:S(2)}) %collective-permute-start) | collective-permute-done | bytes 1048608 | tf_op jit(solution)/shard_map/ppermute | solution.py:174
  71.5 0.4 collective-permute-start.3
  71.9 0.8 constant_dynamic-slice_fusion
  72.7 0.1 copy.26
  72.8 0.1 reshape.26.owner_ref
  72.9 0.1 copy.27
  72.9 0.1 reshape.27
  73.0 0.1 pad_add_fusion
  73.1 0.6 iota_reduce_fusion
  73.8 13.8 %collective-permute-done.1 = bf16[512,1024]{1,0:T(8,128)(2,1)S(1)} collective-permute-done((bf16[512,1024]{1,0:T(8,128)(2,1)S(1)}, bf16[512,1024]{1,0:T(8,128)(2,1)S(1)}, u32[]{:S(2)}, u32[]{:S(2)}) %collective-permute-start.1) | collective-permute-done | bytes 1048608 | tf_op jit(solution)/shard_map/ppermute | solution.py:174
  87.6 2.3 bitcast_dynamic-update-slice_fusion.7
  89.9 0.6 multiply_add_fusion.pick_ref
  90.5 1.0 bitcast_dynamic-update-slice_fusion.6
  91.5 0.5 collective-permute-start.5
  92.0 1.0 bitcast_dynamic-update-slice_fusion.5
  93.1 10.5 %collective-permute-done.2 = bf16[512,1024]{1,0:T(8,128)(2,1)S(1)} collective-permute-done((bf16[512,1024]{1,0:T(8,128)(2,1)S(1)}, bf16[512,1024]{1,0:T(8,128)(2,1)S(1)}, u32[]{:S(2)}, u32[]{:S(2)}) %collective-permute-start.2) | collective-permute-done | bytes 1048608 | tf_op jit(solution)/shard_map/ppermute | solution.py:174
  103.6 1.1 bitcast_dynamic-update-slice_fusion.4
  104.6 1.1 bitcast_dynamic-update-slice_fusion.3
  105.7 1.1 bitcast_dynamic-update-slice_fusion.2
  106.8 1.1 bitcast_dynamic-update-slice_fusion.1
  107.9 1.1 bitcast_dynamic-update-slice_fusion
  108.9 8.2 %gather_fusion = bf16[8,512,1024]{2,1,0:T(8,128)(2,1)} fusion(bf16[8,512,1024]{2,1,0:T(8,128)(2,1)} %bitcast_dynamic-update-slice_fusion, s32[1024]{0:T(1024)S(1)} %pad_clamp_fusion), kind=kCustom, calls=%fused_computation | custom fusion | bytes 16777248 | tf_op jit(solution)/shard_map/jit(_take)/gather | solution.py:186
  117.2 13.8 %bitcast_convert_fusion.g_ref = bf16[512,768]{1,0:T(8,128)(2,1)} fusion(bf16[8,512,1024]{2,1,0:T(8,128)(2,1)} %gather_fusion, bf16[96,8,8,1024]{3,2,1,0:T(8,128)(2,1)} %bitcast.33), kind=kOutput, calls=%fused_computation.5 | convolution fusion | flops 6442844160 | bytes 21757952 | tf_op jit(solution)/shard_map/tqc,htc->qh/dot_general | solution.py:187
  131.0 14.3 %all-gather.2.cloned.1.call-done.rest_0_.rest_1_.rest_2_.rest_3_ = bf16[32,128,1536]{2,1,0:T(8,128)(2,1)} async-done(((bf16[2,128,1536]{2,1,0:T(8,128)(2,1)}), bf16[32,128,1536]{2,1,0:T(8,128)(2,1)}) %all-gather.2.cloned.1.call-update) | async-done | bytes 12582928 | tf_op jit(solution)/shard_map/all_gather | solution.py:164
  145.3 26.9 %shard_map.77 = (bf16[512,768]{1,0:T(8,128)(2,1)}, bf16[16,128,1536]{2,1,0:T(8,128)(2,1)}) custom-call(s32[16]{0:T(128)} %copy-done.2, s32[16]{0:T(128)} %multiply_add_fusion.pick_ref, bf16[512,768]{1,0:T(8,128)(2,1)} %q_ref.1, bf16[512,768]{1,0:T(8,128)(2,1)} %bitcast_convert_fusion.g_ref, ...), custom_call_target="tpu_custom_call" | custom-call | tf_op jit(solution)/shard_map/pallas_call | solution.py:102
  172.2 13.6 %convolution_convert_fusion = bf16[512,8192]{1,0:T(8,128)(2,1)} fusion(bf16[512,768]{1,0:T(8,128)(2,1)} %get-tuple-element.6, bf16[768,8192]{1,0:T(8,128)(2,1)} %param.8), kind=kOutput, calls=%fused_computation.4 | convolution fusion | flops 6446645248 | bytes 21757952 | tf_op jit(solution)/shard_map/dot_general | solution.py:194
  185.8 0.0 reduce-scatter.5.cloned.1.call-update
  185.8 0.0 copy-start
  185.8 0.0 copy-start.1
  185.8 7.2 %all-to-all-start = ((bf16[16,128,1536]{2,1,0:T(8,128)(2,1)}), bf16[16,128,1536]{2,1,0:T(8,128)(2,1)}, u32[]{:S(2)}, u32[]{:S(2)}) async-start(bf16[16,128,1536]{2,1,0:T(8,128)(2,1)} %get-tuple-element.7), calls=%async_computation.2 | async-start | bytes 12582912 | tf_op jit(solution)/shard_map/all_to_all | solution.py:198
  193.1 0.1 copy.30
  193.2 0.1 copy.29
  193.3 0.1 broadcast_in_dim.26
  193.4 0.1 eq.54
  193.5 0.2 select_reduce_fusion
  193.6 0.2 dynamic-slice_reduce_fusion
  193.8 0.1 fusion.5
  194.0 0.2 dynamic-slice_reduce_fusion.1
  194.1 0.7 fusion.7.select_ref
  194.8 104.9 %all-to-all-done.returned_ref = bf16[16,128,1536]{2,1,0:T(8,128)(2,1)} async-done(((bf16[16,128,1536]{2,1,0:T(8,128)(2,1)}), bf16[16,128,1536]{2,1,0:T(8,128)(2,1)}, u32[]{:S(2)}, u32[]{:S(2)}) %all-to-all-start) | async-done | bytes 6291488 | tf_op jit(solution)/shard_map/all_to_all | solution.py:198
  299.7 5.1 %shard_map.78 = bf16[2,128,1536]{2,1,0:T(8,128)(2,1)} custom-call(f32[16,2]{1,0:T(8,128)} %fusion.7.select_ref, bf16[16,128,1536]{2,1,0:T(8,128)(2,1)} %all-to-all-done.returned_ref), custom_call_target="tpu_custom_call" | custom-call | tf_op jit(solution)/shard_map/pallas_call | solution.py:126
  (15 shorter events, 0.0 us)
Async XLA Ops:
  7.2 48.0 %reduce-scatter.3.cloned.1.call-start = ((), (), s32[]{:S(2)}) async-start(), calls=%async_computation.3 | async-start | bytes 7077888 | tf_op jit(solution)/shard_map/reduce_scatter | solution.py:145
  7.9 137.4 %all-gather.2.cloned.1.call-start = ((), (), s32[]{:S(2)}) async-start(), calls=%async_computation.4 | async-start | bytes 13369344 | tf_op jit(solution)/shard_map/all_gather | solution.py:164
  55.2 249.6 %reduce-scatter.5.cloned.1.call-start = ((), (), s32[]{:S(2)}) async-start(), calls=%async_computation.5 | async-start | bytes 9437184 | tf_op jit(solution)/shard_map/reduce_scatter | solution.py:195
  55.3 16.3 %collective-permute-start = (bf16[512,1024]{1,0:T(8,128)(2,1)}, bf16[512,1024]{1,0:T(8,128)(2,1)S(1)}, u32[]{:S(2)}, u32[]{:S(2)}) collective-permute-start(bf16[512,1024]{1,0:T(8,128)(2,1)} %param.9), channel_id=1, source_target_pairs={{0,2},{1,7},{2,4},{3,1},{4,6},{5,3},{6,0},{7,5},{8,10},{9,15},{10,... | collective-permute-start | bytes 3145736 | tf_op jit(solution)/shard_map/ppermute | solution.py:174
  71.5 16.0 %collective-permute-start.1 = (bf16[512,1024]{1,0:T(8,128)(2,1)S(1)}, bf16[512,1024]{1,0:T(8,128)(2,1)S(1)}, u32[]{:S(2)}, u32[]{:S(2)}) collective-permute-start(bf16[512,1024]{1,0:T(8,128)(2,1)S(1)} %collective-permute-done), channel_id=1, source_target_pairs={{0,2},{1,7},{2,4},{3,1},{4,6},{5,3},{6,0},{7,5},{8,10},{9,15},{10,... | collective-permute-start | bytes 3145736 | tf_op jit(solution)/shard_map/ppermute | solution.py:174
  71.5 33.1 %collective-permute-start.3 = (bf16[512,1024]{1,0:T(8,128)(2,1)}, bf16[512,1024]{1,0:T(8,128)(2,1)S(1)}, u32[]{:S(2)}, u32[]{:S(2)}) collective-permute-start(bf16[512,1024]{1,0:T(8,128)(2,1)} %param.9), channel_id=1, source_target_pairs={{0,1},{1,0},{2,3},{3,2},{4,5},{5,4},{6,7},{7,6},{8,9},{9,8},{10,11... | collective-permute-start | bytes 3145736 | tf_op jit(solution)/shard_map/ppermute | solution.py:175
  72.9 36.1 %copy-start.2 = (s32[16]{0:T(128)}, s32[16]{0:T(128)S(1)}, u32[]{:S(2)}) copy-start(s32[16]{0:T(128)S(1)} %reshape.26.owner_ref) | copy-start | bytes 196
  87.6 16.0 %collective-permute-start.2 = (bf16[512,1024]{1,0:T(8,128)(2,1)S(1)}, bf16[512,1024]{1,0:T(8,128)(2,1)S(1)}, u32[]{:S(2)}, u32[]{:S(2)}) collective-permute-start(bf16[512,1024]{1,0:T(8,128)(2,1)S(1)} %collective-permute-done.1), channel_id=1, source_target_pairs={{0,2},{1,7},{2,4},{3,1},{4,6},{5,3},{6,0},{7,5},{8,10},{9,15},{10,... | collective-permute-start | bytes 3145736 | tf_op jit(solution)/shard_map/ppermute | solution.py:174
  90.5 15.2 %collective-permute-start.4 = (bf16[512,1024]{1,0:T(8,128)(2,1)S(1)}, bf16[512,1024]{1,0:T(8,128)(2,1)S(1)}, u32[]{:S(2)}, u32[]{:S(2)}) collective-permute-start(bf16[512,1024]{1,0:T(8,128)(2,1)S(1)} %collective-permute-done), channel_id=1, source_target_pairs={{0,1},{1,0},{2,3},{3,2},{4,5},{5,4},{6,7},{7,6},{8,9},{9,8},{10,11... | collective-permute-start | bytes 3145736 | tf_op jit(solution)/shard_map/ppermute | solution.py:175
  91.5 15.3 %collective-permute-start.5 = (bf16[512,1024]{1,0:T(8,128)(2,1)S(1)}, bf16[512,1024]{1,0:T(8,128)(2,1)S(1)}, u32[]{:S(2)}, u32[]{:S(2)}) collective-permute-start(bf16[512,1024]{1,0:T(8,128)(2,1)S(1)} %collective-permute-done.1), channel_id=1, source_target_pairs={{0,1},{1,0},{2,3},{3,2},{4,5},{5,4},{6,7},{7,6},{8,9},{9,8},{10,11... | collective-permute-start | bytes 3145736 | tf_op jit(solution)/shard_map/ppermute | solution.py:175
  103.6 4.3 %collective-permute-start.6 = (bf16[512,1024]{1,0:T(8,128)(2,1)S(1)}, bf16[512,1024]{1,0:T(8,128)(2,1)S(1)}, u32[]{:S(2)}, u32[]{:S(2)}) collective-permute-start(bf16[512,1024]{1,0:T(8,128)(2,1)S(1)} %collective-permute-done.2), channel_id=1, source_target_pairs={{0,1},{1,0},{2,3},{3,2},{4,5},{5,4},{6,7},{7,6},{8,9},{9,8},{10,11... | collective-permute-start | bytes 3145736 | tf_op jit(solution)/shard_map/ppermute | solution.py:175
  185.8 7.3 %copy-start = (s32[128,2]{0,1:T(2,128)S(1)}, s32[128,2]{0,1:T(2,128)}, u32[]{:S(2)}) copy-start(s32[128,2]{0,1:T(2,128)} %param.11) | copy-start | bytes 3076
  185.8 7.4 %copy-start.1 = (s32[128,2]{0,1:T(2,128)S(1)}, s32[128,2]{0,1:T(2,128)}, u32[]{:S(2)}) copy-start(s32[128,2]{0,1:T(2,128)} %param.10) | copy-start | bytes 3076
  185.8 113.9 %all-to-all-start = ((bf16[16,128,1536]{2,1,0:T(8,128)(2,1)}), bf16[16,128,1536]{2,1,0:T(8,128)(2,1)}, u32[]{:S(2)}, u32[]{:S(2)}) async-start(bf16[16,128,1536]{2,1,0:T(8,128)(2,1)} %get-tuple-element.7), calls=%async_computation.2 | async-start | bytes 12582912 | tf_op jit(solution)/shard_map/all_to_all | solution.py:198
Sparse Core Ops, SparseCore 0:
  10.4 44.7 reduce-scatter.2
  57.4 87.8 all-gather.1
  185.9 53.9 reduce-scatter.4

commit v10 on v9

--- a/solution.py
+++ b/solution.py
@@ -13,9 +13,9 @@
 NB_DEV = 2
 
 
-def attention_kernel(heads, per_step, owner_ref, pick_ref, q_ref, g_ref, *rest):
+def attention_kernel(heads, per_step, split, owner_ref, pick_ref, slot_ref, q_ref, g_ref, *rest):
     kv_refs = rest[: 2 * per_step]
-    att_ref, out_ref, acc_ref = rest[2 * per_step:]
+    att_ref, spread_ref, out_ref, acc_ref = rest[2 * per_step:]
     factor = HD ** (-0.5)
     step = pl.program_id(0)
 
@@ -70,10 +70,17 @@
 
     @pl.when(step == pl.num_programs(0) - 1)
     def _():
-        out_ref[...] = acc_ref[...].astype(out_ref.dtype)
-
-
-def attention(owners, picks, queries, everyone, grad_attended, owner_count):
+        out_ref[...] = acc_ref[:, :, split:].astype(out_ref.dtype)
+        for owner in range(acc_ref.shape[0]):
+            block = acc_ref[owner, :, :split]
+            slot = slot_ref[owner]
+            for target in range(NB_DEV):
+                spread_ref[owner, target] = jnp.where(
+                    slot == target, block, jnp.zeros_like(block)
+                ).astype(spread_ref.dtype)
+
+
+def attention(owners, picks, slots, queries, everyone, grad_attended, owner_count, split):
     rows, width = queries.shape
     per_step = 2
     steps = rows // (SPAN * per_step)
@@ -82,34 +89,36 @@
 
     def neighbour_spec(index):
         return pl.BlockSpec(
-            (1, NBR_LEN, kv_width), lambda c, o, n: (n[2 * per_step * c + index], 0, 0)
+            (1, NBR_LEN, kv_width), lambda c, o, n, s: (n[2 * per_step * c + index], 0, 0)
         )
 
     grid_spec = pltpu.PrefetchScalarGridSpec(
-        num_scalar_prefetch=2,
+        num_scalar_prefetch=3,
         grid=(steps,),
         in_specs=[
-            pl.BlockSpec((SPAN * per_step, width), lambda c, o, n: (c, 0)),
-            pl.BlockSpec((SPAN * per_step, width), lambda c, o, n: (c, 0)),
+            pl.BlockSpec((SPAN * per_step, width), lambda c, o, n, s: (c, 0)),
+            pl.BlockSpec((SPAN * per_step, width), lambda c, o, n, s: (c, 0)),
         ]
         + [neighbour_spec(index) for index in range(2 * per_step)],
         out_specs=[
-            pl.BlockSpec((SPAN * per_step, width), lambda c, o, n: (c, 0)),
-            pl.BlockSpec((owner_count, NBR_LEN, kv_width), lambda c, o, n: (0, 0, 0)),
+            pl.BlockSpec((SPAN * per_step, width), lambda c, o, n, s: (c, 0)),
+            pl.BlockSpec((owner_count, NB_DEV, NBR_LEN, split), lambda c, o, n, s: (0, 0, 0, 0)),
+            pl.BlockSpec((owner_count, NBR_LEN, kv_width - split), lambda c, o, n, s: (0, 0, 0)),
         ],
         scratch_shapes=[pltpu.VMEM((owner_count, NBR_LEN, kv_width), jnp.float32)],
     )
     return pl.pallas_call(
-        functools.partial(attention_kernel, heads, per_step),
+        functools.partial(attention_kernel, heads, per_step, split),
         grid_spec=grid_spec,
         out_shape=[
             jax.ShapeDtypeStruct((rows, width), jnp.bfloat16),
-            jax.ShapeDtypeStruct((owner_count, NBR_LEN, kv_width), jnp.bfloat16),
+            jax.ShapeDtypeStruct((owner_count, NB_DEV, NBR_LEN, split), jnp.bfloat16),
+            jax.ShapeDtypeStruct((owner_count, NBR_LEN, kv_width - split), jnp.bfloat16),
         ],
         compiler_params=pltpu.CompilerParams(
             dimension_semantics=("arbitrary",), vmem_limit_bytes=56 * 1024 * 1024
         ),
-    )(owners, picks, queries, grad_attended, *([everyone] * (2 * per_step)))
+    )(owners, picks, slots, queries, grad_attended, *([everyone] * (2 * per_step)))
 
 
 def slot_sum_kernel(readers, select_ref, returned_ref, out_ref):
@@ -122,7 +131,8 @@
 
 def slot_sum(select, returned):
     readers, length, width = returned.shape
-    tile = 768
+    tile = 384
+    assert width % tile == 0
     return pl.pallas_call(
         functools.partial(slot_sum_kernel, readers),
         grid=(width // tile,),
@@ -190,13 +200,20 @@
         w_out.reshape(head_width, tensor_count, d_out.shape[1]),
         preferred_element_type=jnp.float32,
     ).astype(jnp.bfloat16)
-    attended, per_owner = attention(my_owner, picks, queries, everyone, grad_attended, dp_count)
+    split = share_width // 4
+    my_slots = lax.dynamic_index_in_dim(slot_from, reader, 0, False)
+    attended, spread_part, per_owner = attention(
+        my_owner, picks, my_slots, queries, everyone, grad_attended, dp_count, split
+    )
     partial_out = jnp.dot(attended, w_out, preferred_element_type=jnp.float32)
     mixed = lax.psum_scatter(
         partial_out.astype(jnp.bfloat16), "tensor", scatter_dimension=1, tiled=True
     )
+    reduced_part = lax.psum_scatter(
+        spread_part.reshape(dp_count * NB_DEV, NBR_LEN, split), "dp", scatter_dimension=0, tiled=True
+    )
     returned = lax.all_to_all(per_owner, "dp", split_axis=0, concat_axis=0, tiled=True)
-    owner_grad = slot_sum(owner_select, returned)
+    owner_grad = jnp.concatenate([reduced_part, slot_sum(owner_select, returned)], axis=2)
     d_kv = owner_grad.reshape(NB_DEV * NBR_LEN, share_width)
     return (mixed, d_kv)
 

time: 312 us -> 369 us (1.18)
  waiting for transfers between devices: 208 us -> 259 us
    reduce_scatter x1, waiting for transfers between devices: 0.01 us -> 54.7 us  [local(): lax.psum_scatter(partial_out.astype(jnp.bfloat16), 'tensor', scatter_dime...]
    all_to_all x1, waiting for transfers between devices: 105 us -> 81 us  [local(): lax.all_to_all(per_owner, 'dp', split_axis=0, concat_axis=0, tiled=True)]
    reduce_scatter x0 -> x1, waiting for transfers between devices: none -> 23.5 us  [local(): lax.psum_scatter(spread_part.reshape(dp_count * NB_DEV, NBR_LEN, split),...]
    unnamed x15 -> x11, local copies, waits for them, and re-layouts: 8.96 us -> 10.3 us
  transfers between devices with their start and end apart: 11 -> 12, of which waited for: 6 -> 8; matrix products, arithmetic and copies ran while one was open for 12% -> 15% of each run, Pallas kernels for 2% -> 1%
where the time goes in v10:
time: 369 us; the launch traced here: 368 us
  waiting for transfers between devices  259 us (70%)
  Pallas kernels  32.6 us (9%)
  matrix products  27.4 us (7%)
  local copies, waits for them, and re-layouts  21.8 us (6%)
  between operations  13.8 us (4%)
  starting transfers between devices  8.59 us (2%)
  other arithmetic  4.29 us (1%)
    all_to_all x1, waiting for transfers between devices, local(): lax.all_to_all(per_owner, 'dp', split_axis=0, concat_axis=0, tiled=True)  81 us
    reduce_scatter x1, waiting for transfers between devices, local(): lax.psum_scatter(partial_out.astype(jnp.bfloat16), 'tensor', scatter_dime...  54.7 us
    reduce_scatter x1, waiting for transfers between devices, local(): lax.psum_scatter(kv_part[0], 'tensor', scatter_dimension=1, tiled=True)  47.2 us
    ppermute x3, waiting for transfers between devices, local(): mine.append(lax.ppermute(mine[-1], 'tensor', ring))  38 us
    pallas_call x1, Pallas kernels, attention(): pl.pallas_call(functools.partial(attention_kernel, heads, per_step, split...  27.7 us
    reduce_scatter x1, waiting for transfers between devices, local(): lax.psum_scatter(spread_part.reshape(dp_count * NB_DEV, NBR_LEN, split),...  23.5 us
    all_gather x1, waiting for transfers between devices, local(): everyone = lax.all_gather(share_blocks, 'dp', axis=0, tiled=True)  14.2 us
    dot_general x1, matrix products, local(): jnp.einsum('tqc,htc->qh', ordered, w_out.reshape(head_width, tensor_count...  13.8 us
  transfers between devices with their start and end apart: 12, of which 8 were waited for; matrix products, arithmetic and copies ran while one was open for 15% of the time, Pallas kernels for 1%

profile of v10, /device:TPU:28, one launch (start us, length us, event | category | flops | bytes accessed | tf_op | source)
XLA Modules:
  0.0 367.8 jit_solution(12259838470006689429)
XLA Ops:
  7.2 0.7 reduce-scatter.4.cloned.1.call-update
  7.9 0.0 all-gather.2.cloned.1.call-start
  7.9 47.2 %reduce-scatter.4.cloned.1.call-done = bf16[256,1536]{1,0:T(8,128)(2,1)} async-done(((bf16[256,12288]{1,0:T(8,128)(2,1)}), bf16[256,1536]{1,0:T(8,128)(2,1)}) %reduce-scatter.4.cloned.1.call-update) | async-done | bytes 786448 | tf_op jit(solution)/shard_map/reduce_scatter | solution.py:155
  55.2 0.0 reduce-scatter.8.cloned.1.call-start
  55.3 0.1 collective-permute-start
  55.3 16.2 %collective-permute-done = bf16[512,1024]{1,0:T(8,128)(2,1)S(1)} collective-permute-done((bf16[512,1024]{1,0:T(8,128)(2,1)}, bf16[512,1024]{1,0:T(8,128)(2,1)S(1)}, u32[]{:S(2)}, u32[]{:S(2)}) %collective-permute-start) | collective-permute-done | bytes 1048608 | tf_op jit(solution)/shard_map/ppermute | solution.py:184
  71.5 0.4 collective-permute-start.3
  71.9 0.8 copy.28
  72.7 0.8 copy.29
  73.5 0.8 constant_dynamic-slice_fusion.1
  74.3 0.1 copy.26
  74.3 0.1 reshape.29.owner_ref
  74.4 0.1 copy.27
  74.5 0.1 reshape.30
  74.6 0.1 eq.51
  74.7 0.1 broadcast_in_dim.25
  74.8 0.1 pad_add_fusion
  74.9 0.2 select_reduce_fusion
  75.0 0.6 fusion.8.slot_ref
  75.6 0.6 iota_reduce_fusion
  76.2 11.3 %collective-permute-done.1 = bf16[512,1024]{1,0:T(8,128)(2,1)S(1)} collective-permute-done((bf16[512,1024]{1,0:T(8,128)(2,1)S(1)}, bf16[512,1024]{1,0:T(8,128)(2,1)S(1)}, u32[]{:S(2)}, u32[]{:S(2)}) %collective-permute-start.1) | collective-permute-done | bytes 1048608 | tf_op jit(solution)/shard_map/ppermute | solution.py:184
  87.6 2.3 bitcast_dynamic-update-slice_fusion.7
  89.9 0.6 multiply_add_fusion.pick_ref
  90.5 1.0 bitcast_dynamic-update-slice_fusion.6
  91.5 0.5 collective-permute-start.5
  92.0 1.0 bitcast_dynamic-update-slice_fusion.5
  93.1 10.5 %collective-permute-done.2 = bf16[512,1024]{1,0:T(8,128)(2,1)S(1)} collective-permute-done((bf16[512,1024]{1,0:T(8,128)(2,1)S(1)}, bf16[512,1024]{1,0:T(8,128)(2,1)S(1)}, u32[]{:S(2)}, u32[]{:S(2)}) %collective-permute-start.2) | collective-permute-done | bytes 1048608 | tf_op jit(solution)/shard_map/ppermute | solution.py:184
  103.6 1.1 bitcast_dynamic-update-slice_fusion.4
  104.6 1.1 bitcast_dynamic-update-slice_fusion.3
  105.7 1.1 bitcast_dynamic-update-slice_fusion.2
  106.8 1.1 bitcast_dynamic-update-slice_fusion.1
  107.9 1.1 bitcast_dynamic-update-slice_fusion
  108.9 8.2 %gather_fusion = bf16[8,512,1024]{2,1,0:T(8,128)(2,1)} fusion(bf16[8,512,1024]{2,1,0:T(8,128)(2,1)} %bitcast_dynamic-update-slice_fusion, s32[1024]{0:T(1024)S(1)} %pad_clamp_fusion), kind=kCustom, calls=%fused_computation | custom fusion | bytes 16777248 | tf_op jit(solution)/shard_map/jit(_take)/gather | solution.py:196
  117.2 13.8 %bitcast_convert_fusion.g_ref = bf16[512,768]{1,0:T(8,128)(2,1)} fusion(bf16[8,512,1024]{2,1,0:T(8,128)(2,1)} %gather_fusion, bf16[96,8,8,1024]{3,2,1,0:T(8,128)(2,1)} %bitcast.37), kind=kOutput, calls=%fused_computation.5 | convolution fusion | flops 6442844160 | bytes 21757952 | tf_op jit(solution)/shard_map/tqc,htc->qh/dot_general | solution.py:197
  131.0 14.2 %all-gather.2.cloned.1.call-done.rest_0_.rest_1_.rest_2_.rest_3_ = bf16[32,128,1536]{2,1,0:T(8,128)(2,1)} async-done(((bf16[2,128,1536]{2,1,0:T(8,128)(2,1)}), bf16[32,128,1536]{2,1,0:T(8,128)(2,1)}) %all-gather.2.cloned.1.call-update) | async-done | bytes 12582928 | tf_op jit(solution)/shard_map/all_gather | solution.py:174
  145.2 27.7 %shard_map.77 = (bf16[512,768]{1,0:T(8,128)(2,1)}, bf16[16,2,128,384]{3,2,1,0:T(8,128)(2,1)}, bf16[16,128,1152]{2,1,0:T(8,128)(2,1)}) custom-call(s32[16]{0:T(128)} %copy-done, s32[16]{0:T(128)} %multiply_add_fusion.pick_ref, s32[16]{0:T(128)} %fusion.8.slot_ref, bf16[512,768]{1,0:T(8,128)(2,1)} %q_ref.1, bf16[512,768]{1,0:T(8,128)(2,1)} %bitcast_convert_fusion.g_ref, ...), custom_call_target="tpu_custom_call" | custom-call | tf_op jit(solution)/shard_map/pallas_call | solution.py:110
  172.9 0.0 reduce-scatter.6.cloned.1.call-start
  173.0 13.6 %convolution_convert_fusion = bf16[512,8192]{1,0:T(8,128)(2,1)} fusion(bf16[512,768]{1,0:T(8,128)(2,1)} %get-tuple-element.7, bf16[768,8192]{1,0:T(8,128)(2,1)} %param.8), kind=kOutput, calls=%fused_computation.4 | convolution fusion | flops 6446645248 | bytes 21757952 | tf_op jit(solution)/shard_map/dot_general | solution.py:208
  186.6 7.5 %all-to-all-start = ((bf16[16,128,1152]{2,1,0:T(8,128)(2,1)}), bf16[16,128,1152]{2,1,0:T(8,128)(2,1)}, u32[]{:S(2)}, u32[]{:S(2)}) async-start(bf16[16,128,1152]{2,1,0:T(8,128)(2,1)} %get-tuple-element.9), calls=%async_computation.3 | async-start | bytes 9437184 | tf_op jit(solution)/shard_map/all_to_all | solution.py:215
  194.0 0.2 dynamic-slice_reduce_fusion
  194.2 0.1 fusion.5
  194.3 0.2 dynamic-slice_reduce_fusion.1
  194.5 0.7 fusion.7.select_ref
  195.2 81.0 %all-to-all-done.returned_ref = bf16[16,128,1152]{2,1,0:T(8,128)(2,1)} async-done(((bf16[16,128,1152]{2,1,0:T(8,128)(2,1)}), bf16[16,128,1152]{2,1,0:T(8,128)(2,1)}, u32[]{:S(2)}, u32[]{:S(2)}) %all-to-all-start) | async-done | bytes 4718624 | tf_op jit(solution)/shard_map/all_to_all | solution.py:215
  276.2 4.9 %shard_map.78 = bf16[2,128,1152]{2,1,0:T(8,128)(2,1)} custom-call(f32[16,2]{1,0:T(8,128)} %fusion.7.select_ref, bf16[16,128,1152]{2,1,0:T(8,128)(2,1)} %all-to-all-done.returned_ref), custom_call_target="tpu_custom_call" | custom-call | tf_op jit(solution)/shard_map/pallas_call | solution.py:136
  281.1 23.5 %reduce-scatter.8.cloned.1.call-done = bf16[2,128,384]{2,1,0:T(8,128)(2,1)} async-done(((bf16[32,128,384]{2,1,0:T(8,128)(2,1)}), bf16[2,128,384]{2,1,0:T(8,128)(2,1)}) %reduce-scatter.8.cloned.1.call-update) | async-done | bytes 196624 | tf_op jit(solution)/shard_map/reduce_scatter | solution.py:212
  304.6 2.0 pad_maximum_fusion
  306.6 54.7 %reduce-scatter.6.cloned.1.call-done = bf16[512,1024]{1,0:T(8,128)(2,1)} async-done(((bf16[512,8192]{1,0:T(8,128)(2,1)}), bf16[512,1024]{1,0:T(8,128)(2,1)}) %reduce-scatter.6.cloned.1.call-update) | async-done | bytes 1048592 | tf_op jit(solution)/shard_map/reduce_scatter | solution.py:209
  (16 shorter events, 0.1 us)
Async XLA Ops:
  7.2 48.0 %reduce-scatter.4.cloned.1.call-start = ((), (), s32[]{:S(2)}) async-start(), calls=%async_computation.4 | async-start | bytes 7077888 | tf_op jit(solution)/shard_map/reduce_scatter | solution.py:155
  7.9 137.3 %all-gather.2.cloned.1.call-start = ((), (), s32[]{:S(2)}) async-start(), calls=%async_computation.5 | async-start | bytes 13369344 | tf_op jit(solution)/shard_map/all_gather | solution.py:174
  55.2 249.4 %reduce-scatter.8.cloned.1.call-start = ((), (), s32[]{:S(2)}) async-start(), calls=%async_computation.7 | async-start | bytes 3342336 | tf_op jit(solution)/shard_map/reduce_scatter | solution.py:212
  55.3 16.3 %collective-permute-start = (bf16[512,1024]{1,0:T(8,128)(2,1)}, bf16[512,1024]{1,0:T(8,128)(2,1)S(1)}, u32[]{:S(2)}, u32[]{:S(2)}) collective-permute-start(bf16[512,1024]{1,0:T(8,128)(2,1)} %param.9), channel_id=1, source_target_pairs={{0,2},{1,7},{2,4},{3,1},{4,6},{5,3},{6,0},{7,5},{8,10},{9,15},{10,... | collective-permute-start | bytes 3145736 | tf_op jit(solution)/shard_map/ppermute | solution.py:184
  71.5 16.0 %collective-permute-start.1 = (bf16[512,1024]{1,0:T(8,128)(2,1)S(1)}, bf16[512,1024]{1,0:T(8,128)(2,1)S(1)}, u32[]{:S(2)}, u32[]{:S(2)}) collective-permute-start(bf16[512,1024]{1,0:T(8,128)(2,1)S(1)} %collective-permute-done), channel_id=1, source_target_pairs={{0,2},{1,7},{2,4},{3,1},{4,6},{5,3},{6,0},{7,5},{8,10},{9,15},{10,... | collective-permute-start | bytes 3145736 | tf_op jit(solution)/shard_map/ppermute | solution.py:184
  71.5 33.1 %collective-permute-start.3 = (bf16[512,1024]{1,0:T(8,128)(2,1)}, bf16[512,1024]{1,0:T(8,128)(2,1)S(1)}, u32[]{:S(2)}, u32[]{:S(2)}) collective-permute-start(bf16[512,1024]{1,0:T(8,128)(2,1)} %param.9), channel_id=1, source_target_pairs={{0,1},{1,0},{2,3},{3,2},{4,5},{5,4},{6,7},{7,6},{8,9},{9,8},{10,11... | collective-permute-start | bytes 3145736 | tf_op jit(solution)/shard_map/ppermute | solution.py:185
  74.4 34.5 %copy-start = (s32[16]{0:T(128)}, s32[16]{0:T(128)S(1)}, u32[]{:S(2)}) copy-start(s32[16]{0:T(128)S(1)} %reshape.29.owner_ref) | copy-start | bytes 196
  87.6 16.0 %collective-permute-start.2 = (bf16[512,1024]{1,0:T(8,128)(2,1)S(1)}, bf16[512,1024]{1,0:T(8,128)(2,1)S(1)}, u32[]{:S(2)}, u32[]{:S(2)}) collective-permute-start(bf16[512,1024]{1,0:T(8,128)(2,1)S(1)} %collective-permute-done.1), channel_id=1, source_target_pairs={{0,2},{1,7},{2,4},{3,1},{4,6},{5,3},{6,0},{7,5},{8,10},{9,15},{10,... | collective-permute-start | bytes 3145736 | tf_op jit(solution)/shard_map/ppermute | solution.py:184
  90.5 15.2 %collective-permute-start.4 = (bf16[512,1024]{1,0:T(8,128)(2,1)S(1)}, bf16[512,1024]{1,0:T(8,128)(2,1)S(1)}, u32[]{:S(2)}, u32[]{:S(2)}) collective-permute-start(bf16[512,1024]{1,0:T(8,128)(2,1)S(1)} %collective-permute-done), channel_id=1, source_target_pairs={{0,1},{1,0},{2,3},{3,2},{4,5},{5,4},{6,7},{7,6},{8,9},{9,8},{10,11... | collective-permute-start | bytes 3145736 | tf_op jit(solution)/shard_map/ppermute | solution.py:185
  91.5 15.3 %collective-permute-start.5 = (bf16[512,1024]{1,0:T(8,128)(2,1)S(1)}, bf16[512,1024]{1,0:T(8,128)(2,1)S(1)}, u32[]{:S(2)}, u32[]{:S(2)}) collective-permute-start(bf16[512,1024]{1,0:T(8,128)(2,1)S(1)} %collective-permute-done.1), channel_id=1, source_target_pairs={{0,1},{1,0},{2,3},{3,2},{4,5},{5,4},{6,7},{7,6},{8,9},{9,8},{10,11... | collective-permute-start | bytes 3145736 | tf_op jit(solution)/shard_map/ppermute | solution.py:185
  103.6 4.3 %collective-permute-start.6 = (bf16[512,1024]{1,0:T(8,128)(2,1)S(1)}, bf16[512,1024]{1,0:T(8,128)(2,1)S(1)}, u32[]{:S(2)}, u32[]{:S(2)}) collective-permute-start(bf16[512,1024]{1,0:T(8,128)(2,1)S(1)} %collective-permute-done.2), channel_id=1, source_target_pairs={{0,1},{1,0},{2,3},{3,2},{4,5},{5,4},{6,7},{7,6},{8,9},{9,8},{10,11... | collective-permute-start | bytes 3145736 | tf_op jit(solution)/shard_map/ppermute | solution.py:185
  172.9 188.4 %reduce-scatter.6.cloned.1.call-start = ((), (), s32[]{:S(2)}) async-start(), calls=%async_computation.6 | async-start | bytes 9437184 | tf_op jit(solution)/shard_map/reduce_scatter | solution.py:209
  186.6 89.7 %all-to-all-start = ((bf16[16,128,1152]{2,1,0:T(8,128)(2,1)}), bf16[16,128,1152]{2,1,0:T(8,128)(2,1)}, u32[]{:S(2)}, u32[]{:S(2)}) async-start(bf16[16,128,1152]{2,1,0:T(8,128)(2,1)} %get-tuple-element.9), calls=%async_computation.3 | async-start | bytes 9437184 | tf_op jit(solution)/shard_map/all_to_all | solution.py:215
Sparse Core Ops, SparseCore 0:
  10.4 44.7 reduce-scatter.3
  57.4 87.7 all-gather.1
  173.0 131.5 reduce-scatter.7
  307.4 53.8 reduce-scatter.5

commit v11 on v9

--- a/solution.py
+++ b/solution.py
@@ -29,44 +29,39 @@
         first = owner_ref[2 * span]
         second = owner_ref[2 * span + 1]
         rows = slice(sub * SPAN, (sub + 1) * SPAN)
+        head_cols = [slice(h * HD, (h + 1) * HD) for h in range(heads)]
+        key_cols = [slice(2 * h * HD, 2 * h * HD + HD) for h in range(heads)]
+        value_cols = [slice(2 * h * HD + HD, 2 * (h + 1) * HD) for h in range(heads)]
+        q = jnp.stack([q_ref[rows, c] for c in head_cols])
+        g = jnp.stack([g_ref[rows, c] for c in head_cols])
+        k = jnp.stack(
+            [jnp.concatenate([first_ref[0, :, c], second_ref[0, :, c]], axis=0) for c in key_cols]
+        )
+        v = jnp.stack(
+            [jnp.concatenate([first_ref[0, :, c], second_ref[0, :, c]], axis=0) for c in value_cols]
+        )
+        batch_nt = (((2,), (2,)), ((0,), (0,)))
+        batch_nn = (((2,), (1,)), ((0,), (0,)))
+        batch_tn = (((1,), (1,)), ((0,), (0,)))
+        scores = lax.dot_general(q, k, batch_nt, preferred_element_type=jnp.float32) * factor
+        top = jnp.max(scores, axis=-1, keepdims=True)
+        expo = jnp.exp(scores - top)
+        probs = expo / jnp.sum(expo, axis=-1, keepdims=True)
+        probs_low = probs.astype(jnp.bfloat16)
+        attended = lax.dot_general(probs_low, v, batch_nn, preferred_element_type=jnp.float32)
+        grad_values = lax.dot_general(probs_low, g, batch_tn, preferred_element_type=jnp.float32)
+        grad_probs = lax.dot_general(g, v, batch_nt, preferred_element_type=jnp.float32)
+        grad_scores = probs * (grad_probs - jnp.sum(probs * grad_probs, axis=-1, keepdims=True))
+        grad_scores = grad_scores.astype(jnp.bfloat16)
+        grad_keys = (
+            lax.dot_general(grad_scores, q, batch_tn, preferred_element_type=jnp.float32) * factor
+        )
         for h in range(heads):
-            cols = slice(h * HD, (h + 1) * HD)
-            kcols = slice(2 * h * HD, 2 * h * HD + HD)
-            vcols = slice(2 * h * HD + HD, 2 * (h + 1) * HD)
-            q = q_ref[rows, cols]
-            g = g_ref[rows, cols]
-            k = jnp.concatenate([first_ref[0, :, kcols], second_ref[0, :, kcols]], axis=0)
-            v = jnp.concatenate([first_ref[0, :, vcols], second_ref[0, :, vcols]], axis=0)
-            scores = (
-                lax.dot_general(q, k, (((1,), (1,)), ((), ())), preferred_element_type=jnp.float32)
-                * factor
-            )
-            top = jnp.max(scores, axis=-1, keepdims=True)
-            expo = jnp.exp(scores - top)
-            probs = expo / jnp.sum(expo, axis=-1, keepdims=True)
-            probs_low = probs.astype(jnp.bfloat16)
-            attended = jnp.dot(probs_low, v, preferred_element_type=jnp.float32)
-            att_ref[rows, cols] = attended.astype(att_ref.dtype)
-            grad_values = lax.dot_general(
-                probs_low, g, (((0,), (0,)), ((), ())), preferred_element_type=jnp.float32
-            )
-            grad_probs = lax.dot_general(
-                g, v, (((1,), (1,)), ((), ())), preferred_element_type=jnp.float32
-            )
-            grad_scores = probs * (
-                grad_probs - jnp.sum(probs * grad_probs, axis=-1, keepdims=True)
-            )
-            grad_scores = grad_scores.astype(jnp.bfloat16)
-            grad_keys = (
-                lax.dot_general(
-                    grad_scores, q, (((0,), (0,)), ((), ())), preferred_element_type=jnp.float32
-                )
-                * factor
-            )
-            acc_ref[first, :, kcols] += grad_keys[:NBR_LEN]
-            acc_ref[second, :, kcols] += grad_keys[NBR_LEN:]
-            acc_ref[first, :, vcols] += grad_values[:NBR_LEN]
-            acc_ref[second, :, vcols] += grad_values[NBR_LEN:]
+            att_ref[rows, head_cols[h]] = attended[h].astype(att_ref.dtype)
+            acc_ref[first, :, key_cols[h]] += grad_keys[h, :NBR_LEN]
+            acc_ref[second, :, key_cols[h]] += grad_keys[h, NBR_LEN:]
+            acc_ref[first, :, value_cols[h]] += grad_values[h, :NBR_LEN]
+            acc_ref[second, :, value_cols[h]] += grad_values[h, NBR_LEN:]
 
     @pl.when(step == pl.num_programs(0) - 1)
     def _():

time: 312 us -> 301 us (0.965)
  Pallas kernels: 32 us -> 21.3 us
    pallas_call x1, Pallas kernels: 26.9 us -> 16.2 us  [attention(): pl.pallas_call(functools.partial(attention_kernel, heads, per_step), grid...]
where the time goes in v11:
time: 301 us
  waiting for transfers between devices  208 us (69%)
  matrix products  27.4 us (9%)
  Pallas kernels  21.3 us (7%)
  local copies, waits for them, and re-layouts  19.9 us (7%)
  between operations  13.8 us (5%)
  starting transfers between devices  8.64 us (3%)
    all_to_all x1, waiting for transfers between devices, local(): lax.all_to_all(per_owner, 'dp', split_axis=0, concat_axis=0, tiled=True)  105 us
    reduce_scatter x1, waiting for transfers between devices, local(): lax.psum_scatter(kv_part[0], 'tensor', scatter_dimension=1, tiled=True)  47.2 us
    ppermute x3, waiting for transfers between devices, local(): mine.append(lax.ppermute(mine[-1], 'tensor', ring))  40.5 us
    pallas_call x1, Pallas kernels, attention(): pl.pallas_call(functools.partial(attention_kernel, heads, per_step), grid...  16.2 us
    all_gather x1, waiting for transfers between devices, local(): everyone = lax.all_gather(share_blocks, 'dp', axis=0, tiled=True)  14.3 us
    dot_general x1, matrix products, local(): jnp.einsum('tqc,htc->qh', ordered, w_out.reshape(head_width, tensor_count...  13.8 us
    dot_general x1, matrix products, local(): partial_out = jnp.dot(attended, w_out, preferred_element_type=jnp.float32)  13.6 us
    unnamed x15, local copies, waits for them, and re-layouts  8.96 us
  transfers between devices with their start and end apart: 11, of which 6 were waited for; matrix products, arithmetic and copies ran while one was open for 12% of the time, Pallas kernels for 2%

profile of v11, /device:TPU:28, one launch (start us, length us, event | category | flops | bytes accessed | tf_op | source)
XLA Modules:
  0.0 300.9 jit_solution(15440815863719374861)
XLA Ops:
  7.2 0.0 reduce-scatter.3.cloned.1.call-start
  7.2 0.7 reduce-scatter.3.cloned.1.call-update
  7.9 0.0 all-gather.2.cloned.1.call-start
  7.9 47.2 %reduce-scatter.3.cloned.1.call-done = bf16[256,1536]{1,0:T(8,128)(2,1)} async-done(((bf16[256,12288]{1,0:T(8,128)(2,1)}), bf16[256,1536]{1,0:T(8,128)(2,1)}) %reduce-scatter.3.cloned.1.call-update) | async-done | bytes 786448 | tf_op jit(solution)/shard_map/reduce_scatter | solution.py:140
  55.2 0.0 all-gather.2.cloned.1.call-update
  55.2 0.0 reduce-scatter.5.cloned.1.call-start
  55.3 0.1 collective-permute-start
  55.3 16.2 %collective-permute-done = bf16[512,1024]{1,0:T(8,128)(2,1)S(1)} collective-permute-done((bf16[512,1024]{1,0:T(8,128)(2,1)}, bf16[512,1024]{1,0:T(8,128)(2,1)S(1)}, u32[]{:S(2)}, u32[]{:S(2)}) %collective-permute-start) | collective-permute-done | bytes 1048608 | tf_op jit(solution)/shard_map/ppermute | solution.py:169
  71.5 0.4 collective-permute-start.3
  71.9 0.8 constant_dynamic-slice_fusion
  72.7 0.1 copy.26
  72.8 0.1 reshape.26.owner_ref
  72.9 0.1 copy.27
  72.9 0.1 reshape.27
  73.0 0.1 pad_add_fusion
  73.1 0.6 iota_reduce_fusion
  73.8 13.8 %collective-permute-done.1 = bf16[512,1024]{1,0:T(8,128)(2,1)S(1)} collective-permute-done((bf16[512,1024]{1,0:T(8,128)(2,1)S(1)}, bf16[512,1024]{1,0:T(8,128)(2,1)S(1)}, u32[]{:S(2)}, u32[]{:S(2)}) %collective-permute-start.1) | collective-permute-done | bytes 1048608 | tf_op jit(solution)/shard_map/ppermute | solution.py:169
  87.6 2.3 bitcast_dynamic-update-slice_fusion.7
  89.9 0.6 multiply_add_fusion.pick_ref
  90.5 1.0 bitcast_dynamic-update-slice_fusion.6
  91.5 0.5 collective-permute-start.5
  92.0 1.0 bitcast_dynamic-update-slice_fusion.5
  93.1 10.5 %collective-permute-done.2 = bf16[512,1024]{1,0:T(8,128)(2,1)S(1)} collective-permute-done((bf16[512,1024]{1,0:T(8,128)(2,1)S(1)}, bf16[512,1024]{1,0:T(8,128)(2,1)S(1)}, u32[]{:S(2)}, u32[]{:S(2)}) %collective-permute-start.2) | collective-permute-done | bytes 1048608 | tf_op jit(solution)/shard_map/ppermute | solution.py:169
  103.6 1.1 bitcast_dynamic-update-slice_fusion.4
  104.6 1.1 bitcast_dynamic-update-slice_fusion.3
  105.7 1.1 bitcast_dynamic-update-slice_fusion.2
  106.8 1.1 bitcast_dynamic-update-slice_fusion.1
  107.9 1.1 bitcast_dynamic-update-slice_fusion
  108.9 8.2 %gather_fusion = bf16[8,512,1024]{2,1,0:T(8,128)(2,1)} fusion(bf16[8,512,1024]{2,1,0:T(8,128)(2,1)} %bitcast_dynamic-update-slice_fusion, s32[1024]{0:T(1024)S(1)} %pad_clamp_fusion), kind=kCustom, calls=%fused_computation | custom fusion | bytes 16777248 | tf_op jit(solution)/shard_map/jit(_take)/gather | solution.py:181
  117.2 13.8 %bitcast_convert_fusion.g_ref = bf16[512,768]{1,0:T(8,128)(2,1)} fusion(bf16[8,512,1024]{2,1,0:T(8,128)(2,1)} %gather_fusion, bf16[96,8,8,1024]{3,2,1,0:T(8,128)(2,1)} %bitcast.33), kind=kOutput, calls=%fused_computation.5 | convolution fusion | flops 6442844160 | bytes 21757952 | tf_op jit(solution)/shard_map/tqc,htc->qh/dot_general | solution.py:182
  131.0 14.3 %all-gather.2.cloned.1.call-done.rest_0_.rest_1_.rest_2_.rest_3_ = bf16[32,128,1536]{2,1,0:T(8,128)(2,1)} async-done(((bf16[2,128,1536]{2,1,0:T(8,128)(2,1)}), bf16[32,128,1536]{2,1,0:T(8,128)(2,1)}) %all-gather.2.cloned.1.call-update) | async-done | bytes 12582928 | tf_op jit(solution)/shard_map/all_gather | solution.py:159
  145.3 16.2 %shard_map.77 = (bf16[512,768]{1,0:T(8,128)(2,1)}, bf16[16,128,1536]{2,1,0:T(8,128)(2,1)}) custom-call(s32[16]{0:T(128)} %copy-done.2, s32[16]{0:T(128)} %multiply_add_fusion.pick_ref, bf16[512,768]{1,0:T(8,128)(2,1)} %q_ref.1, bf16[512,768]{1,0:T(8,128)(2,1)} %bitcast_convert_fusion.g_ref, ...), custom_call_target="tpu_custom_call" | custom-call | tf_op jit(solution)/shard_map/pallas_call | solution.py:97
  161.4 13.6 %convolution_convert_fusion = bf16[512,8192]{1,0:T(8,128)(2,1)} fusion(bf16[512,768]{1,0:T(8,128)(2,1)} %get-tuple-element.6, bf16[768,8192]{1,0:T(8,128)(2,1)} %param.8), kind=kOutput, calls=%fused_computation.4 | convolution fusion | flops 6446645248 | bytes 21757952 | tf_op jit(solution)/shard_map/dot_general | solution.py:189
  175.0 0.0 reduce-scatter.5.cloned.1.call-update
  175.0 0.0 copy-start
  175.1 0.0 copy-start.1
  175.1 7.6 %all-to-all-start = ((bf16[16,128,1536]{2,1,0:T(8,128)(2,1)}), bf16[16,128,1536]{2,1,0:T(8,128)(2,1)}, u32[]{:S(2)}, u32[]{:S(2)}) async-start(bf16[16,128,1536]{2,1,0:T(8,128)(2,1)} %get-tuple-element.7), calls=%async_computation.2 | async-start | bytes 12582912 | tf_op jit(solution)/shard_map/all_to_all | solution.py:193
  182.6 0.1 copy.30
  182.8 0.1 copy.29
  182.9 0.1 broadcast_in_dim.26
  182.9 0.1 eq.54
  183.0 0.2 select_reduce_fusion
  183.2 0.2 dynamic-slice_reduce_fusion
  183.4 0.1 fusion.5
  183.5 0.2 dynamic-slice_reduce_fusion.1
  183.7 0.7 fusion.7.select_ref
  184.4 104.9 %all-to-all-done.returned_ref = bf16[16,128,1536]{2,1,0:T(8,128)(2,1)} async-done(((bf16[16,128,1536]{2,1,0:T(8,128)(2,1)}), bf16[16,128,1536]{2,1,0:T(8,128)(2,1)}, u32[]{:S(2)}, u32[]{:S(2)}) %all-to-all-start) | async-done | bytes 6291488 | tf_op jit(solution)/shard_map/all_to_all | solution.py:193
  289.3 5.1 %shard_map.78 = bf16[2,128,1536]{2,1,0:T(8,128)(2,1)} custom-call(f32[16,2]{1,0:T(8,128)} %fusion.7.select_ref, bf16[16,128,1536]{2,1,0:T(8,128)(2,1)} %all-to-all-done.returned_ref), custom_call_target="tpu_custom_call" | custom-call | tf_op jit(solution)/shard_map/pallas_call | solution.py:121
  (15 shorter events, 0.0 us)
Async XLA Ops:
  7.2 48.0 %reduce-scatter.3.cloned.1.call-start = ((), (), s32[]{:S(2)}) async-start(), calls=%async_computation.3 | async-start | bytes 7077888 | tf_op jit(solution)/shard_map/reduce_scatter | solution.py:140
  7.9 137.4 %all-gather.2.cloned.1.call-start = ((), (), s32[]{:S(2)}) async-start(), calls=%async_computation.4 | async-start | bytes 13369344 | tf_op jit(solution)/shard_map/all_gather | solution.py:159
  55.2 239.2 %reduce-scatter.5.cloned.1.call-start = ((), (), s32[]{:S(2)}) async-start(), calls=%async_computation.5 | async-start | bytes 9437184 | tf_op jit(solution)/shard_map/reduce_scatter | solution.py:190
  55.3 16.3 %collective-permute-start = (bf16[512,1024]{1,0:T(8,128)(2,1)}, bf16[512,1024]{1,0:T(8,128)(2,1)S(1)}, u32[]{:S(2)}, u32[]{:S(2)}) collective-permute-start(bf16[512,1024]{1,0:T(8,128)(2,1)} %param.9), channel_id=1, source_target_pairs={{0,2},{1,7},{2,4},{3,1},{4,6},{5,3},{6,0},{7,5},{8,10},{9,15},{10,... | collective-permute-start | bytes 3145736 | tf_op jit(solution)/shard_map/ppermute | solution.py:169
  71.5 16.0 %collective-permute-start.1 = (bf16[512,1024]{1,0:T(8,128)(2,1)S(1)}, bf16[512,1024]{1,0:T(8,128)(2,1)S(1)}, u32[]{:S(2)}, u32[]{:S(2)}) collective-permute-start(bf16[512,1024]{1,0:T(8,128)(2,1)S(1)} %collective-permute-done), channel_id=1, source_target_pairs={{0,2},{1,7},{2,4},{3,1},{4,6},{5,3},{6,0},{7,5},{8,10},{9,15},{10,... | collective-permute-start | bytes 3145736 | tf_op jit(solution)/shard_map/ppermute | solution.py:169
  71.5 33.1 %collective-permute-start.3 = (bf16[512,1024]{1,0:T(8,128)(2,1)}, bf16[512,1024]{1,0:T(8,128)(2,1)S(1)}, u32[]{:S(2)}, u32[]{:S(2)}) collective-permute-start(bf16[512,1024]{1,0:T(8,128)(2,1)} %param.9), channel_id=1, source_target_pairs={{0,1},{1,0},{2,3},{3,2},{4,5},{5,4},{6,7},{7,6},{8,9},{9,8},{10,11... | collective-permute-start | bytes 3145736 | tf_op jit(solution)/shard_map/ppermute | solution.py:170
  72.9 36.1 %copy-start.2 = (s32[16]{0:T(128)}, s32[16]{0:T(128)S(1)}, u32[]{:S(2)}) copy-start(s32[16]{0:T(128)S(1)} %reshape.26.owner_ref) | copy-start | bytes 196
  87.6 16.0 %collective-permute-start.2 = (bf16[512,1024]{1,0:T(8,128)(2,1)S(1)}, bf16[512,1024]{1,0:T(8,128)(2,1)S(1)}, u32[]{:S(2)}, u32[]{:S(2)}) collective-permute-start(bf16[512,1024]{1,0:T(8,128)(2,1)S(1)} %collective-permute-done.1), channel_id=1, source_target_pairs={{0,2},{1,7},{2,4},{3,1},{4,6},{5,3},{6,0},{7,5},{8,10},{9,15},{10,... | collective-permute-start | bytes 3145736 | tf_op jit(solution)/shard_map/ppermute | solution.py:169
  90.5 15.2 %collective-permute-start.4 = (bf16[512,1024]{1,0:T(8,128)(2,1)S(1)}, bf16[512,1024]{1,0:T(8,128)(2,1)S(1)}, u32[]{:S(2)}, u32[]{:S(2)}) collective-permute-start(bf16[512,1024]{1,0:T(8,128)(2,1)S(1)} %collective-permute-done), channel_id=1, source_target_pairs={{0,1},{1,0},{2,3},{3,2},{4,5},{5,4},{6,7},{7,6},{8,9},{9,8},{10,11... | collective-permute-start | bytes 3145736 | tf_op jit(solution)/shard_map/ppermute | solution.py:170
  91.5 15.3 %collective-permute-start.5 = (bf16[512,1024]{1,0:T(8,128)(2,1)S(1)}, bf16[512,1024]{1,0:T(8,128)(2,1)S(1)}, u32[]{:S(2)}, u32[]{:S(2)}) collective-permute-start(bf16[512,1024]{1,0:T(8,128)(2,1)S(1)} %collective-permute-done.1), channel_id=1, source_target_pairs={{0,1},{1,0},{2,3},{3,2},{4,5},{5,4},{6,7},{7,6},{8,9},{9,8},{10,11... | collective-permute-start | bytes 3145736 | tf_op jit(solution)/shard_map/ppermute | solution.py:170
  103.6 4.3 %collective-permute-start.6 = (bf16[512,1024]{1,0:T(8,128)(2,1)S(1)}, bf16[512,1024]{1,0:T(8,128)(2,1)S(1)}, u32[]{:S(2)}, u32[]{:S(2)}) collective-permute-start(bf16[512,1024]{1,0:T(8,128)(2,1)S(1)} %collective-permute-done.2), channel_id=1, source_target_pairs={{0,1},{1,0},{2,3},{3,2},{4,5},{5,4},{6,7},{7,6},{8,9},{9,8},{10,11... | collective-permute-start | bytes 3145736 | tf_op jit(solution)/shard_map/ppermute | solution.py:170
  175.0 7.6 %copy-start = (s32[128,2]{0,1:T(2,128)S(1)}, s32[128,2]{0,1:T(2,128)}, u32[]{:S(2)}) copy-start(s32[128,2]{0,1:T(2,128)} %param.11) | copy-start | bytes 3076
  175.1 7.7 %copy-start.1 = (s32[128,2]{0,1:T(2,128)S(1)}, s32[128,2]{0,1:T(2,128)}, u32[]{:S(2)}) copy-start(s32[128,2]{0,1:T(2,128)} %param.10) | copy-start | bytes 3076
  175.1 114.2 %all-to-all-start = ((bf16[16,128,1536]{2,1,0:T(8,128)(2,1)}), bf16[16,128,1536]{2,1,0:T(8,128)(2,1)}, u32[]{:S(2)}, u32[]{:S(2)}) async-start(bf16[16,128,1536]{2,1,0:T(8,128)(2,1)} %get-tuple-element.7), calls=%async_computation.2 | async-start | bytes 12582912 | tf_op jit(solution)/shard_map/all_to_all | solution.py:193
Sparse Core Ops, SparseCore 0:
  10.4 44.7 reduce-scatter.2
  57.4 87.8 all-gather.1
  175.2 54.2 reduce-scatter.4

commit v12 on v11

--- a/solution.py
+++ b/solution.py
@@ -137,7 +137,8 @@
     share_width = 2 * head_width
     span_count = queries.shape[0] // SPAN
     read_count = 2 * span_count
-    shares = lax.psum_scatter(kv_part[0], "tensor", scatter_dimension=1, tiled=True)
+    by_column = kv_part[0].reshape(NB_DEV * NBR_LEN, -1, share_width).transpose(1, 0, 2)
+    shares = lax.psum_scatter(by_column, "tensor", scatter_dimension=0, tiled=True)
     share_blocks = shares.reshape(NB_DEV, NBR_LEN, share_width)
     owner_ids = jnp.arange(dp_count, dtype=jnp.int32)
     slot_ids = jnp.arange(NB_DEV, dtype=jnp.int32)

time: 301 us -> 309 us (1.027)
  local copies, waits for them, and re-layouts: 19.9 us -> 29.5 us
    unnamed x15 -> x18, local copies, waits for them, and re-layouts: 8.96 us -> 14.5 us
    another operation x0 -> x1, local copies, waits for them, and re-layouts: none -> 4.71 us  [local(): kv_part[0].reshape(NB_DEV * NBR_LEN, -1, share_width).transpose(1, 0, 2)]
  transfers between devices with their start and end apart: 11 -> 11, of which waited for: 6 -> 6; matrix products, arithmetic and copies ran while one was open for 12% -> 11% of each run, Pallas kernels for 2% -> 2%
where the time goes in v12:
time: 309 us; the launch traced here: 308 us
  waiting for transfers between devices  205 us (66%)
  local copies, waits for them, and re-layouts  29.5 us (10%)
  matrix products  27.4 us (9%)
  Pallas kernels  21.4 us (7%)
  between operations  13.8 us (4%)
  starting transfers between devices  8.71 us (3%)
    all_to_all x1, waiting for transfers between devices, local(): lax.all_to_all(per_owner, 'dp', split_axis=0, concat_axis=0, tiled=True)  105 us
    reduce_scatter x1, waiting for transfers between devices, local(): lax.psum_scatter(by_column, 'tensor', scatter_dimension=0, tiled=True)  44.8 us
    ppermute x3, waiting for transfers between devices, local(): mine.append(lax.ppermute(mine[-1], 'tensor', ring))  42.2 us
    pallas_call x1, Pallas kernels, attention(): pl.pallas_call(functools.partial(attention_kernel, heads, per_step), grid...  16.3 us
    unnamed x18, local copies, waits for them, and re-layouts  14.5 us
    dot_general x1, matrix products, local(): jnp.einsum('tqc,htc->qh', ordered, w_out.reshape(head_width, tensor_count...  13.8 us
    dot_general x1, matrix products, local(): partial_out = jnp.dot(attended, w_out, preferred_element_type=jnp.float32)  13.6 us
    all_gather x1, waiting for transfers between devices, local(): everyone = lax.all_gather(share_blocks, 'dp', axis=0, tiled=True)  13.2 us
  transfers between devices with their start and end apart: 11, of which 6 were waited for; matrix products, arithmetic and copies ran while one was open for 11% of the time, Pallas kernels for 2%

profile of v12, /device:TPU:28, one launch (start us, length us, event | category | flops | bytes accessed | tf_op | source)
XLA Modules:
  0.0 308.3 jit_solution(13601171884149481116)
XLA Ops:
  7.2 0.0 reduce-scatter.3.cloned.1.call-start
  7.2 5.4 %copy.37 = bf16[32,8,8,1536]{3,2,1,0:T(8,128)(2,1)S(1)} copy(bf16[32,8,8,1536]{3,1,2,0:T(8,128)(2,1)} %bitcast.37) | data formatting | bytes 12582912
  12.7 4.7 %copy.45 = bf16[256,8,1536]{2,0,1:T(8,128)(2,1)} copy(bf16[256,8,1536]{2,1,0:T(8,128)(2,1)S(1)} %bitcast.36) | data formatting | bytes 12582912 | tf_op jit(solution)/shard_map/reshape;squeeze | solution.py:140
  17.4 0.0 reduce-scatter.3.cloned.1.call-update
  17.4 0.0 all-gather.2.cloned.1.call-start
  17.5 44.8 %reduce-scatter.3.cloned.1.call-done = bf16[1,256,1536]{2,1,0:T(8,128)(2,1)} async-done(((bf16[8,256,1536]{2,1,0:T(8,128)(2,1)}), bf16[1,256,1536]{2,1,0:T(8,128)(2,1)}) %reduce-scatter.3.cloned.1.call-update) | async-done | bytes 786448 | tf_op jit(solution)/shard_map/reduce_scatter | solution.py:141
  62.3 0.0 all-gather.2.cloned.1.call-update
  62.3 0.0 reduce-scatter.5.cloned.1.call-start
  62.4 0.1 collective-permute-start
  62.5 16.0 %collective-permute-done = bf16[512,1024]{1,0:T(8,128)(2,1)S(1)} collective-permute-done((bf16[512,1024]{1,0:T(8,128)(2,1)S(1)}, bf16[512,1024]{1,0:T(8,128)(2,1)S(1)}, u32[]{:S(2)}, u32[]{:S(2)}) %collective-permute-start) | collective-permute-done | bytes 1048608 | tf_op jit(solution)/shard_map/ppermute | solution.py:170
  78.5 0.4 collective-permute-start.3
  78.9 0.1 constant_dynamic-slice_fusion
  78.9 0.1 copy.30
  79.0 0.1 reshape.26.owner_ref
  79.1 0.1 copy.31
  79.2 0.1 reshape.27
  79.3 0.1 pad_add_fusion
  79.4 0.6 iota_reduce_fusion
  80.0 14.5 %collective-permute-done.1 = bf16[512,1024]{1,0:T(8,128)(2,1)S(1)} collective-permute-done((bf16[512,1024]{1,0:T(8,128)(2,1)S(1)}, bf16[512,1024]{1,0:T(8,128)(2,1)S(1)}, u32[]{:S(2)}, u32[]{:S(2)}) %collective-permute-start.1) | collective-permute-done | bytes 1048608 | tf_op jit(solution)/shard_map/ppermute | solution.py:170
  94.5 1.1 bitcast_dynamic-update-slice_fusion.7
  95.6 0.6 multiply_add_fusion.pick_ref
  96.2 1.0 bitcast_dynamic-update-slice_fusion.6
  97.2 0.5 collective-permute-start.5
  97.7 1.0 bitcast_dynamic-update-slice_fusion.5
  98.8 11.7 %collective-permute-done.2 = bf16[512,1024]{1,0:T(8,128)(2,1)S(1)} collective-permute-done((bf16[512,1024]{1,0:T(8,128)(2,1)S(1)}, bf16[512,1024]{1,0:T(8,128)(2,1)S(1)}, u32[]{:S(2)}, u32[]{:S(2)}) %collective-permute-start.2) | collective-permute-done | bytes 1048608 | tf_op jit(solution)/shard_map/ppermute | solution.py:170
  110.5 1.1 bitcast_dynamic-update-slice_fusion.4
  111.6 2.3 bitcast_dynamic-update-slice_fusion.3
  113.9 1.1 bitcast_dynamic-update-slice_fusion.2
  115.0 1.1 bitcast_dynamic-update-slice_fusion.1
  116.1 1.1 bitcast_dynamic-update-slice_fusion
  117.1 8.3 %gather_fusion = bf16[8,512,1024]{2,1,0:T(8,128)(2,1)} fusion(bf16[8,512,1024]{2,1,0:T(8,128)(2,1)} %bitcast_dynamic-update-slice_fusion, s32[1024]{0:T(1024)S(1)} %pad_clamp_fusion), kind=kCustom, calls=%fused_computation | custom fusion | bytes 16777248 | tf_op jit(solution)/shard_map/jit(_take)/gather | solution.py:182
  125.4 13.8 %bitcast_convert_fusion.g_ref = bf16[512,768]{1,0:T(8,128)(2,1)} fusion(bf16[8,512,1024]{2,1,0:T(8,128)(2,1)} %gather_fusion, bf16[96,8,8,1024]{3,2,1,0:T(8,128)(2,1)} %bitcast.40), kind=kOutput, calls=%fused_computation.6 | convolution fusion | flops 6442844160 | bytes 21757952 | tf_op jit(solution)/shard_map/tqc,htc->qh/dot_general | solution.py:183
  139.2 13.2 %all-gather.2.cloned.1.call-done.rest_0_.rest_1_.rest_2_.rest_3_ = bf16[32,128,1536]{2,1,0:T(8,128)(2,1)} async-done(((bf16[2,128,1536]{2,1,0:T(8,128)(2,1)}), bf16[32,128,1536]{2,1,0:T(8,128)(2,1)}) %all-gather.2.cloned.1.call-update) | async-done | bytes 12582928 | tf_op jit(solution)/shard_map/all_gather | solution.py:160
  152.4 16.3 %shard_map.77 = (bf16[512,768]{1,0:T(8,128)(2,1)}, bf16[16,128,1536]{2,1,0:T(8,128)(2,1)}) custom-call(s32[16]{0:T(128)} %copy-done.3, s32[16]{0:T(128)} %multiply_add_fusion.pick_ref, bf16[512,768]{1,0:T(8,128)(2,1)} %q_ref.1, bf16[512,768]{1,0:T(8,128)(2,1)} %bitcast_convert_fusion.g_ref, ...), custom_call_target="tpu_custom_call" | custom-call | tf_op jit(solution)/shard_map/pallas_call | solution.py:97
  168.7 13.6 %convolution_convert_fusion = bf16[512,8192]{1,0:T(8,128)(2,1)} fusion(bf16[512,768]{1,0:T(8,128)(2,1)} %get-tuple-element.6, bf16[768,8192]{1,0:T(8,128)(2,1)} %param.8), kind=kOutput, calls=%fused_computation.4 | convolution fusion | flops 6446645248 | bytes 21757952 | tf_op jit(solution)/shard_map/dot_general | solution.py:190
  182.3 0.0 reduce-scatter.5.cloned.1.call-update
  182.3 7.6 %all-to-all-start = ((bf16[16,128,1536]{2,1,0:T(8,128)(2,1)}), bf16[16,128,1536]{2,1,0:T(8,128)(2,1)}, u32[]{:S(2)}, u32[]{:S(2)}) async-start(bf16[16,128,1536]{2,1,0:T(8,128)(2,1)} %get-tuple-element.7), calls=%async_computation.2 | async-start | bytes 12582912 | tf_op jit(solution)/shard_map/all_to_all | solution.py:194
  190.0 0.1 copy.35
  190.1 0.1 copy.34
  190.2 0.1 broadcast_in_dim.26
  190.3 0.1 eq.54
  190.4 0.2 select_reduce_fusion
  190.5 0.2 dynamic-slice_reduce_fusion
  190.7 0.1 fusion.5
  190.8 0.2 dynamic-slice_reduce_fusion.1
  191.0 0.7 fusion.7.select_ref
  191.7 105.0 %all-to-all-done.returned_ref = bf16[16,128,1536]{2,1,0:T(8,128)(2,1)} async-done(((bf16[16,128,1536]{2,1,0:T(8,128)(2,1)}), bf16[16,128,1536]{2,1,0:T(8,128)(2,1)}, u32[]{:S(2)}, u32[]{:S(2)}) %all-to-all-start) | async-done | bytes 6291488 | tf_op jit(solution)/shard_map/all_to_all | solution.py:194
  296.7 5.1 %shard_map.78 = bf16[2,128,1536]{2,1,0:T(8,128)(2,1)} custom-call(f32[16,2]{1,0:T(8,128)} %fusion.7.select_ref, bf16[16,128,1536]{2,1,0:T(8,128)(2,1)} %all-to-all-done.returned_ref), custom_call_target="tpu_custom_call" | custom-call | tf_op jit(solution)/shard_map/pallas_call | solution.py:121
  (19 shorter events, 0.1 us)
Async XLA Ops:
  7.2 55.2 %reduce-scatter.3.cloned.1.call-start = ((), (), s32[]{:S(2)}) async-start(), calls=%async_computation.3 | async-start | bytes 7077888 | tf_op jit(solution)/shard_map/reduce_scatter | solution.py:141
  12.7 49.7 %copy-start = (bf16[512,1024]{1,0:T(8,128)(2,1)S(1)}, bf16[512,1024]{1,0:T(8,128)(2,1)}, u32[]{:S(2)}) copy-start(bf16[512,1024]{1,0:T(8,128)(2,1)} %param.9) | copy-start | bytes 3145732
  12.7 66.2 %copy-start.1 = (s32[128,2]{0,1:T(2,128)S(1)}, s32[128,2]{0,1:T(2,128)}, u32[]{:S(2)}) copy-start(s32[128,2]{0,1:T(2,128)} %param.11) | copy-start | bytes 3076
  12.7 66.2 %copy-start.2 = (s32[128,2]{0,1:T(2,128)S(1)}, s32[128,2]{0,1:T(2,128)}, u32[]{:S(2)}) copy-start(s32[128,2]{0,1:T(2,128)} %param.10) | copy-start | bytes 3076
  17.4 135.0 %all-gather.2.cloned.1.call-start = ((), (), s32[]{:S(2)}) async-start(), calls=%async_computation.4 | async-start | bytes 13369344 | tf_op jit(solution)/shard_map/all_gather | solution.py:160
  62.3 239.4 %reduce-scatter.5.cloned.1.call-start = ((), (), s32[]{:S(2)}) async-start(), calls=%async_computation.5 | async-start | bytes 9437184 | tf_op jit(solution)/shard_map/reduce_scatter | solution.py:191
  62.4 16.1 %collective-permute-start = (bf16[512,1024]{1,0:T(8,128)(2,1)S(1)}, bf16[512,1024]{1,0:T(8,128)(2,1)S(1)}, u32[]{:S(2)}, u32[]{:S(2)}) collective-permute-start(bf16[512,1024]{1,0:T(8,128)(2,1)S(1)} %copy-done), channel_id=1, source_target_pairs={{0,2},{1,7},{2,4},{3,1},{4,6},{5,3},{6,0},{7,5},{8,10},{9,15},{10,... | collective-permute-start | bytes 3145736 | tf_op jit(solution)/shard_map/ppermute | solution.py:170
  78.5 16.0 %collective-permute-start.1 = (bf16[512,1024]{1,0:T(8,128)(2,1)S(1)}, bf16[512,1024]{1,0:T(8,128)(2,1)S(1)}, u32[]{:S(2)}, u32[]{:S(2)}) collective-permute-start(bf16[512,1024]{1,0:T(8,128)(2,1)S(1)} %collective-permute-done), channel_id=1, source_target_pairs={{0,2},{1,7},{2,4},{3,1},{4,6},{5,3},{6,0},{7,5},{8,10},{9,15},{10,... | collective-permute-start | bytes 3145736 | tf_op jit(solution)/shard_map/ppermute | solution.py:170
  78.5 33.1 %collective-permute-start.3 = (bf16[512,1024]{1,0:T(8,128)(2,1)S(1)}, bf16[512,1024]{1,0:T(8,128)(2,1)}, u32[]{:S(2)}, u32[]{:S(2)}) collective-permute-start(bf16[512,1024]{1,0:T(8,128)(2,1)S(1)} %copy-done), channel_id=1, source_target_pairs={{0,1},{1,0},{2,3},{3,2},{4,5},{5,4},{6,7},{7,6},{8,9},{9,8},{10,11... | collective-permute-start | bytes 3145736 | tf_op jit(solution)/shard_map/ppermute | solution.py:171
  79.1 38.0 %copy-start.3 = (s32[16]{0:T(128)}, s32[16]{0:T(128)S(1)}, u32[]{:S(2)}) copy-start(s32[16]{0:T(128)S(1)} %reshape.26.owner_ref) | copy-start | bytes 196
  94.5 16.0 %collective-permute-start.2 = (bf16[512,1024]{1,0:T(8,128)(2,1)S(1)}, bf16[512,1024]{1,0:T(8,128)(2,1)S(1)}, u32[]{:S(2)}, u32[]{:S(2)}) collective-permute-start(bf16[512,1024]{1,0:T(8,128)(2,1)S(1)} %collective-permute-done.1), channel_id=1, source_target_pairs={{0,2},{1,7},{2,4},{3,1},{4,6},{5,3},{6,0},{7,5},{8,10},{9,15},{10,... | collective-permute-start | bytes 3145736 | tf_op jit(solution)/shard_map/ppermute | solution.py:170
  96.2 17.7 %collective-permute-start.4 = (bf16[512,1024]{1,0:T(8,128)(2,1)S(1)}, bf16[512,1024]{1,0:T(8,128)(2,1)S(1)}, u32[]{:S(2)}, u32[]{:S(2)}) collective-permute-start(bf16[512,1024]{1,0:T(8,128)(2,1)S(1)} %collective-permute-done), channel_id=1, source_target_pairs={{0,1},{1,0},{2,3},{3,2},{4,5},{5,4},{6,7},{7,6},{8,9},{9,8},{10,11... | collective-permute-start | bytes 3145736 | tf_op jit(solution)/shard_map/ppermute | solution.py:171
  97.2 17.8 %collective-permute-start.5 = (bf16[512,1024]{1,0:T(8,128)(2,1)S(1)}, bf16[512,1024]{1,0:T(8,128)(2,1)S(1)}, u32[]{:S(2)}, u32[]{:S(2)}) collective-permute-start(bf16[512,1024]{1,0:T(8,128)(2,1)S(1)} %collective-permute-done.1), channel_id=1, source_target_pairs={{0,1},{1,0},{2,3},{3,2},{4,5},{5,4},{6,7},{7,6},{8,9},{9,8},{10,11... | collective-permute-start | bytes 3145736 | tf_op jit(solution)/shard_map/ppermute | solution.py:171
  110.5 5.6 %collective-permute-start.6 = (bf16[512,1024]{1,0:T(8,128)(2,1)S(1)}, bf16[512,1024]{1,0:T(8,128)(2,1)S(1)}, u32[]{:S(2)}, u32[]{:S(2)}) collective-permute-start(bf16[512,1024]{1,0:T(8,128)(2,1)S(1)} %collective-permute-done.2), channel_id=1, source_target_pairs={{0,1},{1,0},{2,3},{3,2},{4,5},{5,4},{6,7},{7,6},{8,9},{9,8},{10,11... | collective-permute-start | bytes 3145736 | tf_op jit(solution)/shard_map/ppermute | solution.py:171
  182.3 114.3 %all-to-all-start = ((bf16[16,128,1536]{2,1,0:T(8,128)(2,1)}), bf16[16,128,1536]{2,1,0:T(8,128)(2,1)}, u32[]{:S(2)}, u32[]{:S(2)}) async-start(bf16[16,128,1536]{2,1,0:T(8,128)(2,1)} %get-tuple-element.7), calls=%async_computation.2 | async-start | bytes 12582912 | tf_op jit(solution)/shard_map/all_to_all | solution.py:194
Sparse Core Ops, SparseCore 0:
  17.5 44.7 reduce-scatter.2
  64.5 87.8 all-gather.1
  182.5 54.3 reduce-scatter.4

commit v13 on v11

--- a/solution.py
+++ b/solution.py
@@ -58,10 +58,11 @@
         )
         for h in range(heads):
             att_ref[rows, head_cols[h]] = attended[h].astype(att_ref.dtype)
-            acc_ref[first, :, key_cols[h]] += grad_keys[h, :NBR_LEN]
-            acc_ref[second, :, key_cols[h]] += grad_keys[h, NBR_LEN:]
-            acc_ref[first, :, value_cols[h]] += grad_values[h, :NBR_LEN]
-            acc_ref[second, :, value_cols[h]] += grad_values[h, NBR_LEN:]
+        for owner, part in ((first, slice(0, NBR_LEN)), (second, slice(NBR_LEN, 2 * NBR_LEN))):
+            pieces = []
+            for h in range(heads):
+                pieces += [grad_keys[h, part], grad_values[h, part]]
+            acc_ref[owner] += jnp.concatenate(pieces, axis=1)
 
     @pl.when(step == pl.num_programs(0) - 1)
     def _():

time: 301 us -> 301 us (level)
  no operation moved by 1% of the time
where the time goes in v13:
time: 301 us; the launch traced here: 300 us
  waiting for transfers between devices  208 us (69%)
  matrix products  27.4 us (9%)
  Pallas kernels  20.8 us (7%)
  local copies, waits for them, and re-layouts  19.9 us (7%)
  between operations  13.8 us (5%)
  starting transfers between devices  8.32 us (3%)
    all_to_all x1, waiting for transfers between devices, local(): lax.all_to_all(per_owner, 'dp', split_axis=0, concat_axis=0, tiled=True)  105 us
    reduce_scatter x1, waiting for transfers between devices, local(): lax.psum_scatter(kv_part[0], 'tensor', scatter_dimension=1, tiled=True)  47.2 us
    ppermute x3, waiting for transfers between devices, local(): mine.append(lax.ppermute(mine[-1], 'tensor', ring))  40.5 us
    pallas_call x1, Pallas kernels, attention(): pl.pallas_call(functools.partial(attention_kernel, heads, per_step), grid...  15.7 us
    all_gather x1, waiting for transfers between devices, local(): everyone = lax.all_gather(share_blocks, 'dp', axis=0, tiled=True)  14.3 us
    dot_general x1, matrix products, local(): jnp.einsum('tqc,htc->qh', ordered, w_out.reshape(head_width, tensor_count...  13.8 us
    dot_general x1, matrix products, local(): partial_out = jnp.dot(attended, w_out, preferred_element_type=jnp.float32)  13.6 us
    unnamed x15, local copies, waits for them, and re-layouts  8.96 us
  transfers between devices with their start and end apart: 11, of which 6 were waited for; matrix products, arithmetic and copies ran while one was open for 12% of the time, Pallas kernels for 2%

profile of v13, /device:TPU:28, one launch (start us, length us, event | category | flops | bytes accessed | tf_op | source)
XLA Modules:
  0.0 300.1 jit_solution(5459469669390907815)
XLA Ops:
  7.2 0.0 reduce-scatter.3.cloned.1.call-start
  7.2 0.7 reduce-scatter.3.cloned.1.call-update
  7.9 0.0 all-gather.2.cloned.1.call-start
  7.9 47.2 %reduce-scatter.3.cloned.1.call-done = bf16[256,1536]{1,0:T(8,128)(2,1)} async-done(((bf16[256,12288]{1,0:T(8,128)(2,1)}), bf16[256,1536]{1,0:T(8,128)(2,1)}) %reduce-scatter.3.cloned.1.call-update) | async-done | bytes 786448 | tf_op jit(solution)/shard_map/reduce_scatter | solution.py:141
  55.2 0.0 all-gather.2.cloned.1.call-update
  55.2 0.0 reduce-scatter.5.cloned.1.call-start
  55.3 0.1 collective-permute-start
  55.3 16.2 %collective-permute-done = bf16[512,1024]{1,0:T(8,128)(2,1)S(1)} collective-permute-done((bf16[512,1024]{1,0:T(8,128)(2,1)}, bf16[512,1024]{1,0:T(8,128)(2,1)S(1)}, u32[]{:S(2)}, u32[]{:S(2)}) %collective-permute-start) | collective-permute-done | bytes 1048608 | tf_op jit(solution)/shard_map/ppermute | solution.py:170
  71.5 0.4 collective-permute-start.3
  71.9 0.8 constant_dynamic-slice_fusion
  72.7 0.1 copy.26
  72.8 0.1 reshape.26.owner_ref
  72.9 0.1 copy.27
  72.9 0.1 reshape.27
  73.0 0.1 pad_add_fusion
  73.1 0.6 iota_reduce_fusion
  73.8 13.8 %collective-permute-done.1 = bf16[512,1024]{1,0:T(8,128)(2,1)S(1)} collective-permute-done((bf16[512,1024]{1,0:T(8,128)(2,1)S(1)}, bf16[512,1024]{1,0:T(8,128)(2,1)S(1)}, u32[]{:S(2)}, u32[]{:S(2)}) %collective-permute-start.1) | collective-permute-done | bytes 1048608 | tf_op jit(solution)/shard_map/ppermute | solution.py:170
  87.6 2.3 bitcast_dynamic-update-slice_fusion.7
  89.9 0.6 multiply_add_fusion.pick_ref
  90.5 1.0 bitcast_dynamic-update-slice_fusion.6
  91.5 0.5 collective-permute-start.5
  92.0 1.0 bitcast_dynamic-update-slice_fusion.5
  93.1 10.5 %collective-permute-done.2 = bf16[512,1024]{1,0:T(8,128)(2,1)S(1)} collective-permute-done((bf16[512,1024]{1,0:T(8,128)(2,1)S(1)}, bf16[512,1024]{1,0:T(8,128)(2,1)S(1)}, u32[]{:S(2)}, u32[]{:S(2)}) %collective-permute-start.2) | collective-permute-done | bytes 1048608 | tf_op jit(solution)/shard_map/ppermute | solution.py:170
  103.6 1.1 bitcast_dynamic-update-slice_fusion.4
  104.6 1.1 bitcast_dynamic-update-slice_fusion.3
  105.7 1.1 bitcast_dynamic-update-slice_fusion.2
  106.8 1.1 bitcast_dynamic-update-slice_fusion.1
  107.9 1.1 bitcast_dynamic-update-slice_fusion
  108.9 8.2 %gather_fusion = bf16[8,512,1024]{2,1,0:T(8,128)(2,1)} fusion(bf16[8,512,1024]{2,1,0:T(8,128)(2,1)} %bitcast_dynamic-update-slice_fusion, s32[1024]{0:T(1024)S(1)} %pad_clamp_fusion), kind=kCustom, calls=%fused_computation | custom fusion | bytes 16777248 | tf_op jit(solution)/shard_map/jit(_take)/gather | solution.py:182
  117.2 13.8 %bitcast_convert_fusion.g_ref = bf16[512,768]{1,0:T(8,128)(2,1)} fusion(bf16[8,512,1024]{2,1,0:T(8,128)(2,1)} %gather_fusion, bf16[96,8,8,1024]{3,2,1,0:T(8,128)(2,1)} %bitcast.33), kind=kOutput, calls=%fused_computation.5 | convolution fusion | flops 6442844160 | bytes 21757952 | tf_op jit(solution)/shard_map/tqc,htc->qh/dot_general | solution.py:183
  131.0 14.3 %all-gather.2.cloned.1.call-done.rest_0_.rest_1_.rest_2_.rest_3_ = bf16[32,128,1536]{2,1,0:T(8,128)(2,1)} async-done(((bf16[2,128,1536]{2,1,0:T(8,128)(2,1)}), bf16[32,128,1536]{2,1,0:T(8,128)(2,1)}) %all-gather.2.cloned.1.call-update) | async-done | bytes 12582928 | tf_op jit(solution)/shard_map/all_gather | solution.py:160
  145.3 15.7 %shard_map.77 = (bf16[512,768]{1,0:T(8,128)(2,1)}, bf16[16,128,1536]{2,1,0:T(8,128)(2,1)}) custom-call(s32[16]{0:T(128)} %copy-done.2, s32[16]{0:T(128)} %multiply_add_fusion.pick_ref, bf16[512,768]{1,0:T(8,128)(2,1)} %q_ref.1, bf16[512,768]{1,0:T(8,128)(2,1)} %bitcast_convert_fusion.g_ref, ...), custom_call_target="tpu_custom_call" | custom-call | tf_op jit(solution)/shard_map/pallas_call | solution.py:98
  160.9 13.6 %convolution_convert_fusion = bf16[512,8192]{1,0:T(8,128)(2,1)} fusion(bf16[512,768]{1,0:T(8,128)(2,1)} %get-tuple-element.6, bf16[768,8192]{1,0:T(8,128)(2,1)} %param.8), kind=kOutput, calls=%fused_computation.4 | convolution fusion | flops 6446645248 | bytes 21757952 | tf_op jit(solution)/shard_map/dot_general | solution.py:190
  174.5 0.0 reduce-scatter.5.cloned.1.call-update
  174.5 0.0 copy-start
  174.6 0.0 copy-start.1
  174.6 7.2 %all-to-all-start = ((bf16[16,128,1536]{2,1,0:T(8,128)(2,1)}), bf16[16,128,1536]{2,1,0:T(8,128)(2,1)}, u32[]{:S(2)}, u32[]{:S(2)}) async-start(bf16[16,128,1536]{2,1,0:T(8,128)(2,1)} %get-tuple-element.7), calls=%async_computation.2 | async-start | bytes 12582912 | tf_op jit(solution)/shard_map/all_to_all | solution.py:194
  181.8 0.1 copy.30
  181.9 0.1 copy.29
  182.0 0.1 broadcast_in_dim.26
  182.1 0.1 eq.54
  182.2 0.2 select_reduce_fusion
  182.4 0.2 dynamic-slice_reduce_fusion
  182.6 0.1 fusion.5
  182.7 0.2 dynamic-slice_reduce_fusion.1
  182.9 0.7 fusion.7.select_ref
  183.5 104.9 %all-to-all-done.returned_ref = bf16[16,128,1536]{2,1,0:T(8,128)(2,1)} async-done(((bf16[16,128,1536]{2,1,0:T(8,128)(2,1)}), bf16[16,128,1536]{2,1,0:T(8,128)(2,1)}, u32[]{:S(2)}, u32[]{:S(2)}) %all-to-all-start) | async-done | bytes 6291488 | tf_op jit(solution)/shard_map/all_to_all | solution.py:194
  288.4 5.1 %shard_map.78 = bf16[2,128,1536]{2,1,0:T(8,128)(2,1)} custom-call(f32[16,2]{1,0:T(8,128)} %fusion.7.select_ref, bf16[16,128,1536]{2,1,0:T(8,128)(2,1)} %all-to-all-done.returned_ref), custom_call_target="tpu_custom_call" | custom-call | tf_op jit(solution)/shard_map/pallas_call | solution.py:122
  (15 shorter events, 0.0 us)
Async XLA Ops:
  7.2 48.0 %reduce-scatter.3.cloned.1.call-start = ((), (), s32[]{:S(2)}) async-start(), calls=%async_computation.3 | async-start | bytes 7077888 | tf_op jit(solution)/shard_map/reduce_scatter | solution.py:141
  7.9 137.4 %all-gather.2.cloned.1.call-start = ((), (), s32[]{:S(2)}) async-start(), calls=%async_computation.4 | async-start | bytes 13369344 | tf_op jit(solution)/shard_map/all_gather | solution.py:160
  55.2 238.3 %reduce-scatter.5.cloned.1.call-start = ((), (), s32[]{:S(2)}) async-start(), calls=%async_computation.5 | async-start | bytes 9437184 | tf_op jit(solution)/shard_map/reduce_scatter | solution.py:191
  55.3 16.3 %collective-permute-start = (bf16[512,1024]{1,0:T(8,128)(2,1)}, bf16[512,1024]{1,0:T(8,128)(2,1)S(1)}, u32[]{:S(2)}, u32[]{:S(2)}) collective-permute-start(bf16[512,1024]{1,0:T(8,128)(2,1)} %param.9), channel_id=1, source_target_pairs={{0,2},{1,7},{2,4},{3,1},{4,6},{5,3},{6,0},{7,5},{8,10},{9,15},{10,... | collective-permute-start | bytes 3145736 | tf_op jit(solution)/shard_map/ppermute | solution.py:170
  71.5 16.0 %collective-permute-start.1 = (bf16[512,1024]{1,0:T(8,128)(2,1)S(1)}, bf16[512,1024]{1,0:T(8,128)(2,1)S(1)}, u32[]{:S(2)}, u32[]{:S(2)}) collective-permute-start(bf16[512,1024]{1,0:T(8,128)(2,1)S(1)} %collective-permute-done), channel_id=1, source_target_pairs={{0,2},{1,7},{2,4},{3,1},{4,6},{5,3},{6,0},{7,5},{8,10},{9,15},{10,... | collective-permute-start | bytes 3145736 | tf_op jit(solution)/shard_map/ppermute | solution.py:170
  71.5 33.1 %collective-permute-start.3 = (bf16[512,1024]{1,0:T(8,128)(2,1)}, bf16[512,1024]{1,0:T(8,128)(2,1)S(1)}, u32[]{:S(2)}, u32[]{:S(2)}) collective-permute-start(bf16[512,1024]{1,0:T(8,128)(2,1)} %param.9), channel_id=1, source_target_pairs={{0,1},{1,0},{2,3},{3,2},{4,5},{5,4},{6,7},{7,6},{8,9},{9,8},{10,11... | collective-permute-start | bytes 3145736 | tf_op jit(solution)/shard_map/ppermute | solution.py:171
  72.9 36.1 %copy-start.2 = (s32[16]{0:T(128)}, s32[16]{0:T(128)S(1)}, u32[]{:S(2)}) copy-start(s32[16]{0:T(128)S(1)} %reshape.26.owner_ref) | copy-start | bytes 196
  87.6 16.0 %collective-permute-start.2 = (bf16[512,1024]{1,0:T(8,128)(2,1)S(1)}, bf16[512,1024]{1,0:T(8,128)(2,1)S(1)}, u32[]{:S(2)}, u32[]{:S(2)}) collective-permute-start(bf16[512,1024]{1,0:T(8,128)(2,1)S(1)} %collective-permute-done.1), channel_id=1, source_target_pairs={{0,2},{1,7},{2,4},{3,1},{4,6},{5,3},{6,0},{7,5},{8,10},{9,15},{10,... | collective-permute-start | bytes 3145736 | tf_op jit(solution)/shard_map/ppermute | solution.py:170
  90.5 15.2 %collective-permute-start.4 = (bf16[512,1024]{1,0:T(8,128)(2,1)S(1)}, bf16[512,1024]{1,0:T(8,128)(2,1)S(1)}, u32[]{:S(2)}, u32[]{:S(2)}) collective-permute-start(bf16[512,1024]{1,0:T(8,128)(2,1)S(1)} %collective-permute-done), channel_id=1, source_target_pairs={{0,1},{1,0},{2,3},{3,2},{4,5},{5,4},{6,7},{7,6},{8,9},{9,8},{10,11... | collective-permute-start | bytes 3145736 | tf_op jit(solution)/shard_map/ppermute | solution.py:171
  91.5 15.3 %collective-permute-start.5 = (bf16[512,1024]{1,0:T(8,128)(2,1)S(1)}, bf16[512,1024]{1,0:T(8,128)(2,1)S(1)}, u32[]{:S(2)}, u32[]{:S(2)}) collective-permute-start(bf16[512,1024]{1,0:T(8,128)(2,1)S(1)} %collective-permute-done.1), channel_id=1, source_target_pairs={{0,1},{1,0},{2,3},{3,2},{4,5},{5,4},{6,7},{7,6},{8,9},{9,8},{10,11... | collective-permute-start | bytes 3145736 | tf_op jit(solution)/shard_map/ppermute | solution.py:171
  103.6 4.3 %collective-permute-start.6 = (bf16[512,1024]{1,0:T(8,128)(2,1)S(1)}, bf16[512,1024]{1,0:T(8,128)(2,1)S(1)}, u32[]{:S(2)}, u32[]{:S(2)}) collective-permute-start(bf16[512,1024]{1,0:T(8,128)(2,1)S(1)} %collective-permute-done.2), channel_id=1, source_target_pairs={{0,1},{1,0},{2,3},{3,2},{4,5},{5,4},{6,7},{7,6},{8,9},{9,8},{10,11... | collective-permute-start | bytes 3145736 | tf_op jit(solution)/shard_map/ppermute | solution.py:171
  174.5 7.3 %copy-start = (s32[128,2]{0,1:T(2,128)S(1)}, s32[128,2]{0,1:T(2,128)}, u32[]{:S(2)}) copy-start(s32[128,2]{0,1:T(2,128)} %param.11) | copy-start | bytes 3076
  174.6 7.4 %copy-start.1 = (s32[128,2]{0,1:T(2,128)S(1)}, s32[128,2]{0,1:T(2,128)}, u32[]{:S(2)}) copy-start(s32[128,2]{0,1:T(2,128)} %param.10) | copy-start | bytes 3076
  174.6 113.9 %all-to-all-start = ((bf16[16,128,1536]{2,1,0:T(8,128)(2,1)}), bf16[16,128,1536]{2,1,0:T(8,128)(2,1)}, u32[]{:S(2)}, u32[]{:S(2)}) async-start(bf16[16,128,1536]{2,1,0:T(8,128)(2,1)} %get-tuple-element.7), calls=%async_computation.2 | async-start | bytes 12582912 | tf_op jit(solution)/shard_map/all_to_all | solution.py:194
Sparse Core Ops, SparseCore 0:
  10.4 44.7 reduce-scatter.2
  57.4 87.8 all-gather.1
  174.7 53.9 reduce-scatter.4
